TPU v7x, 32 devices: a whole 2x2x4 slice. The times are simulated.
32 devices in a mesh: area: 16 (over z, y, core), depth: 2 (over x).
Axes of the slice: x: 2, y: 2, z: 4, core: 2. Of those that a mesh axis runs over, the one named last changes fastest.
Arguments:
- pressure: float32 [32, 128, 1024], P('depth', 'area'), may hold values from -2.5 to -0.3
- theta_old: float32 [32, 128, 1024], P('depth', 'area'), may hold values from 0.1 to 0.35
- source: float32 [32, 128, 1024], P('depth', 'area'), may hold values from -3 to 3
- soil_type: int32 [32, 128, 1024], P('depth', 'area'), may hold values from 0 to 11
- soil_params: float32 [5, 12], replicated, as said below
Outputs:
- new_pressure: float32 [32, 128, 1024], P('depth', 'area')
- coarse_head: float32 [128, 1024], P('area')
Inputs may be any that keep to these rules, and one draw needn't show every extreme that they name: Each column of soil_params holds theta_r in 0.03 to 0.1, theta_s in 0.35 to 0.5, a in 0.5 to 3, n in 1.3 to 2.5, Ks in 0.2 to 2.
All inputs are finite; a program needn't handle non-finite values.
Results may differ from a plain program's by a relative error of at most 0.00002.
Values sent between devices are 32-bit elements; how exact they have to be, the bound alone decides.
No kernel may reach another device: no remote copies, remote signals or barrier semaphores. Data moves between devices by JAX's collectives and lax.ppermute only.
A program may use at most 64 MiB of HBM per device.

v0:
```python
import jax
import jax.numpy as jnp
from jax import lax
from jax.sharding import PartitionSpec as P

step_time = 0.1
relax = 0.8
small_suction = 0.04


def with_halo(block, sides, width):
    for axis, dim in sides:
        count = lax.axis_size(axis)
        forward = [(i, i + 1) for i in range(count - 1)]
        backward = [(target, source) for source, target in forward]
        low = lax.ppermute(
            lax.slice_in_dim(block, block.shape[dim] - width, None, axis=dim), axis, forward
        )
        high = lax.ppermute(lax.slice_in_dim(block, 0, width, axis=dim), axis, backward)
        block = jnp.concatenate([low, block, high], axis=dim)
    return block


def soil_fields(soil_type, soil_params):
    fields = []
    for row_id in range(5):
        picked = jnp.zeros(soil_type.shape, jnp.float32)
        for kind_id in range(soil_params.shape[1]):
            picked = jnp.where(soil_type == kind_id, soil_params[row_id, kind_id], picked)
        fields.append(picked)
    return fields


def hydraulics(pressure, params):
    theta_r, theta_s, alpha_vg, shape_n, k_sat = params
    suction = jnp.sqrt(pressure * pressure + small_suction)
    shape_m = 1.0 - 1.0 / shape_n
    power_term = jnp.exp(shape_n * jnp.log(alpha_vg * suction))
    one_plus = 1.0 + power_term
    saturation = jnp.exp(-shape_m * jnp.log(one_plus))
    content = theta_r + (theta_s - theta_r) * saturation
    capacity = (
        (theta_s - theta_r) * shape_m * shape_n * power_term * saturation / (one_plus * suction)
    )
    ratio_term = power_term / one_plus
    conduct = (
        k_sat * jnp.sqrt(saturation) * jnp.square(1.0 - jnp.exp(shape_m * jnp.log(ratio_term)))
    )
    return (content, capacity, conduct)


def fine_balance(padded_head, padded_cond, content, capacity, theta_old, source):
    centre_h = padded_head[1:-1, 1:-1, 1:-1]
    centre_k = padded_cond[1:-1, 1:-1, 1:-1]
    inflow = jnp.zeros_like(centre_h)
    totals = jnp.zeros_like(centre_h)
    for axis_pos in range(3):
        for offset, weight in ((0, 1.0), (2, -1.0)):
            window = [slice(1, -1)] * 3
            window[axis_pos] = slice(offset, offset + centre_h.shape[axis_pos])
            near_h = padded_head[tuple(window)]
            near_k = padded_cond[tuple(window)]
            face_k = jnp.sqrt(centre_k * near_k)
            inflow = inflow + face_k * (near_h - centre_h)
            totals = totals + face_k
            if axis_pos == 0:
                inflow = inflow + weight * face_k
    balance = (content - theta_old) / step_time - inflow - source
    diagonal = capacity / step_time + totals
    return (balance, diagonal)


def coarse_balance(padded_head, padded_trans, storage, base):
    centre_h = padded_head[1:-1, 1:-1]
    centre_t = padded_trans[1:-1, 1:-1]
    inflow = jnp.zeros_like(centre_h)
    totals = jnp.zeros_like(centre_h)
    for axis_pos in range(2):
        for offset in (0, 2):
            window = [slice(1, -1)] * 2
            window[axis_pos] = slice(offset, offset + centre_h.shape[axis_pos])
            face_t = jnp.sqrt(centre_t * padded_trans[tuple(window)])
            inflow = inflow + face_t * (padded_head[tuple(window)] - centre_h)
            totals = totals + face_t
    balance = storage / step_time * (centre_h - base) - inflow
    diagonal = storage / step_time + totals
    return (balance, diagonal)


def coarse_rim_rows(stacked):
    extended = with_halo(stacked, (("area", 1),), 1)
    return jnp.pad(extended, ((0, 0), (0, 0), (1, 1)))


def coarse_cycle(columns, depth_total, rim_rows):
    column_kh = columns[0]
    column_k = columns[1]
    storage = columns[2]
    restricted = columns[3]
    column_rate = columns[4] / depth_total
    base = column_kh / column_k
    padded = rim_rows(jnp.stack([base, column_k]))
    start_flow, start_diag = coarse_balance(padded[0], padded[1], storage, base)
    coarse_rhs = start_flow + restricted
    first = base - relax * (start_flow - coarse_rhs) / start_diag
    transmit = column_k * jnp.exp(column_rate * jnp.tanh(first - base))
    padded = rim_rows(jnp.stack([first, transmit]))
    first_flow, first_diag = coarse_balance(padded[0], padded[1], storage, base)
    second = first - relax * (first_flow - coarse_rhs) / first_diag
    return (base, second)


def shards(pressure, theta_old, source, soil_type, soil_params):
    depth_total = pressure.shape[0] * lax.axis_size("depth")
    params = soil_fields(soil_type, soil_params)
    content, capacity, conduct = hydraulics(pressure, params)
    extended = with_halo(jnp.stack([pressure, conduct]), (("area", 2), ("depth", 1)), 1)
    extended = jnp.pad(extended, ((0, 0), (0, 0), (0, 0), (1, 1)))
    balance, diagonal = fine_balance(extended[0], extended[1], content, capacity, theta_old, source)
    smoothed = pressure - relax * balance / diagonal
    content, capacity, conduct = hydraulics(smoothed, params)
    extended = with_halo(jnp.stack([smoothed, conduct]), (("area", 2), ("depth", 1)), 1)
    extended = jnp.pad(extended, ((0, 0), (0, 0), (0, 0), (1, 1)))
    balance, diagonal = fine_balance(extended[0], extended[1], content, capacity, theta_old, source)
    local_sums = jnp.stack(
        [
            jnp.sum(conduct * smoothed, axis=0),
            jnp.sum(conduct, axis=0),
            jnp.sum(capacity, axis=0),
            -jnp.sum(balance, axis=0),
            jnp.sum(params[2], axis=0),
        ]
    )
    columns = lax.psum(local_sums, "depth")
    base, second = coarse_cycle(columns, depth_total, coarse_rim_rows)
    return (smoothed + (second - base)[None], second)


def solution(mesh):
    in_specs = (
        P("depth", "area", None),
        P("depth", "area", None),
        P("depth", "area", None),
        P("depth", "area", None),
        P(),
    )
    out_specs = (P("depth", "area", None), P("area", None))
    return jax.shard_map(shards, mesh=mesh, in_specs=in_specs, out_specs=out_specs, check_vma=False)
```

profile of v0, /device:TPU:5, one launch (start us, length us, event | category | flops | bytes accessed | tf_op | source)
XLA Modules:
  0.0 171.1 jit_solution(90720884499490197)
XLA Ops:
  7.2 0.0 copy-start
  7.2 0.0 all-reduce.6.cloned.1.call-start
  7.2 2.1 %fusion.109 = (f32[1,1]{1,0:T(1,128)}, f32[1,1]{1,0:T(1,128)}, f32[1,1]{1,0:T(1,128)}, f32[1,1]{1,0:T(1,128)}, f32[1,1]{1,0:T(1,128)}, /*index=5*/f32[1,1]{1,0:T...) fusion(f32[5,12]{1,0:T(8,128)} %param.9), kind=kLoop, calls=%fused_computation.233 | loop fusion | bytes 152 | tf_op jit(solution)/shard_map/slice | solution.py:29
  9.3 2.1 %fusion.108 = (f32[1,1]{1,0:T(1,128)}, f32[1,1]{1,0:T(1,128)}, f32[1,1]{1,0:T(1,128)}, f32[1,1]{1,0:T(1,128)}, f32[1,1]{1,0:T(1,128)}, /*index=5*/f32[1,1]{1,0:T...) fusion(f32[5,12]{1,0:T(8,128)} %param.9), kind=kLoop, calls=%fused_computation.232 | loop fusion | bytes 152 | tf_op jit(solution)/shard_map/slice | solution.py:29
  11.4 1.4 fusion.111
  12.8 9.6 %fusion.105 = (f32[8,1024]{1,0:T(8,128)S(1)}, f32[16,8,1024]{2,1,0:T(8,128)S(1)}, pred[16,8,1024]{2,1,0:T(8,128)(4,1)S(1)}, pred[16,8,1024]{2,1,0:T(8,128)(4,1)S...) fusion(f32[]{:T(128)} %bitcast.47, f32[]{:T(128)} %bitcast.46, ...), kind=kLoop, calls=%fused_computation.231 | loop fusion | flops 3268608 | bytes 2654256 | tf_op jit(solution)/shard_map/reduce_sum | solution.py:131
  22.5 0.0 copy-done
  22.5 0.0 copy-start.4
  22.5 16.5 %fusion.63 = (f32[1,16,8,1024]{3,2,1,0:T(8,128)S(1)}, f32[16,8,1024]{2,1,0:T(8,128)S(1)}, f32[16,8,1024]{2,1,0:T(8,128)S(1)}) fusion(f32[16,8,1024]{2,1,0:T(8,128)S(1)} %get-tuple-element.11, f32[16,8,1024]{2,1,0:T(8,128)S(1)} %copy-done, pred[16,8,1024]{2,1,0:T(8,128)(4,1)S(1)} %get-tuple-element.23, pred[16,8,1024]{2,1,0:T(8,128)(4,1)S(1)} %get-tuple-element.22, ...), kind=kLoop, calls=%fused_computation.123 | loop fusion | flops 5111808 | bytes 4194400 | tf_op jit(solution)/shard_map/stack | solution.py:117
  39.0 0.2 pad_maximum_fusion.11
  39.1 3.7 %collective-permute-start = (f32[2,16,1,1024]{3,2,1,0:T(1,128)S(1)}, f32[2,16,1,1024]{3,2,1,0:T(1,128)S(1)}, u32[]{:S(2)}, u32[]{:S(2)}) collective-permute-start(f32[2,16,1,1024]{3,2,1,0:T(1,128)S(1)} %get-tuple-element.41), channel_id=1, source_target_pairs={{0,2},{2,4},{4,6},{6,8},{8,10},{10,12},{12,14},{14,16},{16,18},{18... | collective-permute-start | bytes 393224 | tf_op jit(solution)/shard_map/ppermute | solution.py:16
  42.8 1.9 %collective-permute-start.1 = (f32[2,16,1,1024]{3,2,1,0:T(1,128)S(1)}, f32[2,16,1,1024]{3,2,1,0:T(1,128)S(1)}, u32[]{:S(2)}, u32[]{:S(2)}) collective-permute-start(f32[2,16,1,1024]{3,2,1,0:T(1,128)S(1)} %get-tuple-element.42), channel_id=1, source_target_pairs={{2,0},{4,2},{6,4},{8,6},{10,8},{12,10},{14,12},{16,14},{18,16},{20... | collective-permute-start | bytes 393224 | tf_op jit(solution)/shard_map/ppermute | solution.py:19
  44.8 0.0 collective-permute-done
  44.8 5.2 %collective-permute-done.1 = f32[2,16,1,1024]{3,2,1,0:T(1,128)S(1)} collective-permute-done((f32[2,16,1,1024]{3,2,1,0:T(1,128)S(1)}, f32[2,16,1,1024]{3,2,1,0:T(1,128)S(1)}, u32[]{:S(2)}, u32[]{:S(2)}) %collective-permute-start.1) | collective-permute-done | bytes 131104 | tf_op jit(solution)/shard_map/ppermute | solution.py:19
  50.1 3.1 %collective-permute-start.2 = (f32[2,1,10,1024]{3,2,1,0:T(8,128)S(1)}, f32[2,1,10,1024]{3,2,1,0:T(8,128)S(1)}, u32[]{:S(2)}, u32[]{:S(2)}) collective-permute-start(f32[2,1,10,1024]{3,2,1,0:T(8,128)S(1)} %get-tuple-element.37), channel_id=1, source_target_pairs={{0,1},{2,3},{4,5},{6,7},{8,9},{10,11},{12,13},{14,15},{16,17},{18,... | collective-permute-start | bytes 245768 | tf_op jit(solution)/shard_map/ppermute | solution.py:16
  53.2 1.3 collective-permute-start.3
  54.5 0.0 copy-done.4
  54.5 0.7 fusion.110
  55.3 0.0 collective-permute-done.2
  55.3 3.7 %collective-permute-done.3 = f32[2,1,10,1024]{3,2,1,0:T(8,128)S(1)} collective-permute-done((f32[2,1,10,1024]{3,2,1,0:T(8,128)S(1)}, f32[2,1,10,1024]{3,2,1,0:T(8,128)S(1)}, u32[]{:S(2)}, u32[]{:S(2)}) %collective-permute-start.3) | collective-permute-done | bytes 81952 | tf_op jit(solution)/shard_map/ppermute | solution.py:19
  58.9 1.5 select_maximum_fusion.5
  60.5 0.0 copy-start.1
  60.5 0.0 copy-start.2
  60.5 0.2 slice_bitcast_fusion.3
  60.7 0.8 copy-done.1
  61.5 0.2 copy-done.2
  61.7 19.8 %fusion.62 = (f32[8,1024]{1,0:T(8,128)S(1)}, f32[16,8,1024]{2,1,0:T(8,128)S(1)}, f32[16,8,1024]{2,1,0:T(8,128)S(1)}) fusion(f32[16,8,1024]{2,1,0:T(8,128)S(1)} %get-tuple-element.29, pred[16,8,1024]{2,1,0:T(8,128)(4,1)S(1)} %get-tuple-element.23, pred[16,8,1024]{2,1,0:T(8,128)(4,1)S(1)} %get-tuple-element.22, ...), kind=kLoop, calls=%fused_computation.122 | loop fusion | flops 12181504 | bytes 12615776 | tf_op jit(solution)/shard_map/reduce_sum | solution.py:129
  81.5 0.6 fusion.101
  82.1 0.2 pad_maximum_fusion.5
  82.3 4.2 %collective-permute-start.4 = (f32[2,16,1,1024]{3,2,1,0:T(1,128)S(1)}, f32[2,16,1,1024]{3,2,1,0:T(1,128)S(1)}, u32[]{:S(2)}, u32[]{:S(2)}) collective-permute-start(f32[2,16,1,1024]{3,2,1,0:T(1,128)S(1)} %get-tuple-element.39), channel_id=1, source_target_pairs={{0,2},{2,4},{4,6},{6,8},{8,10},{10,12},{12,14},{14,16},{16,18},{18... | collective-permute-start | bytes 393224 | tf_op jit(solution)/shard_map/ppermute | solution.py:16
  86.5 1.9 %collective-permute-start.5 = (f32[2,16,1,1024]{3,2,1,0:T(1,128)S(1)}, f32[2,16,1,1024]{3,2,1,0:T(1,128)S(1)}, u32[]{:S(2)}, u32[]{:S(2)}) collective-permute-start(f32[2,16,1,1024]{3,2,1,0:T(1,128)S(1)} %get-tuple-element.40), channel_id=1, source_target_pairs={{2,0},{4,2},{6,4},{8,6},{10,8},{12,10},{14,12},{16,14},{18,16},{20... | collective-permute-start | bytes 393224 | tf_op jit(solution)/shard_map/ppermute | solution.py:19
  88.5 0.0 collective-permute-done.4
  88.5 5.2 %collective-permute-done.5 = f32[2,16,1,1024]{3,2,1,0:T(1,128)S(1)} collective-permute-done((f32[2,16,1,1024]{3,2,1,0:T(1,128)S(1)}, f32[2,16,1,1024]{3,2,1,0:T(1,128)S(1)}, u32[]{:S(2)}, u32[]{:S(2)}) %collective-permute-start.5) | collective-permute-done | bytes 131104 | tf_op jit(solution)/shard_map/ppermute | solution.py:19
  93.7 1.3 collective-permute-start.6
  95.1 1.5 collective-permute-start.7
  96.5 0.4 collective-permute-done.6
  97.0 3.8 %collective-permute-done.7 = f32[2,1,10,1024]{3,2,1,0:T(8,128)S(1)} collective-permute-done((f32[2,1,10,1024]{3,2,1,0:T(8,128)S(1)}, f32[2,1,10,1024]{3,2,1,0:T(8,128)S(1)}, u32[]{:S(2)}, u32[]{:S(2)}) %collective-permute-start.7) | collective-permute-done | bytes 81952 | tf_op jit(solution)/shard_map/ppermute | solution.py:19
  100.8 1.5 select_maximum_fusion
  102.3 0.2 slice_bitcast_fusion.1
  102.5 18.4 %fusion.64 = f32[8,1024]{1,0:T(8,128)S(1)} fusion(f32[16,8,1024]{2,1,0:T(8,128)S(1)} %copy-done.1, f32[18,10,1026]{2,1,0:T(8,128)S(1)} %get-tuple-element.32, f32[18,10,1026]{2,1,0:T(8,128)S(1)} %get-tuple-element.31, f32[16,8,1024]{2,1,0:T(8,128)S(1)} %copy-done.2, f32[16,8,1024]{2,1,0:T(8,128)S(1)} %get-tuple-element.25, ...), kind=kLoop, calls=%fused_computation.124 | loop fusion | flops 8249344 | bytes 11042912 | tf_op jit(solution)/shard_map/reduce_sum | solution.py:130
  120.9 0.0 copy-start.3
  120.9 0.7 copy-done.3
  121.6 0.0 all-reduce.6.cloned.1.call-update
  121.6 20.4 %all-reduce.6.cloned.1.call-done = f32[5,8,1024]{2,1,0:T(8,128)} async-done(((f32[5,8,1024]{2,1,0:T(8,128)}), f32[5,8,1024]{2,1,0:T(8,128)}) %all-reduce.6.cloned.1.call-update) | async-done | bytes 163856 | tf_op jit(solution)/shard_map/psum | solution.py:134
  141.9 0.8 slice_divide_fusion
  142.8 4.1 %collective-permute-start.8 = (f32[2,1,1024]{2,1,0:T(1,128)S(1)}, f32[2,1,1024]{2,1,0:T(1,128)S(1)}, u32[]{:S(2)}, u32[]{:S(2)}) collective-permute-start(f32[2,1,1024]{2,1,0:T(1,128)S(1)} %get-tuple-element.51), channel_id=1, source_target_pairs={{0,2},{2,4},{4,6},{6,8},{8,10},{10,12},{12,14},{14,16},{16,18},{18... | collective-permute-start | bytes 24584 | tf_op jit(solution)/shard_map/ppermute | solution.py:16
  146.9 1.9 %collective-permute-start.9 = (f32[2,1,1024]{2,1,0:T(1,128)S(1)}, f32[2,1,1024]{2,1,0:T(1,128)S(1)}, u32[]{:S(2)}, u32[]{:S(2)}) collective-permute-start(f32[2,1,1024]{2,1,0:T(1,128)S(1)} %get-tuple-element.52), channel_id=1, source_target_pairs={{2,0},{4,2},{6,4},{8,6},{10,8},{12,10},{14,12},{16,14},{18,16},{20... | collective-permute-start | bytes 24584 | tf_op jit(solution)/shard_map/ppermute | solution.py:19
  148.8 0.0 collective-permute-done.8
  148.8 3.9 %collective-permute-done.9 = f32[2,1,1024]{2,1,0:T(1,128)S(1)} collective-permute-done((f32[2,1,1024]{2,1,0:T(1,128)S(1)}, f32[2,1,1024]{2,1,0:T(1,128)S(1)}, u32[]{:S(2)}, u32[]{:S(2)}) %collective-permute-start.9) | collective-permute-done | bytes 8224 | tf_op jit(solution)/shard_map/ppermute | solution.py:19
  152.7 0.1 select_maximum_fusion.13
  152.9 1.0 fusion.86
  153.9 1.9 %collective-permute-start.10 = (f32[2,1,1024]{2,1,0:T(1,128)S(1)}, f32[2,1,1024]{2,1,0:T(1,128)S(1)}, u32[]{:S(2)}, u32[]{:S(2)}) collective-permute-start(f32[2,1,1024]{2,1,0:T(1,128)S(1)} %get-tuple-element.49), channel_id=1, source_target_pairs={{0,2},{2,4},{4,6},{6,8},{8,10},{10,12},{12,14},{14,16},{16,18},{18... | collective-permute-start | bytes 24584 | tf_op jit(solution)/shard_map/ppermute | solution.py:16
  155.9 2.4 %collective-permute-start.11 = (f32[2,1,1024]{2,1,0:T(1,128)S(1)}, f32[2,1,1024]{2,1,0:T(1,128)S(1)}, u32[]{:S(2)}, u32[]{:S(2)}) collective-permute-start(f32[2,1,1024]{2,1,0:T(1,128)S(1)} %get-tuple-element.50), channel_id=1, source_target_pairs={{2,0},{4,2},{6,4},{8,6},{10,8},{12,10},{14,12},{16,14},{18,16},{20... | collective-permute-start | bytes 24584 | tf_op jit(solution)/shard_map/ppermute | solution.py:19
  158.3 0.0 collective-permute-done.10
  158.3 3.5 %collective-permute-done.11 = f32[2,1,1024]{2,1,0:T(1,128)S(1)} collective-permute-done((f32[2,1,1024]{2,1,0:T(1,128)S(1)}, f32[2,1,1024]{2,1,0:T(1,128)S(1)}, u32[]{:S(2)}, u32[]{:S(2)}) %collective-permute-start.11) | collective-permute-done | bytes 8224 | tf_op jit(solution)/shard_map/ppermute | solution.py:19
  161.7 0.1 select_maximum_fusion.10
  161.9 1.5 fusion.102
  163.5 0.8 broadcast_add_fusion
  (11 shorter events, 0.2 us)
Async XLA Ops:
  7.2 15.3 %copy-start = (f32[16,8,1024]{2,1,0:T(8,128)S(1)}, f32[16,8,1024]{2,1,0:T(8,128)}, u32[]{:S(2)}) copy-start(f32[16,8,1024]{2,1,0:T(8,128)} %param.5) | copy-start | bytes 1572868
  7.2 134.8 %all-reduce.6.cloned.1.call-start = ((), (), s32[]{:S(2)}) async-start(), calls=%async_computation | async-start | bytes 327680 | tf_op jit(solution)/shard_map/psum | solution.py:134
  22.5 32.0 %copy-start.4 = (f32[5,12]{1,0:T(8,128)S(1)}, f32[5,12]{1,0:T(8,128)}, u32[]{:S(2)}) copy-start(f32[5,12]{1,0:T(8,128)} %param.9) | copy-start | bytes 724
  39.1 5.6 %collective-permute-start = (f32[2,16,1,1024]{3,2,1,0:T(1,128)S(1)}, f32[2,16,1,1024]{3,2,1,0:T(1,128)S(1)}, u32[]{:S(2)}, u32[]{:S(2)}) collective-permute-start(f32[2,16,1,1024]{3,2,1,0:T(1,128)S(1)} %get-tuple-element.41), channel_id=1, source_target_pairs={{0,2},{2,4},{4,6},{6,8},{8,10},{10,12},{12,14},{14,16},{16,18},{18... | collective-permute-start | bytes 393224 | tf_op jit(solution)/shard_map/ppermute | solution.py:16
  42.8 7.2 %collective-permute-start.1 = (f32[2,16,1,1024]{3,2,1,0:T(1,128)S(1)}, f32[2,16,1,1024]{3,2,1,0:T(1,128)S(1)}, u32[]{:S(2)}, u32[]{:S(2)}) collective-permute-start(f32[2,16,1,1024]{3,2,1,0:T(1,128)S(1)} %get-tuple-element.42), channel_id=1, source_target_pairs={{2,0},{4,2},{6,4},{8,6},{10,8},{12,10},{14,12},{16,14},{18,16},{20... | collective-permute-start | bytes 393224 | tf_op jit(solution)/shard_map/ppermute | solution.py:19
  50.1 5.2 %collective-permute-start.2 = (f32[2,1,10,1024]{3,2,1,0:T(8,128)S(1)}, f32[2,1,10,1024]{3,2,1,0:T(8,128)S(1)}, u32[]{:S(2)}, u32[]{:S(2)}) collective-permute-start(f32[2,1,10,1024]{3,2,1,0:T(8,128)S(1)} %get-tuple-element.37), channel_id=1, source_target_pairs={{0,1},{2,3},{4,5},{6,7},{8,9},{10,11},{12,13},{14,15},{16,17},{18,... | collective-permute-start | bytes 245768 | tf_op jit(solution)/shard_map/ppermute | solution.py:16
  53.2 5.7 %collective-permute-start.3 = (f32[2,1,10,1024]{3,2,1,0:T(8,128)S(1)}, f32[2,1,10,1024]{3,2,1,0:T(8,128)S(1)}, u32[]{:S(2)}, u32[]{:S(2)}) collective-permute-start(f32[2,1,10,1024]{3,2,1,0:T(8,128)S(1)} %get-tuple-element.38), channel_id=1, source_target_pairs={{1,0},{3,2},{5,4},{7,6},{9,8},{11,10},{13,12},{15,14},{17,16},{19,... | collective-permute-start | bytes 245768 | tf_op jit(solution)/shard_map/ppermute | solution.py:19
  60.5 1.0 copy-start.1
  60.5 1.2 copy-start.2
  82.3 6.2 %collective-permute-start.4 = (f32[2,16,1,1024]{3,2,1,0:T(1,128)S(1)}, f32[2,16,1,1024]{3,2,1,0:T(1,128)S(1)}, u32[]{:S(2)}, u32[]{:S(2)}) collective-permute-start(f32[2,16,1,1024]{3,2,1,0:T(1,128)S(1)} %get-tuple-element.39), channel_id=1, source_target_pairs={{0,2},{2,4},{4,6},{6,8},{8,10},{10,12},{12,14},{14,16},{16,18},{18... | collective-permute-start | bytes 393224 | tf_op jit(solution)/shard_map/ppermute | solution.py:16
  86.5 7.2 %collective-permute-start.5 = (f32[2,16,1,1024]{3,2,1,0:T(1,128)S(1)}, f32[2,16,1,1024]{3,2,1,0:T(1,128)S(1)}, u32[]{:S(2)}, u32[]{:S(2)}) collective-permute-start(f32[2,16,1,1024]{3,2,1,0:T(1,128)S(1)} %get-tuple-element.40), channel_id=1, source_target_pairs={{2,0},{4,2},{6,4},{8,6},{10,8},{12,10},{14,12},{16,14},{18,16},{20... | collective-permute-start | bytes 393224 | tf_op jit(solution)/shard_map/ppermute | solution.py:19
  93.7 3.2 %collective-permute-start.6 = (f32[2,1,10,1024]{3,2,1,0:T(8,128)S(1)}, f32[2,1,10,1024]{3,2,1,0:T(8,128)S(1)}, u32[]{:S(2)}, u32[]{:S(2)}) collective-permute-start(f32[2,1,10,1024]{3,2,1,0:T(8,128)S(1)} %get-tuple-element.35), channel_id=1, source_target_pairs={{0,1},{2,3},{4,5},{6,7},{8,9},{10,11},{12,13},{14,15},{16,17},{18,... | collective-permute-start | bytes 245768 | tf_op jit(solution)/shard_map/ppermute | solution.py:16
  95.1 5.7 %collective-permute-start.7 = (f32[2,1,10,1024]{3,2,1,0:T(8,128)S(1)}, f32[2,1,10,1024]{3,2,1,0:T(8,128)S(1)}, u32[]{:S(2)}, u32[]{:S(2)}) collective-permute-start(f32[2,1,10,1024]{3,2,1,0:T(8,128)S(1)} %get-tuple-element.36), channel_id=1, source_target_pairs={{1,0},{3,2},{5,4},{7,6},{9,8},{11,10},{13,12},{15,14},{17,16},{19,... | collective-permute-start | bytes 245768 | tf_op jit(solution)/shard_map/ppermute | solution.py:19
  120.9 0.7 copy-start.3
  142.8 6.0 %collective-permute-start.8 = (f32[2,1,1024]{2,1,0:T(1,128)S(1)}, f32[2,1,1024]{2,1,0:T(1,128)S(1)}, u32[]{:S(2)}, u32[]{:S(2)}) collective-permute-start(f32[2,1,1024]{2,1,0:T(1,128)S(1)} %get-tuple-element.51), channel_id=1, source_target_pairs={{0,2},{2,4},{4,6},{6,8},{8,10},{10,12},{12,14},{14,16},{16,18},{18... | collective-permute-start | bytes 24584 | tf_op jit(solution)/shard_map/ppermute | solution.py:16
  146.9 5.9 %collective-permute-start.9 = (f32[2,1,1024]{2,1,0:T(1,128)S(1)}, f32[2,1,1024]{2,1,0:T(1,128)S(1)}, u32[]{:S(2)}, u32[]{:S(2)}) collective-permute-start(f32[2,1,1024]{2,1,0:T(1,128)S(1)} %get-tuple-element.52), channel_id=1, source_target_pairs={{2,0},{4,2},{6,4},{8,6},{10,8},{12,10},{14,12},{16,14},{18,16},{20... | collective-permute-start | bytes 24584 | tf_op jit(solution)/shard_map/ppermute | solution.py:19
  153.9 4.3 %collective-permute-start.10 = (f32[2,1,1024]{2,1,0:T(1,128)S(1)}, f32[2,1,1024]{2,1,0:T(1,128)S(1)}, u32[]{:S(2)}, u32[]{:S(2)}) collective-permute-start(f32[2,1,1024]{2,1,0:T(1,128)S(1)} %get-tuple-element.49), channel_id=1, source_target_pairs={{0,2},{2,4},{4,6},{6,8},{8,10},{10,12},{12,14},{14,16},{16,18},{18... | collective-permute-start | bytes 24584 | tf_op jit(solution)/shard_map/ppermute | solution.py:16
  155.9 5.9 %collective-permute-start.11 = (f32[2,1,1024]{2,1,0:T(1,128)S(1)}, f32[2,1,1024]{2,1,0:T(1,128)S(1)}, u32[]{:S(2)}, u32[]{:S(2)}) collective-permute-start(f32[2,1,1024]{2,1,0:T(1,128)S(1)} %get-tuple-element.50), channel_id=1, source_target_pairs={{2,0},{4,2},{6,4},{8,6},{10,8},{12,10},{14,12},{16,14},{18,16},{20... | collective-permute-start | bytes 24584 | tf_op jit(solution)/shard_map/ppermute | solution.py:19
Sparse Core Ops, SparseCore 0:
  121.7 20.1 all-reduce.5
where the time goes:
time: 173 us; the launch traced here: 171 us
  other arithmetic  72.9 us (42%)
  waiting for transfers between devices  46.1 us (27%)
  starting transfers between devices  29.4 us (17%)
  between operations  14.4 us (8%)
  local copies, waits for them, and re-layouts  8.38 us (5%)
    ppermute x6, waiting for transfers between devices, with_halo(): lax.ppermute(lax.slice_in_dim(block, 0, width, axis=dim), axis, backward)  25.3 us
    psum x1, waiting for transfers between devices, shards(): columns = lax.psum(local_sums, 'depth')  20.4 us
    reduce_sum x1, other arithmetic, shards(): jnp.sum(capacity, axis=0)  19.8 us
    ppermute x6, starting transfers between devices, with_halo(): lax.ppermute(lax.slice_in_dim(block, block.shape[dim] - width, None, axis...  18.4 us
    reduce_sum x1, other arithmetic, shards(): jnp.sum(balance, axis=0)  18.4 us
    another operation x1, other arithmetic, shards(): jnp.stack([pressure, conduct])  16.5 us
    ppermute x6, starting transfers between devices, with_halo(): lax.ppermute(lax.slice_in_dim(block, 0, width, axis=dim), axis, backward)  10.9 us
    reduce_sum x1, other arithmetic, shards(): jnp.sum(params[2], axis=0)  9.63 us
  transfers between devices with their start and end apart: 13, of which 8 were waited for; matrix products, arithmetic and copies ran while one was open for 0% of the time, Pallas kernels for 0%

commit v1 on v0

v1 whole, which is shorter than its diff:
```python
import functools
import math

import jax
import jax.numpy as jnp
from jax import lax
from jax.experimental import pallas as pl
from jax.experimental.pallas import tpu as pltpu
from jax.sharding import PartitionSpec as P

INV_DT = 10.0
RELAX = 0.8
SMALL = 0.04
LOG2E = math.log2(math.e)
LANES = 128
F32 = jnp.float32

T_A, T_N, T_C, T_SK, T_D, T_R, T_CAP, T_RATE = range(8)


def whole(count):
    return [pl.BlockSpec(memory_space=pltpu.VMEM)] * count


def build_table(params_ref, tab_ref):
    kinds = params_ref.shape[1]
    theta_r = params_ref[0:1, :]
    theta_s = params_ref[1:2, :]
    alpha = params_ref[2:3, :]
    shape_n = params_ref[3:4, :]
    k_sat = params_ref[4:5, :]
    shape_m = 1.0 - 1.0 / shape_n
    spread = theta_s - theta_r
    rows = {
        T_A: shape_n * (jnp.log(alpha) * LOG2E),
        T_N: shape_n * (0.5 * LOG2E),
        T_C: shape_m * (-0.25 * LOG2E),
        T_SK: jnp.sqrt(k_sat),
        T_D: spread * INV_DT,
        T_R: theta_r * INV_DT,
        T_CAP: spread * shape_m * shape_n * INV_DT,
        T_RATE: alpha,
    }
    for row_id, value in rows.items():
        tab_ref[row_id, :, 0:kinds] = jnp.broadcast_to(value, (8, kinds))


def lookup(table, kinds):
    rows = []
    for r in range(0, kinds.shape[0], 8):
        cols = []
        for c in range(0, kinds.shape[1], LANES):
            cols.append(
                jnp.take_along_axis(
                    table, kinds[r : r + 8, c : c + LANES], axis=1, mode="promise_in_bounds"
                )
            )
        rows.append(jnp.concatenate(cols, axis=1))
    return rows[0] if len(rows) == 1 else jnp.concatenate(rows, axis=0)


def hydraulics(h, pa, pn, pc, psk):
    q = h * h + SMALL
    u = jnp.exp2(pa + pn * jnp.log(q))
    one_plus = 1.0 + u
    inv = 1.0 / one_plus
    ratio = u * inv
    quarter = jnp.exp2(pc * jnp.log(one_plus))
    w = jnp.exp2((-4.0 * pc) * jnp.log(ratio))
    kappa = psk * quarter * (1.0 - w)
    half = quarter * quarter
    return kappa, half * half, ratio * lax.rsqrt(q)


def kappa_only(h, kinds, tab_ref):
    return hydraulics(
        h,
        lookup(tab_ref[T_A], kinds),
        lookup(tab_ref[T_N], kinds),
        lookup(tab_ref[T_C], kinds),
        lookup(tab_ref[T_SK], kinds),
    )[0]


def pack_kernel(swap, p_ref, soil_ref, params_ref, fwd_ref, bwd_ref, *rest):
    layers, rows, _ = p_ref.shape
    tab_ref = rest[-1]
    build_table(params_ref, tab_ref)
    for out_ref, row in ((fwd_ref, rows - 1), (bwd_ref, 0)):
        h = p_ref[:, row, :]
        out_ref[0] = h
        out_ref[1] = kappa_only(h, soil_ref[:, row, :], tab_ref)
    if swap:
        spots = [jnp.where(lax.axis_index("depth") == 0, layers - 1, 0)]
    else:
        spots = [layers - 1, 0]
    for out_ref, spot in zip(rest[:-1], spots):
        h = p_ref[spot]
        out_ref[0] = h
        out_ref[1] = kappa_only(h, soil_ref[spot], tab_ref)


def row_iota(shape):
    return lax.broadcasted_iota(jnp.int32, shape, 0)


def lane_iota(shape):
    return lax.broadcasted_iota(jnp.int32, shape, 1)


def from_above(x, edge):
    return jnp.where(row_iota(x.shape) == 0, edge, pltpu.roll(x, 1, 0))


def from_below(x, edge):
    last = x.shape[0] - 1
    return jnp.where(row_iota(x.shape) == last, edge, pltpu.roll(x, last, 0))


def from_left(x):
    return jnp.where(lane_iota(x.shape) == 0, 0.0, pltpu.roll(x, 1, 1))


def from_right(x):
    last = x.shape[1] - 1
    return jnp.where(lane_iota(x.shape) == last, 0.0, pltpu.roll(x, last, 1))


def main_kernel(
    swap,
    p_ref,
    theta_ref,
    source_ref,
    soil_ref,
    params_ref,
    lo_ref,
    hi_ref,
    *rest,
):
    layers, rows, width = p_ref.shape
    if swap:
        vert_ref, rest = rest[0], rest[1:]
    else:
        top_ref, bottom_ref, rest = rest[0], rest[1], rest[2:]
    smooth_ref, sums_ref, fwd_ref, bwd_ref, tab_ref, kap_ref, head_ref = rest
    build_table(params_ref, tab_ref)

    if swap:
        d = lax.axis_index("depth")
        vert_k = vert_ref[1]
        kap_ref[0] = jnp.where(d == 0, 0.0, vert_k)
        kap_ref[layers + 1] = jnp.where(d == 0, vert_k, 0.0)
        head_ref[0] = vert_ref[0]
        head_ref[layers + 1] = vert_ref[0]
    else:
        kap_ref[0] = top_ref[1]
        kap_ref[layers + 1] = bottom_ref[1]
        head_ref[0] = top_ref[0]
        head_ref[layers + 1] = bottom_ref[0]

    def first(layer, carry):
        h = p_ref[layer]
        kap_ref[layer + 1] = kappa_only(h, soil_ref[layer], tab_ref)
        head_ref[layer + 1] = h
        return carry

    lax.fori_loop(0, layers, first, 0)

    def step(layer, carry):
        sum_kh, sum_k, sum_cap, sum_rest, sum_rate, flux_x, flux_y = carry
        kinds = soil_ref[layer]
        pa = lookup(tab_ref[T_A], kinds)
        pn = lookup(tab_ref[T_N], kinds)
        pc = lookup(tab_ref[T_C], kinds)
        psk = lookup(tab_ref[T_SK], kinds)
        pd = lookup(tab_ref[T_D], kinds)
        pr = lookup(tab_ref[T_R], kinds)
        pcap = lookup(tab_ref[T_CAP], kinds)
        rate = lookup(tab_ref[T_RATE], kinds)
        h = p_ref[layer]
        kap, sat, over = hydraulics(h, pa, pn, pc, psk)
        fixed = pr - INV_DT * theta_ref[layer] - source_ref[layer]
        k_up = kap_ref[layer]
        k_dn = kap_ref[layer + 2]
        lo_k = lo_ref[1, pl.ds(layer, 1), :]
        hi_k = hi_ref[1, pl.ds(layer, 1), :]
        lo_h = lo_ref[0, pl.ds(layer, 1), :]
        hi_h = hi_ref[0, pl.ds(layer, 1), :]
        g = kap * h
        sum_n = (
            k_up
            + k_dn
            + from_above(kap, lo_k)
            + from_below(kap, hi_k)
            + from_left(kap)
            + from_right(kap)
        )
        sum_g = (
            k_up * head_ref[layer]
            + k_dn * head_ref[layer + 2]
            + from_above(g, lo_k * lo_h)
            + from_below(g, hi_k * hi_h)
            + from_left(g)
            + from_right(g)
        )
        inflow = kap * (sum_g - h * sum_n + (k_up - k_dn))
        balance = pd * sat + fixed - inflow
        diagonal = pcap * sat * over + kap * sum_n
        h = h - RELAX * balance / diagonal
        smooth_ref[layer] = h

        kap, sat, over = hydraulics(h, pa, pn, pc, psk)
        cond = kap * kap
        flux_x = flux_x + kap * from_below(kap, 0.0) * (pltpu.roll(h, rows - 1, 0) - h)
        flux_y = flux_y + kap * from_right(kap) * (pltpu.roll(h, width - 1, 1) - h)
        fwd_ref[pl.ds(layer, 1), :] = h[rows - 1 : rows, :]
        fwd_ref[pl.ds(layers + layer, 1), :] = kap[rows - 1 : rows, :]
        bwd_ref[pl.ds(layer, 1), :] = h[0:1, :]
        bwd_ref[pl.ds(layers + layer, 1), :] = kap[0:1, :]
        return (
            sum_kh + cond * h,
            sum_k + cond,
            sum_cap + pcap * sat * over,
            sum_rest + (pd * sat + fixed),
            sum_rate + rate,
            flux_x,
            flux_y,
        )

    zero = jnp.zeros((rows, width), F32)
    sum_kh, sum_k, sum_cap, sum_rest, sum_rate, flux_x, flux_y = lax.fori_loop(
        0, layers, step, (zero,) * 7
    )
    restricted = (flux_x - from_above(flux_x, 0.0)) + (flux_y - from_left(flux_y)) - sum_rest
    for spot, value in enumerate((sum_kh, sum_k, sum_cap, restricted, sum_rate)):
        sums_ref[spot] = value
    at = 2 * layers
    for out_ref, edge, inner in ((fwd_ref, rows - 1, rows - 2), (bwd_ref, 0, 1)):
        tail = [
            sum_kh[edge : edge + 1],
            sum_k[edge : edge + 1],
            sum_kh[inner : inner + 1],
            sum_k[inner : inner + 1],
            sum_cap[edge : edge + 1],
            restricted[edge : edge + 1],
            sum_rate[edge : edge + 1],
            zero[0:1],
        ]
        out_ref[at : at + 8, :] = jnp.concatenate(tail, axis=0)


def edge_kernel(fwd_ref, bwd_ref, lo_ref, hi_ref, halo_ref):
    layers = (fwd_ref.shape[0] - 8) // 2
    at = 2 * layers
    fluxes = []
    for mine_ref, their_ref in ((bwd_ref, lo_ref), (fwd_ref, hi_ref)):
        flux = (
            mine_ref[layers:at, :]
            * their_ref[layers:at, :]
            * (their_ref[0:layers, :] - mine_ref[0:layers, :])
        )
        fluxes.append(jnp.sum(flux, axis=0, keepdims=True))
    lo = lo_ref[at : at + 8, :]
    hi = hi_ref[at : at + 8, :]
    for side, (block, flux) in enumerate(((lo, fluxes[0]), (hi, fluxes[1]))):
        spot = row_iota(block.shape)
        block = jnp.where(spot == 5, block - flux, block)
        halo_ref[side] = jnp.where(spot == 7, flux, block)


def coarse_kernel(
    depth_total, smooth_ref, sums_ref, their_sums_ref, halo_ref, their_halo_ref, out_ref, head_ref
):
    rows = smooth_ref.shape[1]
    kh, kk, cap, rest, rate = [sums_ref[i] + their_sums_ref[i] for i in range(5)]
    lo = halo_ref[0] + their_halo_ref[0]
    hi = halo_ref[1] + their_halo_ref[1]
    spot = row_iota(rest.shape)
    rest = jnp.where(spot == 0, rest + lo[7:8], rest)
    rest = jnp.where(spot == rows - 1, rest + hi[7:8], rest)

    def pair(i):
        return jnp.where(spot == 0, lo[i : i + 1], jnp.where(spot == rows - 1, hi[i : i + 1], 0.0))

    h_kh, h_k, o_kh, o_k, h_cap, h_rest, h_rate = [pair(i) for i in range(7)]
    edge_lane = lane_iota(rest.shape)

    def sides(x):
        return from_left(x) + from_right(x)

    base = kh / kk
    root = jnp.sqrt(kk)
    h_live = h_k > 0.0
    h_base = jnp.where(h_live, h_kh / jnp.where(h_live, h_k, 1.0), 0.0)
    h_root = jnp.sqrt(h_k)
    o_root = jnp.sqrt(o_k)

    def around(x, halo):
        return from_above(x, halo[0:1]), from_below(x, halo[rows - 1 : rows])

    def flow(head, halo_head, tau, halo_tau):
        tau_u, tau_d = around(tau, halo_tau)
        head_u, head_d = around(head, halo_head)
        tau_l, tau_r = from_left(tau), from_right(tau)
        head_l, head_r = from_left(head), from_right(head)
        inflow = (
            tau_u * (head_u - head)
            + tau_d * (head_d - head)
            + tau_l * (head_l - head)
            + tau_r * (head_r - head)
        )
        return tau * inflow, tau * (tau_u + tau_d + tau_l + tau_r)

    start_in, start_sum = flow(base, h_base, root, h_root)
    rhs = rest - start_in
    first = base + RELAX * rest / (cap + start_sum)
    h_diag = h_cap + h_root * (o_root + root + sides(h_root))
    h_first = h_base + jnp.where(h_live, RELAX * h_rest / jnp.where(h_live, h_diag, 1.0), 0.0)
    half = 0.5 / depth_total
    tau = root * jnp.exp(half * rate * jnp.tanh(first - base))
    h_tau = h_root * jnp.exp(half * h_rate * jnp.tanh(h_first - h_base))
    first_in, first_sum = flow(first, h_first, tau, h_tau)
    first_flow = cap * (first - base) - first_in
    second = first - RELAX * (first_flow - rhs) / (cap + first_sum)
    head_ref[...] = second
    shift = second - base
    out_ref[...] = smooth_ref[...] + shift[None]


def shards(pressure, theta_old, source, soil_type, soil_params):
    layers, rows, width = pressure.shape
    areas = lax.axis_size("area")
    depths = lax.axis_size("depth")
    swap = depths == 2
    forward = [(i, i + 1) for i in range(areas - 1)]
    backward = [(b, a) for a, b in forward]
    down = [(i, i + 1) for i in range(depths - 1)]
    up = [(b, a) for a, b in down]
    swapped = [(0, 1), (1, 0)]

    def shape(*dims):
        return jax.ShapeDtypeStruct(dims, F32)

    params = pltpu.CompilerParams(vmem_limit_bytes=48 << 20)
    tab = pltpu.VMEM((8, 8, LANES), F32)
    verts = 1 if swap else 2
    packed = pl.pallas_call(
        functools.partial(pack_kernel, swap),
        out_shape=[shape(2, layers, width)] * 2 + [shape(2, rows, width)] * verts,
        in_specs=whole(3),
        out_specs=whole(2 + verts),
        scratch_shapes=[tab],
        compiler_params=params,
        name="pack",
    )(pressure, soil_type, soil_params)
    lo = lax.ppermute(packed[0], "area", forward)
    hi = lax.ppermute(packed[1], "area", backward)
    if swap:
        vert = [lax.ppermute(packed[2], "depth", swapped)]
    else:
        vert = [lax.ppermute(packed[2], "depth", down), lax.ppermute(packed[3], "depth", up)]
    smooth, sums, fwd, bwd = pl.pallas_call(
        functools.partial(main_kernel, swap),
        out_shape=[
            shape(layers, rows, width),
            shape(5, rows, width),
            shape(2 * layers + 8, width),
            shape(2 * layers + 8, width),
        ],
        in_specs=whole(7 + verts),
        out_specs=whole(4),
        scratch_shapes=[
            tab,
            pltpu.VMEM((layers + 2, rows, width), F32),
            pltpu.VMEM((layers + 2, rows, width), F32),
        ],
        compiler_params=params,
        name="fine",
    )(pressure, theta_old, source, soil_type, soil_params, lo, hi, *vert)
    lo = lax.ppermute(fwd, "area", forward)
    hi = lax.ppermute(bwd, "area", backward)
    if swap:
        their_sums = lax.ppermute(sums, "depth", swapped)
    else:
        their_sums = lax.psum(sums, "depth") - sums
    halo = pl.pallas_call(
        edge_kernel,
        out_shape=shape(2, 8, width),
        in_specs=whole(4),
        out_specs=whole(1)[0],
        compiler_params=params,
        name="edge",
    )(fwd, bwd, lo, hi)
    if swap:
        their_halo = lax.ppermute(halo, "depth", swapped)
    else:
        their_halo = lax.psum(halo, "depth") - halo
    out, head = pl.pallas_call(
        functools.partial(coarse_kernel, layers * depths),
        out_shape=[shape(layers, rows, width), shape(rows, width)],
        in_specs=whole(5),
        out_specs=whole(2),
        compiler_params=params,
        name="coarse",
    )(smooth, sums, their_sums, halo, their_halo)
    return out, head


def solution(mesh):
    in_specs = (
        P("depth", "area", None),
        P("depth", "area", None),
        P("depth", "area", None),
        P("depth", "area", None),
        P(),
    )
    out_specs = (P("depth", "area", None), P("area", None))
    return jax.shard_map(shards, mesh=mesh, in_specs=in_specs, out_specs=out_specs, check_vma=False)
```

time: 173 us -> 39.8 us (0.23)
  other arithmetic: 72.9 us -> 0 us
  waiting for transfers between devices: 46.1 us -> 10.2 us
  starting transfers between devices: 29.4 us -> 15 us
  between operations: 14.4 us -> 0.69 us
  Pallas kernels: 0 us -> 10.8 us
  local copies, waits for them, and re-layouts: 8.38 us -> 2.77 us
    reduce_sum x4 -> x0, other arithmetic: 48.4 us -> none  [the longest x1 19.8 us: shards(): jnp.sum(capacity, axis=0)]
    psum x1 -> x0, waiting for transfers between devices: 20.4 us -> none  [shards(): columns = lax.psum(local_sums, 'depth')]
    another operation x2 -> x0, other arithmetic: 17.5 us -> none  [the longest x1 16.5 us: shards(): jnp.stack([pressure, conduct])]
    ppermute x12 -> x7, waiting for transfers between devices: 25.8 us -> 10.2 us  [the longest x1 4.33 us: shards(): hi = lax.ppermute(bwd, 'area', backward)]
    ppermute x12 -> x7, starting transfers between devices: 29.3 us -> 15 us  [the longest x1 3.71 us: shards(): lo = lax.ppermute(packed[0], 'area', forward)]
    pallas_call x0 -> x4, Pallas kernels: none -> 10.8 us  [the longest x1 9.08 us: shards(): pl.pallas_call(functools.partial(main_kernel, swap), out_shape=[shape(lay...]
    slice x4 -> x0, local copies, waits for them, and re-layouts: 6.31 us -> none  [soil_fields(): soil_params[row_id, kind_id]]
    concatenate x4 -> x0, other arithmetic: 3.38 us -> none  [with_halo(): block = jnp.concatenate([low, block, high], axis=dim)]
  transfers between devices with their start and end apart: 13 -> 7, of which waited for: 8 -> 4; matrix products, arithmetic and copies ran while one was open for 0% -> 0% of each run, Pallas kernels for 0% -> 0%
where the time goes in v1:
time: 39.8 us; the launch traced here: 39.4 us
  starting transfers between devices  15 us (38%)
  Pallas kernels  10.8 us (27%)
  waiting for transfers between devices  10.2 us (26%)
  local copies, waits for them, and re-layouts  2.77 us (7%)
  between operations  0.69 us (2%)
    pallas_call x1, Pallas kernels, shards(): pl.pallas_call(functools.partial(main_kernel, swap), out_shape=[shape(lay...  9.08 us
    ppermute x1, waiting for transfers between devices, shards(): hi = lax.ppermute(bwd, 'area', backward)  4.33 us
    ppermute x1, starting transfers between devices, shards(): lo = lax.ppermute(packed[0], 'area', forward)  3.71 us
    ppermute x1, starting transfers between devices, shards(): lo = lax.ppermute(fwd, 'area', forward)  3.63 us
    unnamed x10, local copies, waits for them, and re-layouts  2.77 us
    ppermute x1, waiting for transfers between devices, shards(): hi = lax.ppermute(packed[1], 'area', backward)  2.07 us
    ppermute x1, starting transfers between devices, shards(): hi = lax.ppermute(packed[1], 'area', backward)  1.92 us
    ppermute x1, starting transfers between devices, shards(): hi = lax.ppermute(bwd, 'area', backward)  1.92 us
  transfers between devices with their start and end apart: 7, of which 4 were waited for; matrix products, arithmetic and copies ran while one was open for 0% of the time, Pallas kernels for 0%

profile of v1, /device:TPU:5, one launch (start us, length us, event | category | flops | bytes accessed | tf_op | source)
XLA Modules:
  0.0 39.4 jit_solution(5502379290341698841)
XLA Ops:
  0.6 0.0 copy-start
  0.6 1.0 %copy-done = f32[16,8,1024]{2,1,0:T(8,128)S(1)} copy-done((f32[16,8,1024]{2,1,0:T(8,128)S(1)}, f32[16,8,1024]{2,1,0:T(8,128)}, u32[]{:S(2)}) %copy-start) | copy-done | bytes 524312
  1.7 0.0 copy-start.1
  1.7 1.0 %copy-done.1 = s32[16,8,1024]{2,1,0:T(8,128)S(1)} copy-done((s32[16,8,1024]{2,1,0:T(8,128)S(1)}, s32[16,8,1024]{2,1,0:T(8,128)}, u32[]{:S(2)}) %copy-start.1) | copy-done | bytes 524312
  2.7 0.0 copy-start.4
  2.7 0.7 %copy-done.4 = f32[5,12]{1,0:T(8,128)S(1)} copy-done((f32[5,12]{1,0:T(8,128)S(1)}, f32[5,12]{1,0:T(8,128)}, u32[]{:S(2)}) %copy-start.4) | copy-done | bytes 264
  3.4 0.0 copy-start.2
  3.4 0.0 copy-start.3
  3.4 0.6 %pack.1 = (f32[2,16,1024]{2,1,0:T(8,128)S(1)}, f32[2,16,1024]{2,1,0:T(8,128)S(1)}, f32[2,8,1024]{2,1,0:T(8,128)S(1)}) custom-call(f32[16,8,1024]{2,1,0:T(8,128)S(1)} %copy-done, s32[16,8,1024]{2,1,0:T(8,128)S(1)} %copy-done.1, f32[5,12]{1,0:T(8,128)S(1)} %copy-done.4), custom_call_target="tpu_custom_call" | custom-call | tf_op jit(solution)/shard_map/pack/pallas_call | solution.py:347
  4.0 3.7 %collective-permute-start = (f32[2,16,1024]{2,1,0:T(8,128)S(1)}, f32[2,16,1024]{2,1,0:T(8,128)S(1)}, u32[]{:S(2)}, u32[]{:S(2)}) collective-permute-start(f32[2,16,1024]{2,1,0:T(8,128)S(1)} %get-tuple-element.9), channel_id=1, source_target_pairs={{0,2},{2,4},{4,6},{6,8},{8,10},{10,12},{12,14},{14,16},{16,18},{18... | collective-permute-start | bytes 393224 | tf_op jit(solution)/shard_map/ppermute | solution.py:356
  7.7 1.9 %collective-permute-start.1 = (f32[2,16,1024]{2,1,0:T(8,128)S(1)}, f32[2,16,1024]{2,1,0:T(8,128)S(1)}, u32[]{:S(2)}, u32[]{:S(2)}) collective-permute-start(f32[2,16,1024]{2,1,0:T(8,128)S(1)} %get-tuple-element.10), channel_id=1, source_target_pairs={{2,0},{4,2},{6,4},{8,6},{10,8},{12,10},{14,12},{16,14},{18,16},{20... | collective-permute-start | bytes 393224 | tf_op jit(solution)/shard_map/ppermute | solution.py:357
  9.6 1.3 %collective-permute-start.2 = (f32[2,8,1024]{2,1,0:T(8,128)S(1)}, f32[2,8,1024]{2,1,0:T(8,128)S(1)}, u32[]{:S(2)}, u32[]{:S(2)}) collective-permute-start(f32[2,8,1024]{2,1,0:T(8,128)S(1)} %get-tuple-element.11), channel_id=1, source_target_pairs={{0,1},{1,0},{2,3},{3,2},{4,5},{5,4},{6,7},{7,6},{8,9},{9,8},{10,11... | collective-permute-start | bytes 196616 | tf_op jit(solution)/shard_map/ppermute | solution.py:359
  10.9 1.9 %collective-permute-done.2.rest_0_ = f32[2,8,1024]{2,1,0:T(8,128)S(1)} collective-permute-done((f32[2,8,1024]{2,1,0:T(8,128)S(1)}, f32[2,8,1024]{2,1,0:T(8,128)S(1)}, u32[]{:S(2)}, u32[]{:S(2)}) %collective-permute-start.2) | collective-permute-done | bytes 65568 | tf_op jit(solution)/shard_map/ppermute | solution.py:359
  12.8 0.0 collective-permute-done.lo_ref
  12.8 2.1 %collective-permute-done.1.hi_ref = f32[2,16,1024]{2,1,0:T(8,128)S(1)} collective-permute-done((f32[2,16,1024]{2,1,0:T(8,128)S(1)}, f32[2,16,1024]{2,1,0:T(8,128)S(1)}, u32[]{:S(2)}, u32[]{:S(2)}) %collective-permute-start.1) | collective-permute-done | bytes 131104 | tf_op jit(solution)/shard_map/ppermute | solution.py:357
  14.9 0.0 copy-done.2
  14.9 0.0 copy-done.3
  14.9 9.1 %fine.1 = (f32[16,8,1024]{2,1,0:T(8,128)S(1)}, f32[5,8,1024]{2,1,0:T(8,128)S(1)}, f32[40,1024]{1,0:T(8,128)S(1)}, f32[40,1024]{1,0:T(8,128)S(1)}) custom-call(f32[16,8,1024]{2,1,0:T(8,128)S(1)} %copy-done, f32[16,8,1024]{2,1,0:T(8,128)S(1)} %copy-done.2, f32[16,8,1024]{2,1,0:T(8,128)S(1)} %copy-done.3, s32[16,8,1024]{2,1,0:T(8,128)S(1)} %copy-done.1, ...), custom_call_target="tpu_custom_call" | custom-call | tf_op jit(solution)/shard_map/fine/pallas_call | solution.py:362
  24.0 3.6 %collective-permute-start.4 = (f32[40,1024]{1,0:T(8,128)S(1)}, f32[40,1024]{1,0:T(8,128)S(1)}, u32[]{:S(2)}, u32[]{:S(2)}) collective-permute-start(f32[40,1024]{1,0:T(8,128)S(1)} %get-tuple-element.14.fwd_ref), channel_id=1, source_target_pairs={{0,2},{2,4},{4,6},{6,8},{8,10},{10,12},{12,14},{14,16},{16,18},{18... | collective-permute-start | bytes 491528 | tf_op jit(solution)/shard_map/ppermute | solution.py:380
  27.6 1.9 %collective-permute-start.5 = (f32[40,1024]{1,0:T(8,128)S(1)}, f32[40,1024]{1,0:T(8,128)S(1)}, u32[]{:S(2)}, u32[]{:S(2)}) collective-permute-start(f32[40,1024]{1,0:T(8,128)S(1)} %get-tuple-element.15.bwd_ref), channel_id=1, source_target_pairs={{2,0},{4,2},{6,4},{8,6},{10,8},{12,10},{14,12},{16,14},{18,16},{20... | collective-permute-start | bytes 491528 | tf_op jit(solution)/shard_map/ppermute | solution.py:381
  29.5 1.3 %collective-permute-start.3 = (f32[5,8,1024]{2,1,0:T(8,128)S(1)}, f32[5,8,1024]{2,1,0:T(8,128)S(1)}, u32[]{:S(2)}, u32[]{:S(2)}) collective-permute-start(f32[5,8,1024]{2,1,0:T(8,128)S(1)} %get-tuple-element.13.sums_ref), channel_id=1, source_target_pairs={{0,1},{1,0},{2,3},{3,2},{4,5},{5,4},{6,7},{7,6},{8,9},{9,8},{10,11... | collective-permute-start | bytes 491528 | tf_op jit(solution)/shard_map/ppermute | solution.py:383
  30.8 0.0 collective-permute-done.4.lo_ref
  30.8 4.3 %collective-permute-done.5.hi_ref = f32[40,1024]{1,0:T(8,128)S(1)} collective-permute-done((f32[40,1024]{1,0:T(8,128)S(1)}, f32[40,1024]{1,0:T(8,128)S(1)}, u32[]{:S(2)}, u32[]{:S(2)}) %collective-permute-start.5) | collective-permute-done | bytes 163872 | tf_op jit(solution)/shard_map/ppermute | solution.py:381
  35.1 0.1 edge.1.halo_ref
  35.2 1.3 %collective-permute-start.6 = (f32[2,8,1024]{2,1,0:T(8,128)S(1)}, f32[2,8,1024]{2,1,0:T(8,128)S(1)}, u32[]{:S(2)}, u32[]{:S(2)}) collective-permute-start(f32[2,8,1024]{2,1,0:T(8,128)S(1)} %edge.1.halo_ref), channel_id=1, source_target_pairs={{0,1},{1,0},{2,3},{3,2},{4,5},{5,4},{6,7},{7,6},{8,9},{9,8},{10,11... | collective-permute-start | bytes 196616 | tf_op jit(solution)/shard_map/ppermute | solution.py:395
  36.5 0.0 collective-permute-done.3.their_sums_ref
  36.5 1.9 %collective-permute-done.6.their_halo_ref = f32[2,8,1024]{2,1,0:T(8,128)S(1)} collective-permute-done((f32[2,8,1024]{2,1,0:T(8,128)S(1)}, f32[2,8,1024]{2,1,0:T(8,128)S(1)}, u32[]{:S(2)}, u32[]{:S(2)}) %collective-permute-start.6) | collective-permute-done | bytes 65568 | tf_op jit(solution)/shard_map/ppermute | solution.py:395
  38.4 1.1 %coarse.1 = (f32[16,8,1024]{2,1,0:T(8,128)}, f32[8,1024]{1,0:T(8,128)}) custom-call(f32[16,8,1024]{2,1,0:T(8,128)S(1)} %get-tuple-element.12.smooth_ref, f32[5,8,1024]{2,1,0:T(8,128)S(1)} %get-tuple-element.13.sums_ref, f32[5,8,1024]{2,1,0:T(8,128)S(1)} %collective-permute-done.3.their_sums_ref, f32[2,8,1024]{2,1,0:T(8,128)S(1)} %edge.1.halo_ref, ...), custom_call_target="tpu_custom_call" | custom-call | tf_op jit(solution)/shard_map/coarse/pallas_call | solution.py:398
Async XLA Ops:
  0.6 1.0 %copy-start = (f32[16,8,1024]{2,1,0:T(8,128)S(1)}, f32[16,8,1024]{2,1,0:T(8,128)}, u32[]{:S(2)}) copy-start(f32[16,8,1024]{2,1,0:T(8,128)} %p_ref.3) | copy-start | bytes 1572868
  1.7 1.0 %copy-start.1 = (s32[16,8,1024]{2,1,0:T(8,128)S(1)}, s32[16,8,1024]{2,1,0:T(8,128)}, u32[]{:S(2)}) copy-start(s32[16,8,1024]{2,1,0:T(8,128)} %soil_ref.3) | copy-start | bytes 1572868
  2.7 0.7 %copy-start.4 = (f32[5,12]{1,0:T(8,128)S(1)}, f32[5,12]{1,0:T(8,128)}, u32[]{:S(2)}) copy-start(f32[5,12]{1,0:T(8,128)} %params_ref.3) | copy-start | bytes 724
  3.4 11.5 %copy-start.2 = (f32[16,8,1024]{2,1,0:T(8,128)S(1)}, f32[16,8,1024]{2,1,0:T(8,128)}, u32[]{:S(2)}) copy-start(f32[16,8,1024]{2,1,0:T(8,128)} %theta_ref.1) | copy-start | bytes 1572868
  3.4 11.5 %copy-start.3 = (f32[16,8,1024]{2,1,0:T(8,128)S(1)}, f32[16,8,1024]{2,1,0:T(8,128)}, u32[]{:S(2)}) copy-start(f32[16,8,1024]{2,1,0:T(8,128)} %source_ref.1) | copy-start | bytes 1572868
  4.0 8.8 %collective-permute-start = (f32[2,16,1024]{2,1,0:T(8,128)S(1)}, f32[2,16,1024]{2,1,0:T(8,128)S(1)}, u32[]{:S(2)}, u32[]{:S(2)}) collective-permute-start(f32[2,16,1024]{2,1,0:T(8,128)S(1)} %get-tuple-element.9), channel_id=1, source_target_pairs={{0,2},{2,4},{4,6},{6,8},{8,10},{10,12},{12,14},{14,16},{16,18},{18... | collective-permute-start | bytes 393224 | tf_op jit(solution)/shard_map/ppermute | solution.py:356
  7.7 7.2 %collective-permute-start.1 = (f32[2,16,1024]{2,1,0:T(8,128)S(1)}, f32[2,16,1024]{2,1,0:T(8,128)S(1)}, u32[]{:S(2)}, u32[]{:S(2)}) collective-permute-start(f32[2,16,1024]{2,1,0:T(8,128)S(1)} %get-tuple-element.10), channel_id=1, source_target_pairs={{2,0},{4,2},{6,4},{8,6},{10,8},{12,10},{14,12},{16,14},{18,16},{20... | collective-permute-start | bytes 393224 | tf_op jit(solution)/shard_map/ppermute | solution.py:357
  9.6 3.2 %collective-permute-start.2 = (f32[2,8,1024]{2,1,0:T(8,128)S(1)}, f32[2,8,1024]{2,1,0:T(8,128)S(1)}, u32[]{:S(2)}, u32[]{:S(2)}) collective-permute-start(f32[2,8,1024]{2,1,0:T(8,128)S(1)} %get-tuple-element.11), channel_id=1, source_target_pairs={{0,1},{1,0},{2,3},{3,2},{4,5},{5,4},{6,7},{7,6},{8,9},{9,8},{10,11... | collective-permute-start | bytes 196616 | tf_op jit(solution)/shard_map/ppermute | solution.py:359
  24.0 6.8 %collective-permute-start.4 = (f32[40,1024]{1,0:T(8,128)S(1)}, f32[40,1024]{1,0:T(8,128)S(1)}, u32[]{:S(2)}, u32[]{:S(2)}) collective-permute-start(f32[40,1024]{1,0:T(8,128)S(1)} %get-tuple-element.14.fwd_ref), channel_id=1, source_target_pairs={{0,2},{2,4},{4,6},{6,8},{8,10},{10,12},{12,14},{14,16},{16,18},{18... | collective-permute-start | bytes 491528 | tf_op jit(solution)/shard_map/ppermute | solution.py:380
  27.6 7.5 %collective-permute-start.5 = (f32[40,1024]{1,0:T(8,128)S(1)}, f32[40,1024]{1,0:T(8,128)S(1)}, u32[]{:S(2)}, u32[]{:S(2)}) collective-permute-start(f32[40,1024]{1,0:T(8,128)S(1)} %get-tuple-element.15.bwd_ref), channel_id=1, source_target_pairs={{2,0},{4,2},{6,4},{8,6},{10,8},{12,10},{14,12},{16,14},{18,16},{20... | collective-permute-start | bytes 491528 | tf_op jit(solution)/shard_map/ppermute | solution.py:381
  29.5 6.9 %collective-permute-start.3 = (f32[5,8,1024]{2,1,0:T(8,128)S(1)}, f32[5,8,1024]{2,1,0:T(8,128)S(1)}, u32[]{:S(2)}, u32[]{:S(2)}) collective-permute-start(f32[5,8,1024]{2,1,0:T(8,128)S(1)} %get-tuple-element.13.sums_ref), channel_id=1, source_target_pairs={{0,1},{1,0},{2,3},{3,2},{4,5},{5,4},{6,7},{7,6},{8,9},{9,8},{10,11... | collective-permute-start | bytes 491528 | tf_op jit(solution)/shard_map/ppermute | solution.py:383
  35.2 3.2 %collective-permute-start.6 = (f32[2,8,1024]{2,1,0:T(8,128)S(1)}, f32[2,8,1024]{2,1,0:T(8,128)S(1)}, u32[]{:S(2)}, u32[]{:S(2)}) collective-permute-start(f32[2,8,1024]{2,1,0:T(8,128)S(1)} %edge.1.halo_ref), channel_id=1, source_target_pairs={{0,1},{1,0},{2,3},{3,2},{4,5},{5,4},{6,7},{7,6},{8,9},{9,8},{10,11... | collective-permute-start | bytes 196616 | tf_op jit(solution)/shard_map/ppermute | solution.py:395

commit v2 on v1

--- a/solution.py
+++ b/solution.py
@@ -82,14 +82,22 @@
     )[0]
 
 
-def pack_kernel(swap, p_ref, soil_ref, params_ref, fwd_ref, bwd_ref, *rest):
+def even_area():
+    return lax.rem(lax.axis_index("area"), 2) == 0
+
+
+def pack_kernel(swap, p_ref, soil_ref, params_ref, even_ref, odd_ref, *rest):
     layers, rows, _ = p_ref.shape
     tab_ref = rest[-1]
     build_table(params_ref, tab_ref)
-    for out_ref, row in ((fwd_ref, rows - 1), (bwd_ref, 0)):
-        h = p_ref[:, row, :]
-        out_ref[0] = h
-        out_ref[1] = kappa_only(h, soil_ref[:, row, :], tab_ref)
+    even = even_area()
+    low_h, high_h = p_ref[:, 0, :], p_ref[:, rows - 1, :]
+    low_k = kappa_only(low_h, soil_ref[:, 0, :], tab_ref)
+    high_k = kappa_only(high_h, soil_ref[:, rows - 1, :], tab_ref)
+    even_ref[0] = jnp.where(even, high_h, low_h)
+    even_ref[1] = jnp.where(even, high_k, low_k)
+    odd_ref[0] = jnp.where(even, low_h, high_h)
+    odd_ref[1] = jnp.where(even, low_k, high_k)
     if swap:
         spots = [jnp.where(lax.axis_index("depth") == 0, layers - 1, 0)]
     else:
@@ -133,8 +141,8 @@
     source_ref,
     soil_ref,
     params_ref,
-    lo_ref,
-    hi_ref,
+    from_even_ref,
+    from_odd_ref,
     *rest,
 ):
     layers, rows, width = p_ref.shape
@@ -142,8 +150,9 @@
         vert_ref, rest = rest[0], rest[1:]
     else:
         top_ref, bottom_ref, rest = rest[0], rest[1], rest[2:]
-    smooth_ref, sums_ref, fwd_ref, bwd_ref, tab_ref, kap_ref, head_ref = rest
+    smooth_ref, sums_ref, to_even_ref, to_odd_ref, tab_ref, kap_ref, head_ref = rest
     build_table(params_ref, tab_ref)
+    even = even_area()
 
     if swap:
         d = lax.axis_index("depth")
@@ -182,10 +191,14 @@
         fixed = pr - INV_DT * theta_ref[layer] - source_ref[layer]
         k_up = kap_ref[layer]
         k_dn = kap_ref[layer + 2]
-        lo_k = lo_ref[1, pl.ds(layer, 1), :]
-        hi_k = hi_ref[1, pl.ds(layer, 1), :]
-        lo_h = lo_ref[0, pl.ds(layer, 1), :]
-        hi_h = hi_ref[0, pl.ds(layer, 1), :]
+        even_k = from_even_ref[1, pl.ds(layer, 1), :]
+        odd_k = from_odd_ref[1, pl.ds(layer, 1), :]
+        even_h = from_even_ref[0, pl.ds(layer, 1), :]
+        odd_h = from_odd_ref[0, pl.ds(layer, 1), :]
+        lo_k = jnp.where(even, odd_k, even_k)
+        hi_k = jnp.where(even, even_k, odd_k)
+        lo_h = jnp.where(even, odd_h, even_h)
+        hi_h = jnp.where(even, even_h, odd_h)
         g = kap * h
         sum_n = (
             k_up
@@ -213,10 +226,10 @@
         cond = kap * kap
         flux_x = flux_x + kap * from_below(kap, 0.0) * (pltpu.roll(h, rows - 1, 0) - h)
         flux_y = flux_y + kap * from_right(kap) * (pltpu.roll(h, width - 1, 1) - h)
-        fwd_ref[pl.ds(layer, 1), :] = h[rows - 1 : rows, :]
-        fwd_ref[pl.ds(layers + layer, 1), :] = kap[rows - 1 : rows, :]
-        bwd_ref[pl.ds(layer, 1), :] = h[0:1, :]
-        bwd_ref[pl.ds(layers + layer, 1), :] = kap[0:1, :]
+        for at, value in ((0, h), (layers, kap)):
+            low, high = value[0:1, :], value[rows - 1 : rows, :]
+            to_even_ref[pl.ds(at + layer, 1), :] = jnp.where(even, high, low)
+            to_odd_ref[pl.ds(at + layer, 1), :] = jnp.where(even, low, high)
         return (
             sum_kh + cond * h,
             sum_k + cond,
@@ -235,7 +248,8 @@
     for spot, value in enumerate((sum_kh, sum_k, sum_cap, restricted, sum_rate)):
         sums_ref[spot] = value
     at = 2 * layers
-    for out_ref, edge, inner in ((fwd_ref, rows - 1, rows - 2), (bwd_ref, 0, 1)):
+    tails = []
+    for edge, inner in ((rows - 1, rows - 2), (0, 1)):
         tail = [
             sum_kh[edge : edge + 1],
             sum_k[edge : edge + 1],
@@ -246,23 +260,25 @@
             sum_rate[edge : edge + 1],
             zero[0:1],
         ]
-        out_ref[at : at + 8, :] = jnp.concatenate(tail, axis=0)
-
-
-def edge_kernel(fwd_ref, bwd_ref, lo_ref, hi_ref, halo_ref):
-    layers = (fwd_ref.shape[0] - 8) // 2
+        tails.append(jnp.concatenate(tail, axis=0))
+    high, low = tails
+    to_even_ref[at : at + 8, :] = jnp.where(even, high, low)
+    to_odd_ref[at : at + 8, :] = jnp.where(even, low, high)
+
+
+def edge_kernel(to_even_ref, to_odd_ref, from_even_ref, from_odd_ref, halo_ref):
+    layers = (to_even_ref.shape[0] - 8) // 2
     at = 2 * layers
-    fluxes = []
-    for mine_ref, their_ref in ((bwd_ref, lo_ref), (fwd_ref, hi_ref)):
+    for side, (mine_ref, their_ref) in enumerate(
+        ((to_even_ref, from_even_ref), (to_odd_ref, from_odd_ref))
+    ):
         flux = (
             mine_ref[layers:at, :]
             * their_ref[layers:at, :]
             * (their_ref[0:layers, :] - mine_ref[0:layers, :])
         )
-        fluxes.append(jnp.sum(flux, axis=0, keepdims=True))
-    lo = lo_ref[at : at + 8, :]
-    hi = hi_ref[at : at + 8, :]
-    for side, (block, flux) in enumerate(((lo, fluxes[0]), (hi, fluxes[1]))):
+        flux = jnp.sum(flux, axis=0, keepdims=True)
+        block = their_ref[at : at + 8, :]
         spot = row_iota(block.shape)
         block = jnp.where(spot == 5, block - flux, block)
         halo_ref[side] = jnp.where(spot == 7, flux, block)
@@ -273,8 +289,11 @@
 ):
     rows = smooth_ref.shape[1]
     kh, kk, cap, rest, rate = [sums_ref[i] + their_sums_ref[i] for i in range(5)]
-    lo = halo_ref[0] + their_halo_ref[0]
-    hi = halo_ref[1] + their_halo_ref[1]
+    by_even = halo_ref[0] + their_halo_ref[0]
+    by_odd = halo_ref[1] + their_halo_ref[1]
+    even = even_area()
+    lo = jnp.where(even, by_odd, by_even)
+    hi = jnp.where(even, by_even, by_odd)
     spot = row_iota(rest.shape)
     rest = jnp.where(spot == 0, rest + lo[7:8], rest)
     rest = jnp.where(spot == rows - 1, rest + hi[7:8], rest)
@@ -332,8 +351,8 @@
     areas = lax.axis_size("area")
     depths = lax.axis_size("depth")
     swap = depths == 2
-    forward = [(i, i + 1) for i in range(areas - 1)]
-    backward = [(b, a) for a, b in forward]
+    even_pairs = [p for i in range(0, areas - 1, 2) for p in ((i, i + 1), (i + 1, i))]
+    odd_pairs = [p for i in range(1, areas - 1, 2) for p in ((i, i + 1), (i + 1, i))]
     down = [(i, i + 1) for i in range(depths - 1)]
     up = [(b, a) for a, b in down]
     swapped = [(0, 1), (1, 0)]
@@ -353,13 +372,13 @@
         compiler_params=params,
         name="pack",
     )(pressure, soil_type, soil_params)
-    lo = lax.ppermute(packed[0], "area", forward)
-    hi = lax.ppermute(packed[1], "area", backward)
+    from_even = lax.ppermute(packed[0], "area", even_pairs)
+    from_odd = lax.ppermute(packed[1], "area", odd_pairs)
     if swap:
         vert = [lax.ppermute(packed[2], "depth", swapped)]
     else:
         vert = [lax.ppermute(packed[2], "depth", down), lax.ppermute(packed[3], "depth", up)]
-    smooth, sums, fwd, bwd = pl.pallas_call(
+    smooth, sums, to_even, to_odd = pl.pallas_call(
         functools.partial(main_kernel, swap),
         out_shape=[
             shape(layers, rows, width),
@@ -376,13 +395,13 @@
         ],
         compiler_params=params,
         name="fine",
-    )(pressure, theta_old, source, soil_type, soil_params, lo, hi, *vert)
-    lo = lax.ppermute(fwd, "area", forward)
-    hi = lax.ppermute(bwd, "area", backward)
+    )(pressure, theta_old, source, soil_type, soil_params, from_even, from_odd, *vert)
+    from_even = lax.ppermute(to_even, "area", even_pairs)
+    from_odd = lax.ppermute(to_odd, "area", odd_pairs)
     if swap:
         their_sums = lax.ppermute(sums, "depth", swapped)
     else:
-        their_sums = lax.psum(sums, "depth") - sums
+        sums, their_sums = lax.psum(sums, "depth"), jnp.zeros_like(sums)
     halo = pl.pallas_call(
         edge_kernel,
         out_shape=shape(2, 8, width),
@@ -390,11 +409,11 @@
         out_specs=whole(1)[0],
         compiler_params=params,
         name="edge",
-    )(fwd, bwd, lo, hi)
+    )(to_even, to_odd, from_even, from_odd)
     if swap:
         their_halo = lax.ppermute(halo, "depth", swapped)
     else:
-        their_halo = lax.psum(halo, "depth") - halo
+        halo, their_halo = lax.psum(halo, "depth"), jnp.zeros_like(halo)
     out, head = pl.pallas_call(
         functools.partial(coarse_kernel, layers * depths),
         out_shape=[shape(layers, rows, width), shape(rows, width)],

time: 39.8 us -> 35.8 us (0.90)
  the two profiles are of different devices: /device:TPU:5 before, /device:TPU:27 now
where the time goes in v2:
time: 35.8 us; the launch traced here: 35.6 us
  waiting for transfers between devices  14.1 us (39%)
  Pallas kernels  11 us (31%)
  starting transfers between devices  7.05 us (20%)
  local copies, waits for them, and re-layouts  2.77 us (8%)
  between operations  0.68 us (2%)
    pallas_call x1, Pallas kernels, shards(): pl.pallas_call(functools.partial(main_kernel, swap), out_shape=[shape(lay...  9.33 us
    ppermute x1, waiting for transfers between devices, shards(): from_odd = lax.ppermute(to_odd, 'area', odd_pairs)  5.96 us
    ppermute x1, waiting for transfers between devices, shards(): their_halo = lax.ppermute(halo, 'depth', swapped)  3.79 us
    ppermute x1, waiting for transfers between devices, shards(): vert = [lax.ppermute(packed[2], 'depth', swapped)]  3.16 us
    ppermute x1, starting transfers between devices, shards(): from_odd = lax.ppermute(packed[1], 'area', odd_pairs)  3.05 us
    unnamed x10, local copies, waits for them, and re-layouts  2.77 us
    ppermute x1, starting transfers between devices, shards(): from_odd = lax.ppermute(to_odd, 'area', odd_pairs)  2.15 us
    ppermute x1, waiting for transfers between devices, shards(): from_odd = lax.ppermute(packed[1], 'area', odd_pairs)  1.14 us
  transfers between devices with their start and end apart: 7, of which 4 were waited for; matrix products, arithmetic and copies ran while one was open for 0% of the time, Pallas kernels for 0%

profile of v2, /device:TPU:27, one launch (start us, length us, event | category | flops | bytes accessed | tf_op | source)
XLA Modules:
  0.0 35.6 jit_solution(1497778156018831619)
XLA Ops:
  0.6 0.0 copy-start
  0.6 1.0 %copy-done = f32[16,8,1024]{2,1,0:T(8,128)S(1)} copy-done((f32[16,8,1024]{2,1,0:T(8,128)S(1)}, f32[16,8,1024]{2,1,0:T(8,128)}, u32[]{:S(2)}) %copy-start) | copy-done | bytes 524312
  1.7 0.0 copy-start.1
  1.7 1.0 %copy-done.1 = s32[16,8,1024]{2,1,0:T(8,128)S(1)} copy-done((s32[16,8,1024]{2,1,0:T(8,128)S(1)}, s32[16,8,1024]{2,1,0:T(8,128)}, u32[]{:S(2)}) %copy-start.1) | copy-done | bytes 524312
  2.7 0.0 copy-start.4
  2.7 0.7 %copy-done.4 = f32[5,12]{1,0:T(8,128)S(1)} copy-done((f32[5,12]{1,0:T(8,128)S(1)}, f32[5,12]{1,0:T(8,128)}, u32[]{:S(2)}) %copy-start.4) | copy-done | bytes 264
  3.4 0.0 copy-start.2
  3.4 0.0 copy-start.3
  3.4 0.6 %pack.1 = (f32[2,16,1024]{2,1,0:T(8,128)S(1)}, f32[2,16,1024]{2,1,0:T(8,128)S(1)}, f32[2,8,1024]{2,1,0:T(8,128)S(1)}) custom-call(f32[16,8,1024]{2,1,0:T(8,128)S(1)} %copy-done, s32[16,8,1024]{2,1,0:T(8,128)S(1)} %copy-done.1, f32[5,12]{1,0:T(8,128)S(1)} %copy-done.4), custom_call_target="tpu_custom_call" | custom-call | tf_op jit(solution)/shard_map/pack/pallas_call | solution.py:366
  4.0 0.7 %collective-permute-start = (f32[2,16,1024]{2,1,0:T(8,128)S(1)}, f32[2,16,1024]{2,1,0:T(8,128)S(1)}, u32[]{:S(2)}, u32[]{:S(2)}) collective-permute-start(f32[2,16,1024]{2,1,0:T(8,128)S(1)} %get-tuple-element.9), channel_id=1, source_target_pairs={{0,2},{2,0},{4,6},{6,4},{8,10},{10,8},{12,14},{14,12},{16,18},{18,... | collective-permute-start | bytes 393224 | tf_op jit(solution)/shard_map/ppermute | solution.py:375
  4.7 3.0 %collective-permute-start.1 = (f32[2,16,1024]{2,1,0:T(8,128)S(1)}, f32[2,16,1024]{2,1,0:T(8,128)S(1)}, u32[]{:S(2)}, u32[]{:S(2)}) collective-permute-start(f32[2,16,1024]{2,1,0:T(8,128)S(1)} %get-tuple-element.10), channel_id=1, source_target_pairs={{2,4},{4,2},{6,8},{8,6},{10,12},{12,10},{14,16},{16,14},{18,20},{2... | collective-permute-start | bytes 393224 | tf_op jit(solution)/shard_map/ppermute | solution.py:376
  7.8 0.3 collective-permute-start.2
  8.1 3.2 %collective-permute-done.2.rest_0_ = f32[2,8,1024]{2,1,0:T(8,128)S(1)} collective-permute-done((f32[2,8,1024]{2,1,0:T(8,128)S(1)}, f32[2,8,1024]{2,1,0:T(8,128)S(1)}, u32[]{:S(2)}, u32[]{:S(2)}) %collective-permute-start.2) | collective-permute-done | bytes 65568 | tf_op jit(solution)/shard_map/ppermute | solution.py:378
  11.2 0.0 collective-permute-done.from_even_ref
  11.2 1.1 %collective-permute-done.1.from_odd_ref = f32[2,16,1024]{2,1,0:T(8,128)S(1)} collective-permute-done((f32[2,16,1024]{2,1,0:T(8,128)S(1)}, f32[2,16,1024]{2,1,0:T(8,128)S(1)}, u32[]{:S(2)}, u32[]{:S(2)}) %collective-permute-start.1) | collective-permute-done | bytes 131104 | tf_op jit(solution)/shard_map/ppermute | solution.py:376
  12.4 0.0 copy-done.2
  12.4 0.0 copy-done.3
  12.4 9.3 %fine.1 = (f32[16,8,1024]{2,1,0:T(8,128)S(1)}, f32[5,8,1024]{2,1,0:T(8,128)S(1)}, f32[40,1024]{1,0:T(8,128)S(1)}, f32[40,1024]{1,0:T(8,128)S(1)}) custom-call(f32[16,8,1024]{2,1,0:T(8,128)S(1)} %copy-done, f32[16,8,1024]{2,1,0:T(8,128)S(1)} %copy-done.2, f32[16,8,1024]{2,1,0:T(8,128)S(1)} %copy-done.3, s32[16,8,1024]{2,1,0:T(8,128)S(1)} %copy-done.1, ...), custom_call_target="tpu_custom_call" | custom-call | tf_op jit(solution)/shard_map/fine/pallas_call | solution.py:381
  21.7 0.2 collective-permute-start.4
  21.9 2.1 %collective-permute-start.5 = (f32[40,1024]{1,0:T(8,128)S(1)}, f32[40,1024]{1,0:T(8,128)S(1)}, u32[]{:S(2)}, u32[]{:S(2)}) collective-permute-start(f32[40,1024]{1,0:T(8,128)S(1)} %get-tuple-element.15.to_odd_ref), channel_id=1, source_target_pairs={{2,4},{4,2},{6,8},{8,6},{10,12},{12,10},{14,16},{16,14},{18,20},{2... | collective-permute-start | bytes 491528 | tf_op jit(solution)/shard_map/ppermute | solution.py:400
  24.1 0.3 collective-permute-start.3
  24.4 0.0 collective-permute-done.4.from_even_ref
  24.4 6.0 %collective-permute-done.5.from_odd_ref = f32[40,1024]{1,0:T(8,128)S(1)} collective-permute-done((f32[40,1024]{1,0:T(8,128)S(1)}, f32[40,1024]{1,0:T(8,128)S(1)}, u32[]{:S(2)}, u32[]{:S(2)}) %collective-permute-start.5) | collective-permute-done | bytes 163872 | tf_op jit(solution)/shard_map/ppermute | solution.py:400
  30.3 0.1 edge.1.halo_ref
  30.4 0.3 collective-permute-start.6
  30.7 0.0 collective-permute-done.3.their_sums_ref
  30.7 3.8 %collective-permute-done.6.their_halo_ref = f32[2,8,1024]{2,1,0:T(8,128)S(1)} collective-permute-done((f32[2,8,1024]{2,1,0:T(8,128)S(1)}, f32[2,8,1024]{2,1,0:T(8,128)S(1)}, u32[]{:S(2)}, u32[]{:S(2)}) %collective-permute-start.6) | collective-permute-done | bytes 65568 | tf_op jit(solution)/shard_map/ppermute | solution.py:414
  34.5 1.1 %coarse.1 = (f32[16,8,1024]{2,1,0:T(8,128)}, f32[8,1024]{1,0:T(8,128)}) custom-call(f32[16,8,1024]{2,1,0:T(8,128)S(1)} %get-tuple-element.12.smooth_ref, f32[5,8,1024]{2,1,0:T(8,128)S(1)} %get-tuple-element.13.sums_ref, f32[5,8,1024]{2,1,0:T(8,128)S(1)} %collective-permute-done.3.their_sums_ref, f32[2,8,1024]{2,1,0:T(8,128)S(1)} %edge.1.halo_ref, ...), custom_call_target="tpu_custom_call" | custom-call | tf_op jit(solution)/shard_map/coarse/pallas_call | solution.py:417
Async XLA Ops:
  0.6 1.0 %copy-start = (f32[16,8,1024]{2,1,0:T(8,128)S(1)}, f32[16,8,1024]{2,1,0:T(8,128)}, u32[]{:S(2)}) copy-start(f32[16,8,1024]{2,1,0:T(8,128)} %p_ref.3) | copy-start | bytes 1572868
  1.7 1.0 %copy-start.1 = (s32[16,8,1024]{2,1,0:T(8,128)S(1)}, s32[16,8,1024]{2,1,0:T(8,128)}, u32[]{:S(2)}) copy-start(s32[16,8,1024]{2,1,0:T(8,128)} %soil_ref.3) | copy-start | bytes 1572868
  2.7 0.7 %copy-start.4 = (f32[5,12]{1,0:T(8,128)S(1)}, f32[5,12]{1,0:T(8,128)}, u32[]{:S(2)}) copy-start(f32[5,12]{1,0:T(8,128)} %params_ref.3) | copy-start | bytes 724
  3.4 9.0 %copy-start.2 = (f32[16,8,1024]{2,1,0:T(8,128)S(1)}, f32[16,8,1024]{2,1,0:T(8,128)}, u32[]{:S(2)}) copy-start(f32[16,8,1024]{2,1,0:T(8,128)} %theta_ref.1) | copy-start | bytes 1572868
  3.4 9.0 %copy-start.3 = (f32[16,8,1024]{2,1,0:T(8,128)S(1)}, f32[16,8,1024]{2,1,0:T(8,128)}, u32[]{:S(2)}) copy-start(f32[16,8,1024]{2,1,0:T(8,128)} %source_ref.1) | copy-start | bytes 1572868
  4.0 7.3 %collective-permute-start = (f32[2,16,1024]{2,1,0:T(8,128)S(1)}, f32[2,16,1024]{2,1,0:T(8,128)S(1)}, u32[]{:S(2)}, u32[]{:S(2)}) collective-permute-start(f32[2,16,1024]{2,1,0:T(8,128)S(1)} %get-tuple-element.9), channel_id=1, source_target_pairs={{0,2},{2,0},{4,6},{6,4},{8,10},{10,8},{12,14},{14,12},{16,18},{18,... | collective-permute-start | bytes 393224 | tf_op jit(solution)/shard_map/ppermute | solution.py:375
  4.7 7.7 %collective-permute-start.1 = (f32[2,16,1024]{2,1,0:T(8,128)S(1)}, f32[2,16,1024]{2,1,0:T(8,128)S(1)}, u32[]{:S(2)}, u32[]{:S(2)}) collective-permute-start(f32[2,16,1024]{2,1,0:T(8,128)S(1)} %get-tuple-element.10), channel_id=1, source_target_pairs={{2,4},{4,2},{6,8},{8,6},{10,12},{12,10},{14,16},{16,14},{18,20},{2... | collective-permute-start | bytes 393224 | tf_op jit(solution)/shard_map/ppermute | solution.py:376
  7.8 3.5 %collective-permute-start.2 = (f32[2,8,1024]{2,1,0:T(8,128)S(1)}, f32[2,8,1024]{2,1,0:T(8,128)S(1)}, u32[]{:S(2)}, u32[]{:S(2)}) collective-permute-start(f32[2,8,1024]{2,1,0:T(8,128)S(1)} %get-tuple-element.11), channel_id=1, source_target_pairs={{0,1},{1,0},{2,3},{3,2},{4,5},{5,4},{6,7},{7,6},{8,9},{9,8},{10,11... | collective-permute-start | bytes 196616 | tf_op jit(solution)/shard_map/ppermute | solution.py:378
  21.7 2.6 %collective-permute-start.4 = (f32[40,1024]{1,0:T(8,128)S(1)}, f32[40,1024]{1,0:T(8,128)S(1)}, u32[]{:S(2)}, u32[]{:S(2)}) collective-permute-start(f32[40,1024]{1,0:T(8,128)S(1)} %get-tuple-element.14.to_even_ref), channel_id=1, source_target_pairs={{0,2},{2,0},{4,6},{6,4},{8,10},{10,8},{12,14},{14,12},{16,18},{18,... | collective-permute-start | bytes 491528 | tf_op jit(solution)/shard_map/ppermute | solution.py:399
  21.9 8.4 %collective-permute-start.5 = (f32[40,1024]{1,0:T(8,128)S(1)}, f32[40,1024]{1,0:T(8,128)S(1)}, u32[]{:S(2)}, u32[]{:S(2)}) collective-permute-start(f32[40,1024]{1,0:T(8,128)S(1)} %get-tuple-element.15.to_odd_ref), channel_id=1, source_target_pairs={{2,4},{4,2},{6,8},{8,6},{10,12},{12,10},{14,16},{16,14},{18,20},{2... | collective-permute-start | bytes 491528 | tf_op jit(solution)/shard_map/ppermute | solution.py:400
  24.1 6.7 %collective-permute-start.3 = (f32[5,8,1024]{2,1,0:T(8,128)S(1)}, f32[5,8,1024]{2,1,0:T(8,128)S(1)}, u32[]{:S(2)}, u32[]{:S(2)}) collective-permute-start(f32[5,8,1024]{2,1,0:T(8,128)S(1)} %get-tuple-element.13.sums_ref), channel_id=1, source_target_pairs={{0,1},{1,0},{2,3},{3,2},{4,5},{5,4},{6,7},{7,6},{8,9},{9,8},{10,11... | collective-permute-start | bytes 491528 | tf_op jit(solution)/shard_map/ppermute | solution.py:402
  30.4 4.1 %collective-permute-start.6 = (f32[2,8,1024]{2,1,0:T(8,128)S(1)}, f32[2,8,1024]{2,1,0:T(8,128)S(1)}, u32[]{:S(2)}, u32[]{:S(2)}) collective-permute-start(f32[2,8,1024]{2,1,0:T(8,128)S(1)} %edge.1.halo_ref), channel_id=1, source_target_pairs={{0,1},{1,0},{2,3},{3,2},{4,5},{5,4},{6,7},{7,6},{8,9},{9,8},{10,11... | collective-permute-start | bytes 196616 | tf_op jit(solution)/shard_map/ppermute | solution.py:414

commit v3 on v2

--- a/solution.py
+++ b/solution.py
@@ -15,37 +15,26 @@
 LANES = 128
 F32 = jnp.float32
 
-T_A, T_N, T_C, T_SK, T_D, T_R, T_CAP, T_RATE = range(8)
+T_A, T_N, T_SK, T_D, T_R = range(5)
 
 
 def whole(count):
     return [pl.BlockSpec(memory_space=pltpu.VMEM)] * count
 
 
-def build_table(params_ref, tab_ref):
-    kinds = params_ref.shape[1]
-    theta_r = params_ref[0:1, :]
-    theta_s = params_ref[1:2, :]
+def build_table(params_ref):
     alpha = params_ref[2:3, :]
-    shape_n = params_ref[3:4, :]
-    k_sat = params_ref[4:5, :]
-    shape_m = 1.0 - 1.0 / shape_n
-    spread = theta_s - theta_r
-    rows = {
-        T_A: shape_n * (jnp.log(alpha) * LOG2E),
-        T_N: shape_n * (0.5 * LOG2E),
-        T_C: shape_m * (-0.25 * LOG2E),
-        T_SK: jnp.sqrt(k_sat),
-        T_D: spread * INV_DT,
-        T_R: theta_r * INV_DT,
-        T_CAP: spread * shape_m * shape_n * INV_DT,
-        T_RATE: alpha,
+    return {
+        T_A: jnp.log(alpha) * LOG2E,
+        T_N: params_ref[3:4, :],
+        T_SK: jnp.sqrt(params_ref[4:5, :]),
+        T_D: (params_ref[1:2, :] - params_ref[0:1, :]) * INV_DT,
+        T_R: params_ref[0:1, :] * INV_DT,
     }
-    for row_id, value in rows.items():
-        tab_ref[row_id, :, 0:kinds] = jnp.broadcast_to(value, (8, kinds))
-
-
-def lookup(table, kinds):
+
+
+def gather(row, kinds):
+    table = jnp.broadcast_to(jnp.pad(row, ((0, 0), (0, LANES - row.shape[1]))), (8, LANES))
     rows = []
     for r in range(0, kinds.shape[0], 8):
         cols = []
@@ -59,9 +48,33 @@
     return rows[0] if len(rows) == 1 else jnp.concatenate(rows, axis=0)
 
 
-def hydraulics(h, pa, pn, pc, psk):
+def spread_table(table, tab_ref):
+    for row_id, row in table.items():
+        for kind in range(row.shape[1]):
+            tab_ref[row_id, kind] = jnp.broadcast_to(row[:, kind : kind + 1], (8, LANES))
+
+
+def pick(tab_ref, row_id, bits, width):
+    level = [
+        jnp.concatenate([tab_ref[row_id, kind]] * (width // LANES), axis=1)
+        for kind in range(tab_ref.shape[1])
+    ]
+    for bit in bits:
+        pairs = [
+            jnp.where(bit, level[i + 1], level[i]) for i in range(0, len(level) - 1, 2)
+        ]
+        level = pairs + ([level[-1]] if len(level) % 2 else [])
+    return level[0]
+
+
+def type_bits(kinds, count):
+    return [(kinds & (1 << i)) != 0 for i in range((count - 1).bit_length())]
+
+
+def hydraulics(h, pa, pn, psk):
+    pc = (1.0 / pn - 1.0) * (0.25 * LOG2E)
     q = h * h + SMALL
-    u = jnp.exp2(pa + pn * jnp.log(q))
+    u = jnp.exp2(pn * (pa + (0.5 * LOG2E) * jnp.log(q)))
     one_plus = 1.0 + u
     inv = 1.0 / one_plus
     ratio = u * inv
@@ -72,13 +85,9 @@
     return kappa, half * half, ratio * lax.rsqrt(q)
 
 
-def kappa_only(h, kinds, tab_ref):
+def kappa_by_gather(h, kinds, table):
     return hydraulics(
-        h,
-        lookup(tab_ref[T_A], kinds),
-        lookup(tab_ref[T_N], kinds),
-        lookup(tab_ref[T_C], kinds),
-        lookup(tab_ref[T_SK], kinds),
+        h, gather(table[T_A], kinds), gather(table[T_N], kinds), gather(table[T_SK], kinds)
     )[0]
 
 
@@ -88,24 +97,41 @@
 
 def pack_kernel(swap, p_ref, soil_ref, params_ref, even_ref, odd_ref, *rest):
     layers, rows, _ = p_ref.shape
-    tab_ref = rest[-1]
-    build_table(params_ref, tab_ref)
+    count = 1 if swap else 2
+    vert_refs = rest[:count]
+    p_buf, soil_buf, vert_p, vert_soil, params_buf, sems = rest[count:]
     even = even_area()
-    low_h, high_h = p_ref[:, 0, :], p_ref[:, rows - 1, :]
-    low_k = kappa_only(low_h, soil_ref[:, 0, :], tab_ref)
-    high_k = kappa_only(high_h, soil_ref[:, rows - 1, :], tab_ref)
+    if swap:
+        spots = [jnp.where(lax.axis_index("depth") == 0, layers - 1, 0)]
+    else:
+        spots = [layers - 1, 0]
+    copies = [(params_ref, params_buf)]
+    for side, row in enumerate((0, rows - 1)):
+        copies.append((p_ref.at[:, row, :], p_buf.at[side]))
+        copies.append((soil_ref.at[:, row, :], soil_buf.at[side]))
+    for side, spot in enumerate(spots):
+        copies.append((p_ref.at[spot], vert_p.at[side]))
+        copies.append((soil_ref.at[spot], vert_soil.at[side]))
+    copies = [
+        pltpu.make_async_copy(source, target, sems.at[i])
+        for i, (source, target) in enumerate(copies)
+    ]
+    for copy in copies:
+        copy.start()
+    for copy in copies:
+        copy.wait()
+    table = build_table(params_buf)
+    low_h, high_h = p_buf[0], p_buf[1]
+    low_k = kappa_by_gather(low_h, soil_buf[0], table)
+    high_k = kappa_by_gather(high_h, soil_buf[1], table)
     even_ref[0] = jnp.where(even, high_h, low_h)
     even_ref[1] = jnp.where(even, high_k, low_k)
     odd_ref[0] = jnp.where(even, low_h, high_h)
     odd_ref[1] = jnp.where(even, low_k, high_k)
-    if swap:
-        spots = [jnp.where(lax.axis_index("depth") == 0, layers - 1, 0)]
-    else:
-        spots = [layers - 1, 0]
-    for out_ref, spot in zip(rest[:-1], spots):
-        h = p_ref[spot]
+    for side, out_ref in enumerate(vert_refs):
+        h = vert_p[side]
         out_ref[0] = h
-        out_ref[1] = kappa_only(h, soil_ref[spot], tab_ref)
+        out_ref[1] = kappa_by_gather(h, vert_soil[side], table)
 
 
 def row_iota(shape):
@@ -134,63 +160,110 @@
     return jnp.where(lane_iota(x.shape) == last, 0.0, pltpu.roll(x, last, 1))
 
 
-def main_kernel(
-    swap,
+def local_kernel(
+    p_hbm,
+    theta_hbm,
+    source_hbm,
+    soil_hbm,
+    params_hbm,
+    kept_ref,
+    kap_ref,
     p_ref,
+    sums_ref,
     theta_ref,
     source_ref,
     soil_ref,
     params_ref,
-    from_even_ref,
-    from_odd_ref,
-    *rest,
+    tab_ref,
+    sems,
+    params_sem,
 ):
+    layers, rows, width = p_hbm.shape
+    chunks = sems.shape[1]
+    part = layers // chunks
+    pairs = (
+        (soil_hbm, soil_ref),
+        (p_hbm, p_ref),
+        (theta_hbm, theta_ref),
+        (source_hbm, source_ref),
+    )
+
+    def copy(i, chunk):
+        at = pl.ds(chunk * part, part)
+        return pltpu.make_async_copy(pairs[i][0].at[at], pairs[i][1].at[at], sems.at[i, chunk])
+
+    params_copy = pltpu.make_async_copy(params_hbm, params_ref, params_sem)
+    params_copy.start()
+    for chunk in range(chunks):
+        for i in range(4):
+            copy(i, chunk).start()
+    params_copy.wait()
+    kind_count = params_ref.shape[1]
+    spread_table(build_table(params_ref), tab_ref)
+
+    def step(layer, carry):
+        sum_fixed, sum_rate = carry
+        bits = type_bits(soil_ref[layer], kind_count)
+        pa, pn, psk, pd, pr = [pick(tab_ref, i, bits, width) for i in range(5)]
+        h = p_ref[layer]
+        kap, sat, over = hydraulics(h, pa, pn, psk)
+        fixed = pr - INV_DT * theta_ref[layer] - source_ref[layer]
+        k_l, k_r = from_left(kap), from_right(kap)
+        k_u, k_d = from_above(kap, 0.0), from_below(kap, 0.0)
+        inflow = (
+            k_l * (pltpu.roll(h, 1, 1) - h)
+            + k_r * (pltpu.roll(h, width - 1, 1) - h)
+            + k_u * (pltpu.roll(h, 1, 0) - h)
+            + k_d * (pltpu.roll(h, rows - 1, 0) - h)
+        )
+        kap_ref[layer] = kap
+        kept_ref[0, layer] = pd * sat + fixed - kap * inflow
+        kept_ref[1, layer] = pd * (pn - 1.0) * sat * over + kap * ((k_l + k_r) + (k_u + k_d))
+        kept_ref[2, layer] = pa
+        kept_ref[3, layer] = pn
+        kept_ref[4, layer] = psk
+        kept_ref[5, layer] = pd
+        return sum_fixed + fixed, sum_rate + jnp.exp2(pa)
+
+    def part_step(chunk, carry):
+        for i in range(4):
+            copy(i, chunk).wait()
+        return lax.fori_loop(chunk * part, (chunk + 1) * part, step, carry)
+
+    zero = jnp.zeros((rows, width), F32)
+    sum_fixed, sum_rate = lax.fori_loop(0, chunks, part_step, (zero, zero))
+    sums_ref[0] = sum_fixed
+    sums_ref[1] = sum_rate
+
+
+def fine_kernel(swap, p_ref, kept_ref, kap_ref, local_ref, from_even_ref, from_odd_ref, *rest):
     layers, rows, width = p_ref.shape
     if swap:
         vert_ref, rest = rest[0], rest[1:]
     else:
         top_ref, bottom_ref, rest = rest[0], rest[1], rest[2:]
-    smooth_ref, sums_ref, to_even_ref, to_odd_ref, tab_ref, kap_ref, head_ref = rest
-    build_table(params_ref, tab_ref)
+    smooth_ref, sums_ref, to_even_ref, to_odd_ref = rest
     even = even_area()
+    spot = row_iota((rows, width))
+    is_first, is_last = spot == 0, spot == rows - 1
 
     if swap:
-        d = lax.axis_index("depth")
-        vert_k = vert_ref[1]
-        kap_ref[0] = jnp.where(d == 0, 0.0, vert_k)
-        kap_ref[layers + 1] = jnp.where(d == 0, vert_k, 0.0)
-        head_ref[0] = vert_ref[0]
-        head_ref[layers + 1] = vert_ref[0]
+        at_top = lax.axis_index("depth") == 0
+        top_k = jnp.where(at_top, 0.0, vert_ref[1])
+        bottom_k = jnp.where(at_top, vert_ref[1], 0.0)
+        top_h = bottom_h = vert_ref[0]
     else:
-        kap_ref[0] = top_ref[1]
-        kap_ref[layers + 1] = bottom_ref[1]
-        head_ref[0] = top_ref[0]
-        head_ref[layers + 1] = bottom_ref[0]
-
-    def first(layer, carry):
+        top_h, top_k = top_ref[0], top_ref[1]
+        bottom_h, bottom_k = bottom_ref[0], bottom_ref[1]
+
+    def step(layer, carry):
+        sum_kh, sum_k, sum_cap, sum_sat, flux_x, flux_y = carry
         h = p_ref[layer]
-        kap_ref[layer + 1] = kappa_only(h, soil_ref[layer], tab_ref)
-        head_ref[layer + 1] = h
-        return carry
-
-    lax.fori_loop(0, layers, first, 0)
-
-    def step(layer, carry):
-        sum_kh, sum_k, sum_cap, sum_rest, sum_rate, flux_x, flux_y = carry
-        kinds = soil_ref[layer]
-        pa = lookup(tab_ref[T_A], kinds)
-        pn = lookup(tab_ref[T_N], kinds)
-        pc = lookup(tab_ref[T_C], kinds)
-        psk = lookup(tab_ref[T_SK], kinds)
-        pd = lookup(tab_ref[T_D], kinds)
-        pr = lookup(tab_ref[T_R], kinds)
-        pcap = lookup(tab_ref[T_CAP], kinds)
-        rate = lookup(tab_ref[T_RATE], kinds)
-        h = p_ref[layer]
-        kap, sat, over = hydraulics(h, pa, pn, pc, psk)
-        fixed = pr - INV_DT * theta_ref[layer] - source_ref[layer]
-        k_up = kap_ref[layer]
-        k_dn = kap_ref[layer + 2]
+        above, below = jnp.maximum(layer - 1, 0), jnp.minimum(layer + 1, layers - 1)
+        k_u = jnp.where(layer == 0, top_k, kap_ref[above])
+        h_u = jnp.where(layer == 0, top_h, p_ref[above])
+        k_d = jnp.where(layer == layers - 1, bottom_k, kap_ref[below])
+        h_d = jnp.where(layer == layers - 1, bottom_h, p_ref[below])
         even_k = from_even_ref[1, pl.ds(layer, 1), :]
         odd_k = from_odd_ref[1, pl.ds(layer, 1), :]
         even_h = from_even_ref[0, pl.ds(layer, 1), :]
@@ -199,30 +272,18 @@
         hi_k = jnp.where(even, even_k, odd_k)
         lo_h = jnp.where(even, odd_h, even_h)
         hi_h = jnp.where(even, even_h, odd_h)
-        g = kap * h
-        sum_n = (
-            k_up
-            + k_dn
-            + from_above(kap, lo_k)
-            + from_below(kap, hi_k)
-            + from_left(kap)
-            + from_right(kap)
-        )
-        sum_g = (
-            k_up * head_ref[layer]
-            + k_dn * head_ref[layer + 2]
-            + from_above(g, lo_k * lo_h)
-            + from_below(g, hi_k * hi_h)
-            + from_left(g)
-            + from_right(g)
-        )
-        inflow = kap * (sum_g - h * sum_n + (k_up - k_dn))
-        balance = pd * sat + fixed - inflow
-        diagonal = pcap * sat * over + kap * sum_n
+        side_k = jnp.where(is_first, lo_k, jnp.where(is_last, hi_k, 0.0))
+        side_h = jnp.where(is_first, lo_h, hi_h)
+        kap = kap_ref[layer]
+        inflow = k_u * (h_u - h + 1.0) + k_d * (h_d - h - 1.0) + side_k * (side_h - h)
+        balance = kept_ref[0, layer] - kap * inflow
+        diagonal = kept_ref[1, layer] + kap * (k_u + k_d + side_k)
         h = h - RELAX * balance / diagonal
         smooth_ref[layer] = h
 
-        kap, sat, over = hydraulics(h, pa, pn, pc, psk)
+        pn = kept_ref[3, layer]
+        pd = kept_ref[5, layer]
+        kap, sat, over = hydraulics(h, kept_ref[2, layer], pn, kept_ref[4, layer])
         cond = kap * kap
         flux_x = flux_x + kap * from_below(kap, 0.0) * (pltpu.roll(h, rows - 1, 0) - h)
         flux_y = flux_y + kap * from_right(kap) * (pltpu.roll(h, width - 1, 1) - h)
@@ -233,20 +294,20 @@
         return (
             sum_kh + cond * h,
             sum_k + cond,
-            sum_cap + pcap * sat * over,
-            sum_rest + (pd * sat + fixed),
-            sum_rate + rate,
+            sum_cap + pd * (pn - 1.0) * sat * over,
+            sum_sat + pd * sat,
             flux_x,
             flux_y,
         )
 
     zero = jnp.zeros((rows, width), F32)
-    sum_kh, sum_k, sum_cap, sum_rest, sum_rate, flux_x, flux_y = lax.fori_loop(
-        0, layers, step, (zero,) * 7
+    sum_kh, sum_k, sum_cap, sum_sat, flux_x, flux_y = lax.fori_loop(0, layers, step, (zero,) * 6)
+    sum_rate = local_ref[1]
+    restricted = (
+        (flux_x - from_above(flux_x, 0.0)) + (flux_y - from_left(flux_y)) - sum_sat - local_ref[0]
     )
-    restricted = (flux_x - from_above(flux_x, 0.0)) + (flux_y - from_left(flux_y)) - sum_rest
-    for spot, value in enumerate((sum_kh, sum_k, sum_cap, restricted, sum_rate)):
-        sums_ref[spot] = value
+    for at, value in enumerate((sum_kh, sum_k, sum_cap, restricted, sum_rate)):
+        sums_ref[at] = value
     at = 2 * layers
     tails = []
     for edge, inner in ((rows - 1, rows - 2), (0, 1)):
@@ -361,41 +422,66 @@
         return jax.ShapeDtypeStruct(dims, F32)
 
     params = pltpu.CompilerParams(vmem_limit_bytes=48 << 20)
-    tab = pltpu.VMEM((8, 8, LANES), F32)
     verts = 1 if swap else 2
+    kind_count = soil_params.shape[1]
+    in_hbm = [
+        pltpu.with_memory_space_constraint(x, pltpu.HBM)
+        for x in (pressure, theta_old, source, soil_type, soil_params)
+    ]
     packed = pl.pallas_call(
         functools.partial(pack_kernel, swap),
         out_shape=[shape(2, layers, width)] * 2 + [shape(2, rows, width)] * verts,
-        in_specs=whole(3),
+        in_specs=[pl.BlockSpec(memory_space=pltpu.HBM)] * 3,
         out_specs=whole(2 + verts),
-        scratch_shapes=[tab],
+        scratch_shapes=[
+            pltpu.VMEM((2, layers, width), F32),
+            pltpu.VMEM((2, layers, width), jnp.int32),
+            pltpu.VMEM((verts, rows, width), F32),
+            pltpu.VMEM((verts, rows, width), jnp.int32),
+            pltpu.VMEM(soil_params.shape, F32),
+            pltpu.SemaphoreType.DMA((5 + 2 * verts,)),
+        ],
         compiler_params=params,
         name="pack",
-    )(pressure, soil_type, soil_params)
+    )(in_hbm[0], in_hbm[3], in_hbm[4])
     from_even = lax.ppermute(packed[0], "area", even_pairs)
     from_odd = lax.ppermute(packed[1], "area", odd_pairs)
     if swap:
         vert = [lax.ppermute(packed[2], "depth", swapped)]
     else:
         vert = [lax.ppermute(packed[2], "depth", down), lax.ppermute(packed[3], "depth", up)]
+    chunks = math.gcd(layers, 4)
+    block = (layers, rows, width)
+    kept, kap, head, local_sums = pl.pallas_call(
+        local_kernel,
+        out_shape=[shape(6, *block), shape(*block), shape(*block), shape(2, rows, width)],
+        in_specs=[pl.BlockSpec(memory_space=pltpu.HBM)] * 5,
+        out_specs=whole(4),
+        scratch_shapes=[
+            pltpu.VMEM(block, F32),
+            pltpu.VMEM(block, F32),
+            pltpu.VMEM(block, jnp.int32),
+            pltpu.VMEM(soil_params.shape, F32),
+            pltpu.VMEM((5, kind_count, 8, LANES), F32),
+            pltpu.SemaphoreType.DMA((4, chunks)),
+            pltpu.SemaphoreType.DMA(()),
+        ],
+        compiler_params=params,
+        name="local",
+    )(in_hbm[0], in_hbm[1], in_hbm[2], in_hbm[3], in_hbm[4])
     smooth, sums, to_even, to_odd = pl.pallas_call(
-        functools.partial(main_kernel, swap),
+        functools.partial(fine_kernel, swap),
         out_shape=[
             shape(layers, rows, width),
             shape(5, rows, width),
             shape(2 * layers + 8, width),
             shape(2 * layers + 8, width),
         ],
-        in_specs=whole(7 + verts),
+        in_specs=whole(6 + verts),
         out_specs=whole(4),
-        scratch_shapes=[
-            tab,
-            pltpu.VMEM((layers + 2, rows, width), F32),
-            pltpu.VMEM((layers + 2, rows, width), F32),
-        ],
         compiler_params=params,
         name="fine",
-    )(pressure, theta_old, source, soil_type, soil_params, from_even, from_odd, *vert)
+    )(head, kept, kap, local_sums, from_even, from_odd, *vert)
     from_even = lax.ppermute(to_even, "area", even_pairs)
     from_odd = lax.ppermute(to_odd, "area", odd_pairs)
     if swap:

time: 35.8 us -> 29.4 us (0.82)
  the two profiles are of different devices: /device:TPU:27 before, /device:TPU:9 now
where the time goes in v3:
time: 29.4 us; the launch traced here: 29.2 us
  Pallas kernels  10.7 us (36%)
  starting transfers between devices  9.3 us (32%)
  waiting for transfers between devices  8.48 us (29%)
  between operations  0.7 us (2%)
    ppermute x1, waiting for transfers between devices, shards(): from_odd = lax.ppermute(to_odd, 'area', odd_pairs)  5.46 us
    pallas_call x1, Pallas kernels, shards(): pl.pallas_call(local_kernel, out_shape=[shape(6, *block), shape(*block),...  4.79 us
    pallas_call x1, Pallas kernels, shards(): pl.pallas_call(functools.partial(fine_kernel, swap), out_shape=[shape(lay...  3.38 us
    ppermute x1, starting transfers between devices, shards(): from_odd = lax.ppermute(packed[1], 'area', odd_pairs)  3.05 us
    ppermute x1, waiting for transfers between devices, shards(): their_halo = lax.ppermute(halo, 'depth', swapped)  3 us
    ppermute x1, starting transfers between devices, shards(): from_odd = lax.ppermute(to_odd, 'area', odd_pairs)  2.88 us
    pallas_call x1, Pallas kernels, shards(): pl.pallas_call(functools.partial(pack_kernel, swap), out_shape=[shape(2,...  1.47 us
    ppermute x1, starting transfers between devices, shards(): vert = [lax.ppermute(packed[2], 'depth', swapped)]  1.28 us
  transfers between devices with their start and end apart: 7, of which 2 were waited for; matrix products, arithmetic and copies ran while one was open for 0% of the time, Pallas kernels for 17%

profile of v3, /device:TPU:9, one launch (start us, length us, event | category | flops | bytes accessed | tf_op | source)
XLA Modules:
  0.0 29.2 jit_solution(4075599251662867027)
XLA Ops:
  0.6 1.5 %pack.1 = (f32[2,16,1024]{2,1,0:T(8,128)S(1)}, f32[2,16,1024]{2,1,0:T(8,128)S(1)}, f32[2,8,1024]{2,1,0:T(8,128)S(1)}) custom-call(f32[16,8,1024]{2,1,0:T(8,128)} %p_ref.1, s32[16,8,1024]{2,1,0:T(8,128)} %soil_ref.1, f32[5,12]{1,0:T(8,128)} %params_ref.1), custom_call_target="tpu_custom_call" | custom-call | tf_op jit(solution)/shard_map/pack/pallas_call | solution.py:431
  2.1 0.7 %collective-permute-start = (f32[2,16,1024]{2,1,0:T(8,128)S(1)}, f32[2,16,1024]{2,1,0:T(8,128)S(1)}, u32[]{:S(2)}, u32[]{:S(2)}) collective-permute-start(f32[2,16,1024]{2,1,0:T(8,128)S(1)} %get-tuple-element.17), channel_id=1, source_target_pairs={{0,2},{2,0},{4,6},{6,4},{8,10},{10,8},{12,14},{14,12},{16,18},{18,... | collective-permute-start | bytes 393224 | tf_op jit(solution)/shard_map/ppermute | solution.py:447
  2.8 3.0 %collective-permute-start.1 = (f32[2,16,1024]{2,1,0:T(8,128)S(1)}, f32[2,16,1024]{2,1,0:T(8,128)S(1)}, u32[]{:S(2)}, u32[]{:S(2)}) collective-permute-start(f32[2,16,1024]{2,1,0:T(8,128)S(1)} %get-tuple-element.18), channel_id=1, source_target_pairs={{2,4},{4,2},{6,8},{8,6},{10,12},{12,10},{14,16},{16,14},{18,20},{2... | collective-permute-start | bytes 393224 | tf_op jit(solution)/shard_map/ppermute | solution.py:448
  5.9 1.3 %collective-permute-start.2 = (f32[2,8,1024]{2,1,0:T(8,128)S(1)}, f32[2,8,1024]{2,1,0:T(8,128)S(1)}, u32[]{:S(2)}, u32[]{:S(2)}) collective-permute-start(f32[2,8,1024]{2,1,0:T(8,128)S(1)} %get-tuple-element.19), channel_id=1, source_target_pairs={{0,1},{1,0},{2,3},{3,2},{4,5},{5,4},{6,7},{7,6},{8,9},{9,8},{10,11... | collective-permute-start | bytes 196616 | tf_op jit(solution)/shard_map/ppermute | solution.py:450
  7.2 4.8 %local.1 = (f32[6,16,8,1024]{3,2,1,0:T(8,128)S(1)}, f32[16,8,1024]{2,1,0:T(8,128)S(1)}, f32[16,8,1024]{2,1,0:T(8,128)S(1)}, f32[2,8,1024]{2,1,0:T(8,128)S(1)}) custom-call(f32[16,8,1024]{2,1,0:T(8,128)} %p_ref.1, f32[16,8,1024]{2,1,0:T(8,128)} %theta_hbm.1, f32[16,8,1024]{2,1,0:T(8,128)} %source_hbm.1, s32[16,8,1024]{2,1,0:T(8,128)} %soil_ref.1, ...), custom_call_target="tpu_custom_call" | custom-call | tf_op jit(solution)/shard_map/local/pallas_call | solution.py:455
  12.0 0.0 collective-permute-done.2.rest_0_
  12.0 0.0 collective-permute-done.from_even_ref
  12.0 0.0 collective-permute-done.1.from_odd_ref
  12.0 3.4 %fine.1 = (f32[16,8,1024]{2,1,0:T(8,128)S(1)}, f32[5,8,1024]{2,1,0:T(8,128)S(1)}, f32[40,1024]{1,0:T(8,128)S(1)}, f32[40,1024]{1,0:T(8,128)S(1)}) custom-call(f32[16,8,1024]{2,1,0:T(8,128)S(1)} %get-tuple-element.13.p_ref, f32[6,16,8,1024]{3,2,1,0:T(8,128)S(1)} %get-tuple-element.14.kept_ref, f32[16,8,1024]{2,1,0:T(8,128)S(1)} %get-tuple-element.15.kap_ref, ...), custom_call_target="tpu_custom_call" | custom-call | tf_op jit(solution)/shard_map/fine/pallas_call | solution.py:472
  15.4 0.7 %collective-permute-start.4 = (f32[40,1024]{1,0:T(8,128)S(1)}, f32[40,1024]{1,0:T(8,128)S(1)}, u32[]{:S(2)}, u32[]{:S(2)}) collective-permute-start(f32[40,1024]{1,0:T(8,128)S(1)} %get-tuple-element.22.to_even_ref), channel_id=1, source_target_pairs={{0,2},{2,0},{4,6},{6,4},{8,10},{10,8},{12,14},{14,12},{16,18},{18,... | collective-permute-start | bytes 491528 | tf_op jit(solution)/shard_map/ppermute | solution.py:485
  16.1 2.9 %collective-permute-start.5 = (f32[40,1024]{1,0:T(8,128)S(1)}, f32[40,1024]{1,0:T(8,128)S(1)}, u32[]{:S(2)}, u32[]{:S(2)}) collective-permute-start(f32[40,1024]{1,0:T(8,128)S(1)} %get-tuple-element.23.to_odd_ref), channel_id=1, source_target_pairs={{2,4},{4,2},{6,8},{8,6},{10,12},{12,10},{14,16},{16,14},{18,20},{2... | collective-permute-start | bytes 491528 | tf_op jit(solution)/shard_map/ppermute | solution.py:486
  19.0 0.3 %collective-permute-start.3 = (f32[5,8,1024]{2,1,0:T(8,128)S(1)}, f32[5,8,1024]{2,1,0:T(8,128)S(1)}, u32[]{:S(2)}, u32[]{:S(2)}) collective-permute-start(f32[5,8,1024]{2,1,0:T(8,128)S(1)} %get-tuple-element.21.sums_ref), channel_id=1, source_target_pairs={{0,1},{1,0},{2,3},{3,2},{4,5},{5,4},{6,7},{7,6},{8,9},{9,8},{10,11... | collective-permute-start | bytes 491528 | tf_op jit(solution)/shard_map/ppermute | solution.py:488
  19.3 0.0 collective-permute-done.4.from_even_ref
  19.3 5.5 %collective-permute-done.5.from_odd_ref = f32[40,1024]{1,0:T(8,128)S(1)} collective-permute-done((f32[40,1024]{1,0:T(8,128)S(1)}, f32[40,1024]{1,0:T(8,128)S(1)}, u32[]{:S(2)}, u32[]{:S(2)}) %collective-permute-start.5) | collective-permute-done | bytes 163872 | tf_op jit(solution)/shard_map/ppermute | solution.py:486
  24.8 0.3 %collective-permute-start.6 = (f32[2,8,1024]{2,1,0:T(8,128)S(1)}, f32[2,8,1024]{2,1,0:T(8,128)S(1)}, u32[]{:S(2)}, u32[]{:S(2)}) collective-permute-start(f32[2,8,1024]{2,1,0:T(8,128)S(1)} %edge.1.halo_ref), channel_id=1, source_target_pairs={{0,1},{1,0},{2,3},{3,2},{4,5},{5,4},{6,7},{7,6},{8,9},{9,8},{10,11... | collective-permute-start | bytes 196616 | tf_op jit(solution)/shard_map/ppermute | solution.py:500
  25.2 0.0 collective-permute-done.3.their_sums_ref
  25.2 3.0 %collective-permute-done.6.their_halo_ref = f32[2,8,1024]{2,1,0:T(8,128)S(1)} collective-permute-done((f32[2,8,1024]{2,1,0:T(8,128)S(1)}, f32[2,8,1024]{2,1,0:T(8,128)S(1)}, u32[]{:S(2)}, u32[]{:S(2)}) %collective-permute-start.6) | collective-permute-done | bytes 65568 | tf_op jit(solution)/shard_map/ppermute | solution.py:500
  28.2 1.1 %coarse.1 = (f32[16,8,1024]{2,1,0:T(8,128)}, f32[8,1024]{1,0:T(8,128)}) custom-call(f32[16,8,1024]{2,1,0:T(8,128)S(1)} %get-tuple-element.20.smooth_ref, f32[5,8,1024]{2,1,0:T(8,128)S(1)} %get-tuple-element.21.sums_ref, f32[5,8,1024]{2,1,0:T(8,128)S(1)} %collective-permute-done.3.their_sums_ref, f32[2,8,1024]{2,1,0:T(8,128)S(1)} %edge.1.halo_ref, ...), custom_call_target="tpu_custom_call" | custom-call | tf_op jit(solution)/shard_map/coarse/pallas_call | solution.py:503
  (1 shorter events, 0.0 us)
Async XLA Ops:
  2.1 9.9 %collective-permute-start = (f32[2,16,1024]{2,1,0:T(8,128)S(1)}, f32[2,16,1024]{2,1,0:T(8,128)S(1)}, u32[]{:S(2)}, u32[]{:S(2)}) collective-permute-start(f32[2,16,1024]{2,1,0:T(8,128)S(1)} %get-tuple-element.17), channel_id=1, source_target_pairs={{0,2},{2,0},{4,6},{6,4},{8,10},{10,8},{12,14},{14,12},{16,18},{18,... | collective-permute-start | bytes 393224 | tf_op jit(solution)/shard_map/ppermute | solution.py:447
  2.8 9.2 %collective-permute-start.1 = (f32[2,16,1024]{2,1,0:T(8,128)S(1)}, f32[2,16,1024]{2,1,0:T(8,128)S(1)}, u32[]{:S(2)}, u32[]{:S(2)}) collective-permute-start(f32[2,16,1024]{2,1,0:T(8,128)S(1)} %get-tuple-element.18), channel_id=1, source_target_pairs={{2,4},{4,2},{6,8},{8,6},{10,12},{12,10},{14,16},{16,14},{18,20},{2... | collective-permute-start | bytes 393224 | tf_op jit(solution)/shard_map/ppermute | solution.py:448
  5.9 6.1 %collective-permute-start.2 = (f32[2,8,1024]{2,1,0:T(8,128)S(1)}, f32[2,8,1024]{2,1,0:T(8,128)S(1)}, u32[]{:S(2)}, u32[]{:S(2)}) collective-permute-start(f32[2,8,1024]{2,1,0:T(8,128)S(1)} %get-tuple-element.19), channel_id=1, source_target_pairs={{0,1},{1,0},{2,3},{3,2},{4,5},{5,4},{6,7},{7,6},{8,9},{9,8},{10,11... | collective-permute-start | bytes 196616 | tf_op jit(solution)/shard_map/ppermute | solution.py:450
  15.4 3.9 %collective-permute-start.4 = (f32[40,1024]{1,0:T(8,128)S(1)}, f32[40,1024]{1,0:T(8,128)S(1)}, u32[]{:S(2)}, u32[]{:S(2)}) collective-permute-start(f32[40,1024]{1,0:T(8,128)S(1)} %get-tuple-element.22.to_even_ref), channel_id=1, source_target_pairs={{0,2},{2,0},{4,6},{6,4},{8,10},{10,8},{12,14},{14,12},{16,18},{18,... | collective-permute-start | bytes 491528 | tf_op jit(solution)/shard_map/ppermute | solution.py:485
  16.1 8.7 %collective-permute-start.5 = (f32[40,1024]{1,0:T(8,128)S(1)}, f32[40,1024]{1,0:T(8,128)S(1)}, u32[]{:S(2)}, u32[]{:S(2)}) collective-permute-start(f32[40,1024]{1,0:T(8,128)S(1)} %get-tuple-element.23.to_odd_ref), channel_id=1, source_target_pairs={{2,4},{4,2},{6,8},{8,6},{10,12},{12,10},{14,16},{16,14},{18,20},{2... | collective-permute-start | bytes 491528 | tf_op jit(solution)/shard_map/ppermute | solution.py:486
  19.0 6.2 %collective-permute-start.3 = (f32[5,8,1024]{2,1,0:T(8,128)S(1)}, f32[5,8,1024]{2,1,0:T(8,128)S(1)}, u32[]{:S(2)}, u32[]{:S(2)}) collective-permute-start(f32[5,8,1024]{2,1,0:T(8,128)S(1)} %get-tuple-element.21.sums_ref), channel_id=1, source_target_pairs={{0,1},{1,0},{2,3},{3,2},{4,5},{5,4},{6,7},{7,6},{8,9},{9,8},{10,11... | collective-permute-start | bytes 491528 | tf_op jit(solution)/shard_map/ppermute | solution.py:488
  24.8 3.3 %collective-permute-start.6 = (f32[2,8,1024]{2,1,0:T(8,128)S(1)}, f32[2,8,1024]{2,1,0:T(8,128)S(1)}, u32[]{:S(2)}, u32[]{:S(2)}) collective-permute-start(f32[2,8,1024]{2,1,0:T(8,128)S(1)} %edge.1.halo_ref), channel_id=1, source_target_pairs={{0,1},{1,0},{2,3},{3,2},{4,5},{5,4},{6,7},{7,6},{8,9},{9,8},{10,11... | collective-permute-start | bytes 196616 | tf_op jit(solution)/shard_map/ppermute | solution.py:500

commit v4 on v3

--- a/solution.py
+++ b/solution.py
@@ -13,6 +13,7 @@
 SMALL = 0.04
 LOG2E = math.log2(math.e)
 LANES = 128
+PACK_COST = 4_000_000_000
 F32 = jnp.float32
 
 T_A, T_N, T_SK, T_D, T_R = range(5)
@@ -95,7 +96,7 @@
     return lax.rem(lax.axis_index("area"), 2) == 0
 
 
-def pack_kernel(swap, p_ref, soil_ref, params_ref, even_ref, odd_ref, *rest):
+def pack_kernel(swap, p_ref, soil_ref, params_ref, tab_ref, even_ref, odd_ref, *rest):
     layers, rows, _ = p_ref.shape
     count = 1 if swap else 2
     vert_refs = rest[:count]
@@ -118,9 +119,11 @@
     ]
     for copy in copies:
         copy.start()
-    for copy in copies:
+    copies[0].wait()
+    table = build_table(params_buf)
+    spread_table(table, tab_ref)
+    for copy in copies[1:]:
         copy.wait()
-    table = build_table(params_buf)
     low_h, high_h = p_buf[0], p_buf[1]
     low_k = kappa_by_gather(low_h, soil_buf[0], table)
     high_k = kappa_by_gather(high_h, soil_buf[1], table)
@@ -161,45 +164,10 @@
 
 
 def local_kernel(
-    p_hbm,
-    theta_hbm,
-    source_hbm,
-    soil_hbm,
-    params_hbm,
-    kept_ref,
-    kap_ref,
-    p_ref,
-    sums_ref,
-    theta_ref,
-    source_ref,
-    soil_ref,
-    params_ref,
-    tab_ref,
-    sems,
-    params_sem,
+    p_ref, theta_ref, source_ref, soil_ref, tab_ref, kept_ref, kap_ref, sums_ref
 ):
-    layers, rows, width = p_hbm.shape
-    chunks = sems.shape[1]
-    part = layers // chunks
-    pairs = (
-        (soil_hbm, soil_ref),
-        (p_hbm, p_ref),
-        (theta_hbm, theta_ref),
-        (source_hbm, source_ref),
-    )
-
-    def copy(i, chunk):
-        at = pl.ds(chunk * part, part)
-        return pltpu.make_async_copy(pairs[i][0].at[at], pairs[i][1].at[at], sems.at[i, chunk])
-
-    params_copy = pltpu.make_async_copy(params_hbm, params_ref, params_sem)
-    params_copy.start()
-    for chunk in range(chunks):
-        for i in range(4):
-            copy(i, chunk).start()
-    params_copy.wait()
-    kind_count = params_ref.shape[1]
-    spread_table(build_table(params_ref), tab_ref)
+    layers, rows, width = p_ref.shape
+    kind_count = tab_ref.shape[1]
 
     def step(layer, carry):
         sum_fixed, sum_rate = carry
@@ -225,13 +193,8 @@
         kept_ref[5, layer] = pd
         return sum_fixed + fixed, sum_rate + jnp.exp2(pa)
 
-    def part_step(chunk, carry):
-        for i in range(4):
-            copy(i, chunk).wait()
-        return lax.fori_loop(chunk * part, (chunk + 1) * part, step, carry)
-
     zero = jnp.zeros((rows, width), F32)
-    sum_fixed, sum_rate = lax.fori_loop(0, chunks, part_step, (zero, zero))
+    sum_fixed, sum_rate = lax.fori_loop(0, layers, step, (zero, zero), unroll=True)
     sums_ref[0] = sum_fixed
     sums_ref[1] = sum_rate
 
@@ -301,7 +264,9 @@
         )
 
     zero = jnp.zeros((rows, width), F32)
-    sum_kh, sum_k, sum_cap, sum_sat, flux_x, flux_y = lax.fori_loop(0, layers, step, (zero,) * 6)
+    sum_kh, sum_k, sum_cap, sum_sat, flux_x, flux_y = lax.fori_loop(
+        0, layers, step, (zero,) * 6, unroll=True
+    )
     sum_rate = local_ref[1]
     restricted = (
         (flux_x - from_above(flux_x, 0.0)) + (flux_y - from_left(flux_y)) - sum_sat - local_ref[0]
@@ -426,13 +391,15 @@
     kind_count = soil_params.shape[1]
     in_hbm = [
         pltpu.with_memory_space_constraint(x, pltpu.HBM)
-        for x in (pressure, theta_old, source, soil_type, soil_params)
+        for x in (pressure, soil_type, soil_params)
     ]
     packed = pl.pallas_call(
         functools.partial(pack_kernel, swap),
-        out_shape=[shape(2, layers, width)] * 2 + [shape(2, rows, width)] * verts,
+        out_shape=[shape(5, kind_count, 8, LANES)]
+        + [shape(2, layers, width)] * 2
+        + [shape(2, rows, width)] * verts,
         in_specs=[pl.BlockSpec(memory_space=pltpu.HBM)] * 3,
-        out_specs=whole(2 + verts),
+        out_specs=whole(3 + verts),
         scratch_shapes=[
             pltpu.VMEM((2, layers, width), F32),
             pltpu.VMEM((2, layers, width), jnp.int32),
@@ -442,33 +409,23 @@
             pltpu.SemaphoreType.DMA((5 + 2 * verts,)),
         ],
         compiler_params=params,
+        cost_estimate=pl.CostEstimate(flops=PACK_COST, transcendentals=0, bytes_accessed=0),
         name="pack",
-    )(in_hbm[0], in_hbm[3], in_hbm[4])
-    from_even = lax.ppermute(packed[0], "area", even_pairs)
-    from_odd = lax.ppermute(packed[1], "area", odd_pairs)
-    if swap:
-        vert = [lax.ppermute(packed[2], "depth", swapped)]
-    else:
-        vert = [lax.ppermute(packed[2], "depth", down), lax.ppermute(packed[3], "depth", up)]
-    chunks = math.gcd(layers, 4)
-    block = (layers, rows, width)
-    kept, kap, head, local_sums = pl.pallas_call(
+    )(*in_hbm)
+    from_even = lax.ppermute(packed[1], "area", even_pairs)
+    from_odd = lax.ppermute(packed[2], "area", odd_pairs)
+    if swap:
+        vert = [lax.ppermute(packed[3], "depth", swapped)]
+    else:
+        vert = [lax.ppermute(packed[3], "depth", down), lax.ppermute(packed[4], "depth", up)]
+    kept, kap, local_sums = pl.pallas_call(
         local_kernel,
-        out_shape=[shape(6, *block), shape(*block), shape(*block), shape(2, rows, width)],
-        in_specs=[pl.BlockSpec(memory_space=pltpu.HBM)] * 5,
-        out_specs=whole(4),
-        scratch_shapes=[
-            pltpu.VMEM(block, F32),
-            pltpu.VMEM(block, F32),
-            pltpu.VMEM(block, jnp.int32),
-            pltpu.VMEM(soil_params.shape, F32),
-            pltpu.VMEM((5, kind_count, 8, LANES), F32),
-            pltpu.SemaphoreType.DMA((4, chunks)),
-            pltpu.SemaphoreType.DMA(()),
-        ],
+        out_shape=[shape(6, layers, rows, width), shape(layers, rows, width), shape(2, rows, width)],
+        in_specs=whole(5),
+        out_specs=whole(3),
         compiler_params=params,
         name="local",
-    )(in_hbm[0], in_hbm[1], in_hbm[2], in_hbm[3], in_hbm[4])
+    )(pressure, theta_old, source, soil_type, packed[0])
     smooth, sums, to_even, to_odd = pl.pallas_call(
         functools.partial(fine_kernel, swap),
         out_shape=[
@@ -481,7 +438,7 @@
         out_specs=whole(4),
         compiler_params=params,
         name="fine",
-    )(head, kept, kap, local_sums, from_even, from_odd, *vert)
+    )(pressure, kept, kap, local_sums, from_even, from_odd, *vert)
     from_even = lax.ppermute(to_even, "area", even_pairs)
     from_odd = lax.ppermute(to_odd, "area", odd_pairs)
     if swap:

time: 29.4 us -> 26.4 us (0.90)
  the two profiles are of different devices: /device:TPU:9 before, /device:TPU:27 now
where the time goes in v4:
time: 26.4 us; the launch traced here: 26.3 us
  waiting for transfers between devices  11.5 us (44%)
  starting transfers between devices  7.04 us (27%)
  Pallas kernels  7.03 us (27%)
  between operations  0.71 us (3%)
    ppermute x1, waiting for transfers between devices, shards(): from_odd = lax.ppermute(to_odd, 'area', odd_pairs)  5.96 us
    ppermute x1, waiting for transfers between devices, shards(): their_halo = lax.ppermute(halo, 'depth', swapped)  3.78 us
    ppermute x1, starting transfers between devices, shards(): from_odd = lax.ppermute(packed[2], 'area', odd_pairs)  3.05 us
    pallas_call x1, Pallas kernels, shards(): pl.pallas_call(local_kernel, out_shape=[shape(6, layers, rows, width), sh...  2.58 us
    ppermute x1, starting transfers between devices, shards(): from_odd = lax.ppermute(to_odd, 'area', odd_pairs)  2.15 us
    pallas_call x1, Pallas kernels, shards(): pl.pallas_call(functools.partial(fine_kernel, swap), out_shape=[shape(lay...  1.74 us
    pallas_call x1, Pallas kernels, shards(): pl.pallas_call(functools.partial(pack_kernel, swap), out_shape=[shape(5,...  1.6 us
    ppermute x1, waiting for transfers between devices, shards(): from_odd = lax.ppermute(packed[2], 'area', odd_pairs)  1.14 us
  transfers between devices with their start and end apart: 7, of which 4 were waited for; matrix products, arithmetic and copies ran while one was open for 0% of the time, Pallas kernels for 10%

profile of v4, /device:TPU:27, one launch (start us, length us, event | category | flops | bytes accessed | tf_op | source)
XLA Modules:
  0.0 26.3 jit_solution(18351426901400099824)
XLA Ops:
  0.6 0.0 copy-start
  0.6 0.0 copy-start.3
  0.7 0.0 copy-start.2
  0.7 0.0 copy-start.1
  0.7 1.6 %pack.1 = (f32[5,12,8,128]{3,2,1,0:T(8,128)S(1)}, f32[2,16,1024]{2,1,0:T(8,128)S(1)}, f32[2,16,1024]{2,1,0:T(8,128)S(1)}, f32[2,8,1024]{2,1,0:T(8,128)S(1)}) custom-call(f32[16,8,1024]{2,1,0:T(8,128)} %p_ref.5, s32[16,8,1024]{2,1,0:T(8,128)} %soil_ref.3, f32[5,12]{1,0:T(8,128)} %params_ref.1), custom_call_target="tpu_custom_call" | custom-call | flops 4000000000 | tf_op jit(solution)/shard_map/pack/pallas_call | solution.py:396
  2.3 0.7 %collective-permute-start = (f32[2,16,1024]{2,1,0:T(8,128)S(1)}, f32[2,16,1024]{2,1,0:T(8,128)S(1)}, u32[]{:S(2)}, u32[]{:S(2)}) collective-permute-start(f32[2,16,1024]{2,1,0:T(8,128)S(1)} %get-tuple-element.17), channel_id=1, source_target_pairs={{0,2},{2,0},{4,6},{6,4},{8,10},{10,8},{12,14},{14,12},{16,18},{18,... | collective-permute-start | bytes 393224 | tf_op jit(solution)/shard_map/ppermute | solution.py:415
  3.0 3.0 %collective-permute-start.1 = (f32[2,16,1024]{2,1,0:T(8,128)S(1)}, f32[2,16,1024]{2,1,0:T(8,128)S(1)}, u32[]{:S(2)}, u32[]{:S(2)}) collective-permute-start(f32[2,16,1024]{2,1,0:T(8,128)S(1)} %get-tuple-element.18), channel_id=1, source_target_pairs={{2,4},{4,2},{6,8},{8,6},{10,12},{12,10},{14,16},{16,14},{18,20},{2... | collective-permute-start | bytes 393224 | tf_op jit(solution)/shard_map/ppermute | solution.py:416
  6.1 0.3 %collective-permute-start.2 = (f32[2,8,1024]{2,1,0:T(8,128)S(1)}, f32[2,8,1024]{2,1,0:T(8,128)S(1)}, u32[]{:S(2)}, u32[]{:S(2)}) collective-permute-start(f32[2,8,1024]{2,1,0:T(8,128)S(1)} %get-tuple-element.19), channel_id=1, source_target_pairs={{0,1},{1,0},{2,3},{3,2},{4,5},{5,4},{6,7},{7,6},{8,9},{9,8},{10,11... | collective-permute-start | bytes 196616 | tf_op jit(solution)/shard_map/ppermute | solution.py:418
  6.4 0.0 copy-done
  6.4 0.0 copy-done.3
  6.4 0.0 copy-done.2
  6.4 0.0 copy-done.1
  6.4 2.6 %local.1 = (f32[6,16,8,1024]{3,2,1,0:T(8,128)S(1)}, f32[16,8,1024]{2,1,0:T(8,128)S(1)}, f32[2,8,1024]{2,1,0:T(8,128)S(1)}) custom-call(f32[16,8,1024]{2,1,0:T(8,128)S(1)} %copy-done, f32[16,8,1024]{2,1,0:T(8,128)S(1)} %copy-done.1, f32[16,8,1024]{2,1,0:T(8,128)S(1)} %copy-done.2, s32[16,8,1024]{2,1,0:T(8,128)S(1)} %copy-done.3, ...), custom_call_target="tpu_custom_call" | custom-call | tf_op jit(solution)/shard_map/local/pallas_call | solution.py:421
  9.0 0.6 %collective-permute-done.2.rest_0_ = f32[2,8,1024]{2,1,0:T(8,128)S(1)} collective-permute-done((f32[2,8,1024]{2,1,0:T(8,128)S(1)}, f32[2,8,1024]{2,1,0:T(8,128)S(1)}, u32[]{:S(2)}, u32[]{:S(2)}) %collective-permute-start.2) | collective-permute-done | bytes 65568 | tf_op jit(solution)/shard_map/ppermute | solution.py:418
  9.6 0.0 collective-permute-done.from_even_ref
  9.6 1.1 %collective-permute-done.1.from_odd_ref = f32[2,16,1024]{2,1,0:T(8,128)S(1)} collective-permute-done((f32[2,16,1024]{2,1,0:T(8,128)S(1)}, f32[2,16,1024]{2,1,0:T(8,128)S(1)}, u32[]{:S(2)}, u32[]{:S(2)}) %collective-permute-start.1) | collective-permute-done | bytes 131104 | tf_op jit(solution)/shard_map/ppermute | solution.py:416
  10.7 1.7 %fine.1 = (f32[16,8,1024]{2,1,0:T(8,128)S(1)}, f32[5,8,1024]{2,1,0:T(8,128)S(1)}, f32[40,1024]{1,0:T(8,128)S(1)}, f32[40,1024]{1,0:T(8,128)S(1)}) custom-call(f32[16,8,1024]{2,1,0:T(8,128)S(1)} %copy-done, f32[6,16,8,1024]{3,2,1,0:T(8,128)S(1)} %get-tuple-element.14.kept_ref, f32[16,8,1024]{2,1,0:T(8,128)S(1)} %get-tuple-element.15.kap_ref, ...), custom_call_target="tpu_custom_call" | custom-call | tf_op jit(solution)/shard_map/fine/pallas_call | solution.py:429
  12.5 0.1 collective-permute-start.4
  12.6 2.1 %collective-permute-start.5 = (f32[40,1024]{1,0:T(8,128)S(1)}, f32[40,1024]{1,0:T(8,128)S(1)}, u32[]{:S(2)}, u32[]{:S(2)}) collective-permute-start(f32[40,1024]{1,0:T(8,128)S(1)} %get-tuple-element.23.to_odd_ref), channel_id=1, source_target_pairs={{2,4},{4,2},{6,8},{8,6},{10,12},{12,10},{14,16},{16,14},{18,20},{2... | collective-permute-start | bytes 491528 | tf_op jit(solution)/shard_map/ppermute | solution.py:443
  14.8 0.3 %collective-permute-start.3 = (f32[5,8,1024]{2,1,0:T(8,128)S(1)}, f32[5,8,1024]{2,1,0:T(8,128)S(1)}, u32[]{:S(2)}, u32[]{:S(2)}) collective-permute-start(f32[5,8,1024]{2,1,0:T(8,128)S(1)} %get-tuple-element.21.sums_ref), channel_id=1, source_target_pairs={{0,1},{1,0},{2,3},{3,2},{4,5},{5,4},{6,7},{7,6},{8,9},{9,8},{10,11... | collective-permute-start | bytes 491528 | tf_op jit(solution)/shard_map/ppermute | solution.py:445
  15.1 0.0 collective-permute-done.4.from_even_ref
  15.1 6.0 %collective-permute-done.5.from_odd_ref = f32[40,1024]{1,0:T(8,128)S(1)} collective-permute-done((f32[40,1024]{1,0:T(8,128)S(1)}, f32[40,1024]{1,0:T(8,128)S(1)}, u32[]{:S(2)}, u32[]{:S(2)}) %collective-permute-start.5) | collective-permute-done | bytes 163872 | tf_op jit(solution)/shard_map/ppermute | solution.py:443
  21.1 0.3 %collective-permute-start.6 = (f32[2,8,1024]{2,1,0:T(8,128)S(1)}, f32[2,8,1024]{2,1,0:T(8,128)S(1)}, u32[]{:S(2)}, u32[]{:S(2)}) collective-permute-start(f32[2,8,1024]{2,1,0:T(8,128)S(1)} %edge.1.halo_ref), channel_id=1, source_target_pairs={{0,1},{1,0},{2,3},{3,2},{4,5},{5,4},{6,7},{7,6},{8,9},{9,8},{10,11... | collective-permute-start | bytes 196616 | tf_op jit(solution)/shard_map/ppermute | solution.py:457
  21.4 0.0 collective-permute-done.3.their_sums_ref
  21.4 3.8 %collective-permute-done.6.their_halo_ref = f32[2,8,1024]{2,1,0:T(8,128)S(1)} collective-permute-done((f32[2,8,1024]{2,1,0:T(8,128)S(1)}, f32[2,8,1024]{2,1,0:T(8,128)S(1)}, u32[]{:S(2)}, u32[]{:S(2)}) %collective-permute-start.6) | collective-permute-done | bytes 65568 | tf_op jit(solution)/shard_map/ppermute | solution.py:457
  25.2 1.1 %coarse.1 = (f32[16,8,1024]{2,1,0:T(8,128)}, f32[8,1024]{1,0:T(8,128)}) custom-call(f32[16,8,1024]{2,1,0:T(8,128)S(1)} %get-tuple-element.20.smooth_ref, f32[5,8,1024]{2,1,0:T(8,128)S(1)} %get-tuple-element.21.sums_ref, f32[5,8,1024]{2,1,0:T(8,128)S(1)} %collective-permute-done.3.their_sums_ref, f32[2,8,1024]{2,1,0:T(8,128)S(1)} %edge.1.halo_ref, ...), custom_call_target="tpu_custom_call" | custom-call | tf_op jit(solution)/shard_map/coarse/pallas_call | solution.py:460
  (1 shorter events, 0.0 us)
Async XLA Ops:
  0.6 5.8 %copy-start = (f32[16,8,1024]{2,1,0:T(8,128)S(1)}, f32[16,8,1024]{2,1,0:T(8,128)}, u32[]{:S(2)}) copy-start(f32[16,8,1024]{2,1,0:T(8,128)} %p_ref.5) | copy-start | bytes 1572868
  0.6 5.8 %copy-start.3 = (s32[16,8,1024]{2,1,0:T(8,128)S(1)}, s32[16,8,1024]{2,1,0:T(8,128)}, u32[]{:S(2)}) copy-start(s32[16,8,1024]{2,1,0:T(8,128)} %soil_ref.3) | copy-start | bytes 1572868
  0.7 5.8 %copy-start.2 = (f32[16,8,1024]{2,1,0:T(8,128)S(1)}, f32[16,8,1024]{2,1,0:T(8,128)}, u32[]{:S(2)}) copy-start(f32[16,8,1024]{2,1,0:T(8,128)} %source_ref.1) | copy-start | bytes 1572868
  0.7 5.7 %copy-start.1 = (f32[16,8,1024]{2,1,0:T(8,128)S(1)}, f32[16,8,1024]{2,1,0:T(8,128)}, u32[]{:S(2)}) copy-start(f32[16,8,1024]{2,1,0:T(8,128)} %theta_ref.1) | copy-start | bytes 1572868
  2.3 7.3 %collective-permute-start = (f32[2,16,1024]{2,1,0:T(8,128)S(1)}, f32[2,16,1024]{2,1,0:T(8,128)S(1)}, u32[]{:S(2)}, u32[]{:S(2)}) collective-permute-start(f32[2,16,1024]{2,1,0:T(8,128)S(1)} %get-tuple-element.17), channel_id=1, source_target_pairs={{0,2},{2,0},{4,6},{6,4},{8,10},{10,8},{12,14},{14,12},{16,18},{18,... | collective-permute-start | bytes 393224 | tf_op jit(solution)/shard_map/ppermute | solution.py:415
  3.0 7.7 %collective-permute-start.1 = (f32[2,16,1024]{2,1,0:T(8,128)S(1)}, f32[2,16,1024]{2,1,0:T(8,128)S(1)}, u32[]{:S(2)}, u32[]{:S(2)}) collective-permute-start(f32[2,16,1024]{2,1,0:T(8,128)S(1)} %get-tuple-element.18), channel_id=1, source_target_pairs={{2,4},{4,2},{6,8},{8,6},{10,12},{12,10},{14,16},{16,14},{18,20},{2... | collective-permute-start | bytes 393224 | tf_op jit(solution)/shard_map/ppermute | solution.py:416
  6.1 3.5 %collective-permute-start.2 = (f32[2,8,1024]{2,1,0:T(8,128)S(1)}, f32[2,8,1024]{2,1,0:T(8,128)S(1)}, u32[]{:S(2)}, u32[]{:S(2)}) collective-permute-start(f32[2,8,1024]{2,1,0:T(8,128)S(1)} %get-tuple-element.19), channel_id=1, source_target_pairs={{0,1},{1,0},{2,3},{3,2},{4,5},{5,4},{6,7},{7,6},{8,9},{9,8},{10,11... | collective-permute-start | bytes 196616 | tf_op jit(solution)/shard_map/ppermute | solution.py:418
  12.5 2.6 %collective-permute-start.4 = (f32[40,1024]{1,0:T(8,128)S(1)}, f32[40,1024]{1,0:T(8,128)S(1)}, u32[]{:S(2)}, u32[]{:S(2)}) collective-permute-start(f32[40,1024]{1,0:T(8,128)S(1)} %get-tuple-element.22.to_even_ref), channel_id=1, source_target_pairs={{0,2},{2,0},{4,6},{6,4},{8,10},{10,8},{12,14},{14,12},{16,18},{18,... | collective-permute-start | bytes 491528 | tf_op jit(solution)/shard_map/ppermute | solution.py:442
  12.6 8.4 %collective-permute-start.5 = (f32[40,1024]{1,0:T(8,128)S(1)}, f32[40,1024]{1,0:T(8,128)S(1)}, u32[]{:S(2)}, u32[]{:S(2)}) collective-permute-start(f32[40,1024]{1,0:T(8,128)S(1)} %get-tuple-element.23.to_odd_ref), channel_id=1, source_target_pairs={{2,4},{4,2},{6,8},{8,6},{10,12},{12,10},{14,16},{16,14},{18,20},{2... | collective-permute-start | bytes 491528 | tf_op jit(solution)/shard_map/ppermute | solution.py:443
  14.8 6.7 %collective-permute-start.3 = (f32[5,8,1024]{2,1,0:T(8,128)S(1)}, f32[5,8,1024]{2,1,0:T(8,128)S(1)}, u32[]{:S(2)}, u32[]{:S(2)}) collective-permute-start(f32[5,8,1024]{2,1,0:T(8,128)S(1)} %get-tuple-element.21.sums_ref), channel_id=1, source_target_pairs={{0,1},{1,0},{2,3},{3,2},{4,5},{5,4},{6,7},{7,6},{8,9},{9,8},{10,11... | collective-permute-start | bytes 491528 | tf_op jit(solution)/shard_map/ppermute | solution.py:445
  21.1 4.1 %collective-permute-start.6 = (f32[2,8,1024]{2,1,0:T(8,128)S(1)}, f32[2,8,1024]{2,1,0:T(8,128)S(1)}, u32[]{:S(2)}, u32[]{:S(2)}) collective-permute-start(f32[2,8,1024]{2,1,0:T(8,128)S(1)} %edge.1.halo_ref), channel_id=1, source_target_pairs={{0,1},{1,0},{2,3},{3,2},{4,5},{5,4},{6,7},{7,6},{8,9},{9,8},{10,11... | collective-permute-start | bytes 196616 | tf_op jit(solution)/shard_map/ppermute | solution.py:457

commit v5 on v4

--- a/solution.py
+++ b/solution.py
@@ -34,21 +34,6 @@
     }
 
 
-def gather(row, kinds):
-    table = jnp.broadcast_to(jnp.pad(row, ((0, 0), (0, LANES - row.shape[1]))), (8, LANES))
-    rows = []
-    for r in range(0, kinds.shape[0], 8):
-        cols = []
-        for c in range(0, kinds.shape[1], LANES):
-            cols.append(
-                jnp.take_along_axis(
-                    table, kinds[r : r + 8, c : c + LANES], axis=1, mode="promise_in_bounds"
-                )
-            )
-        rows.append(jnp.concatenate(cols, axis=1))
-    return rows[0] if len(rows) == 1 else jnp.concatenate(rows, axis=0)
-
-
 def spread_table(table, tab_ref):
     for row_id, row in table.items():
         for kind in range(row.shape[1]):
@@ -57,7 +42,7 @@
 
 def pick(tab_ref, row_id, bits, width):
     level = [
-        jnp.concatenate([tab_ref[row_id, kind]] * (width // LANES), axis=1)
+        jnp.tile(tab_ref[row_id, kind], (bits[0].shape[0] // 8, width // LANES))
         for kind in range(tab_ref.shape[1])
     ]
     for bit in bits:
@@ -86,14 +71,40 @@
     return kappa, half * half, ratio * lax.rsqrt(q)
 
 
-def kappa_by_gather(h, kinds, table):
-    return hydraulics(
-        h, gather(table[T_A], kinds), gather(table[T_N], kinds), gather(table[T_SK], kinds)
-    )[0]
+def code(kinds):
+    return (kinds + 1).astype(F32)
+
+
+def code_params(codes, tab_ref):
+    kinds = jnp.maximum(codes.astype(jnp.int32) - 1, 0)
+    bits = type_bits(kinds, tab_ref.shape[1])
+    pa, pn, psk = [pick(tab_ref, i, bits, codes.shape[1]) for i in (T_A, T_N, T_SK)]
+    return pa, pn, jnp.where(codes > 0.5, psk, 0.0)
 
 
 def even_area():
     return lax.rem(lax.axis_index("area"), 2) == 0
+
+
+def paired():
+    area, last = lax.axis_index("area"), lax.axis_size("area") - 1
+    is_even = even_area()
+    return (
+        jnp.logical_or(jnp.logical_not(is_even), area < last),
+        jnp.where(is_even, area, last - area) > 0,
+    )
+
+
+def full_swap(pairs, areas, depths):
+    target = {a: b for a, b in pairs}
+    target.update({b: a for a, b in pairs})
+    moves = []
+    for a in range(areas):
+        for d in range(depths):
+            other = d if a in target else d ^ 1
+            if other < depths:
+                moves.append((a * depths + d, target.get(a, a) * depths + other))
+    return moves
 
 
 def pack_kernel(swap, p_ref, soil_ref, params_ref, tab_ref, even_ref, odd_ref, *rest):
@@ -120,21 +131,15 @@
     for copy in copies:
         copy.start()
     copies[0].wait()
-    table = build_table(params_buf)
-    spread_table(table, tab_ref)
+    spread_table(build_table(params_buf), tab_ref)
     for copy in copies[1:]:
         copy.wait()
-    low_h, high_h = p_buf[0], p_buf[1]
-    low_k = kappa_by_gather(low_h, soil_buf[0], table)
-    high_k = kappa_by_gather(high_h, soil_buf[1], table)
-    even_ref[0] = jnp.where(even, high_h, low_h)
-    even_ref[1] = jnp.where(even, high_k, low_k)
-    odd_ref[0] = jnp.where(even, low_h, high_h)
-    odd_ref[1] = jnp.where(even, low_k, high_k)
+    for i, low, high in ((0, p_buf[0], p_buf[1]), (1, code(soil_buf[0]), code(soil_buf[1]))):
+        even_ref[i] = jnp.where(even, high, low)
+        odd_ref[i] = jnp.where(even, low, high)
     for side, out_ref in enumerate(vert_refs):
-        h = vert_p[side]
-        out_ref[0] = h
-        out_ref[1] = kappa_by_gather(h, vert_soil[side], table)
+        out_ref[0] = vert_p[side]
+        out_ref[1] = code(vert_soil[side])
 
 
 def row_iota(shape):
@@ -199,25 +204,39 @@
     sums_ref[1] = sum_rate
 
 
-def fine_kernel(swap, p_ref, kept_ref, kap_ref, local_ref, from_even_ref, from_odd_ref, *rest):
+def fine_kernel(swap, p_ref, kept_ref, kap_ref, local_ref, tab_ref, *rest):
     layers, rows, width = p_ref.shape
-    if swap:
-        vert_ref, rest = rest[0], rest[1:]
-    else:
-        top_ref, bottom_ref, rest = rest[0], rest[1], rest[2:]
-    smooth_ref, sums_ref, to_even_ref, to_odd_ref = rest
+    left = iter(rest)
+    from_even_ref = next(left)
+    from_odd_ref = next(left)
+    vert_refs = [next(left) for _ in range(1 if swap else 2)]
+    smooth_ref, sums_ref, to_even_ref, to_odd_ref, rim_ref, side_ref = left
     even = even_area()
     spot = row_iota((rows, width))
     is_first, is_last = spot == 0, spot == rows - 1
 
     if swap:
         at_top = lax.axis_index("depth") == 0
-        top_k = jnp.where(at_top, 0.0, vert_ref[1])
-        bottom_k = jnp.where(at_top, vert_ref[1], 0.0)
+        (vert_ref,) = vert_refs
         top_h = bottom_h = vert_ref[0]
+        vert_k = hydraulics(top_h, *code_params(vert_ref[1], tab_ref))[0]
+        top_k = jnp.where(at_top, 0.0, vert_k)
+        bottom_k = jnp.where(at_top, vert_k, 0.0)
     else:
-        top_h, top_k = top_ref[0], top_ref[1]
-        bottom_h, bottom_k = bottom_ref[0], bottom_ref[1]
+        top_ref, bottom_ref = vert_refs
+        top_h, bottom_h = top_ref[0], bottom_ref[0]
+        top_k = hydraulics(top_h, *code_params(top_ref[1], tab_ref))[0]
+        bottom_k = hydraulics(bottom_h, *code_params(bottom_ref[1], tab_ref))[0]
+    def side_step(i, carry):
+        at = pl.ds(i * 8, 8)
+        for side, (from_ref, live) in enumerate(zip((from_even_ref, from_odd_ref), paired())):
+            fields = code_params(jnp.where(live, from_ref[1, at, :], 0.0), tab_ref)
+            for spot, field in enumerate(fields):
+                rim_ref[side, spot, at, :] = field
+            side_ref[side, at, :] = hydraulics(from_ref[0, at, :], *fields)[0]
+        return carry
+
+    lax.fori_loop(0, layers // 8, side_step, 0)
 
     def step(layer, carry):
         sum_kh, sum_k, sum_cap, sum_sat, flux_x, flux_y = carry
@@ -227,8 +246,8 @@
         h_u = jnp.where(layer == 0, top_h, p_ref[above])
         k_d = jnp.where(layer == layers - 1, bottom_k, kap_ref[below])
         h_d = jnp.where(layer == layers - 1, bottom_h, p_ref[below])
-        even_k = from_even_ref[1, pl.ds(layer, 1), :]
-        odd_k = from_odd_ref[1, pl.ds(layer, 1), :]
+        even_k = side_ref[0, pl.ds(layer, 1), :]
+        odd_k = side_ref[1, pl.ds(layer, 1), :]
         even_h = from_even_ref[0, pl.ds(layer, 1), :]
         odd_h = from_odd_ref[0, pl.ds(layer, 1), :]
         lo_k = jnp.where(even, odd_k, even_k)
@@ -250,10 +269,13 @@
         cond = kap * kap
         flux_x = flux_x + kap * from_below(kap, 0.0) * (pltpu.roll(h, rows - 1, 0) - h)
         flux_y = flux_y + kap * from_right(kap) * (pltpu.roll(h, width - 1, 1) - h)
-        for at, value in ((0, h), (layers, kap)):
+        for even_at, odd_at, value in (
+            (to_even_ref, to_odd_ref, h),
+            (rim_ref.at[0, 3], rim_ref.at[1, 3], kap),
+        ):
             low, high = value[0:1, :], value[rows - 1 : rows, :]
-            to_even_ref[pl.ds(at + layer, 1), :] = jnp.where(even, high, low)
-            to_odd_ref[pl.ds(at + layer, 1), :] = jnp.where(even, low, high)
+            even_at[pl.ds(layer, 1), :] = jnp.where(even, high, low)
+            odd_at[pl.ds(layer, 1), :] = jnp.where(even, low, high)
         return (
             sum_kh + cond * h,
             sum_k + cond,
@@ -273,7 +295,7 @@
     )
     for at, value in enumerate((sum_kh, sum_k, sum_cap, restricted, sum_rate)):
         sums_ref[at] = value
-    at = 2 * layers
+    at = layers
     tails = []
     for edge, inner in ((rows - 1, rows - 2), (0, 1)):
         tail = [
@@ -292,19 +314,17 @@
     to_odd_ref[at : at + 8, :] = jnp.where(even, low, high)
 
 
-def edge_kernel(to_even_ref, to_odd_ref, from_even_ref, from_odd_ref, halo_ref):
-    layers = (to_even_ref.shape[0] - 8) // 2
-    at = 2 * layers
-    for side, (mine_ref, their_ref) in enumerate(
-        ((to_even_ref, from_even_ref), (to_odd_ref, from_odd_ref))
+def edge_kernel(rim_ref, to_odd_ref, to_even_ref, from_odd_ref, from_even_ref, halo_ref):
+    layers = rim_ref.shape[2]
+    at = layers
+    for side, (mine_ref, their_ref, live) in enumerate(
+        zip((to_even_ref, to_odd_ref), (from_even_ref, from_odd_ref), paired())
     ):
-        flux = (
-            mine_ref[layers:at, :]
-            * their_ref[layers:at, :]
-            * (their_ref[0:layers, :] - mine_ref[0:layers, :])
-        )
+        theirs = their_ref[0:layers, :]
+        kap = hydraulics(theirs, rim_ref[side, 0], rim_ref[side, 1], rim_ref[side, 2])[0]
+        flux = rim_ref[side, 3] * kap * (theirs - mine_ref[0:layers, :])
         flux = jnp.sum(flux, axis=0, keepdims=True)
-        block = their_ref[at : at + 8, :]
+        block = jnp.where(live, their_ref[at : at + 8, :], 0.0)
         spot = row_iota(block.shape)
         block = jnp.where(spot == 5, block - flux, block)
         halo_ref[side] = jnp.where(spot == 7, flux, block)
@@ -377,8 +397,9 @@
     areas = lax.axis_size("area")
     depths = lax.axis_size("depth")
     swap = depths == 2
-    even_pairs = [p for i in range(0, areas - 1, 2) for p in ((i, i + 1), (i + 1, i))]
-    odd_pairs = [p for i in range(1, areas - 1, 2) for p in ((i, i + 1), (i + 1, i))]
+    both = ("area", "depth")
+    even_moves = full_swap([(i, i + 1) for i in range(0, areas - 1, 2)], areas, depths)
+    odd_moves = full_swap([(i, i + 1) for i in range(1, areas - 1, 2)], areas, depths)
     down = [(i, i + 1) for i in range(depths - 1)]
     up = [(b, a) for a, b in down]
     swapped = [(0, 1), (1, 0)]
@@ -386,7 +407,7 @@
     def shape(*dims):
         return jax.ShapeDtypeStruct(dims, F32)
 
-    params = pltpu.CompilerParams(vmem_limit_bytes=48 << 20)
+    params = pltpu.CompilerParams(vmem_limit_bytes=16 << 20)
     verts = 1 if swap else 2
     kind_count = soil_params.shape[1]
     in_hbm = [
@@ -412,8 +433,8 @@
         cost_estimate=pl.CostEstimate(flops=PACK_COST, transcendentals=0, bytes_accessed=0),
         name="pack",
     )(*in_hbm)
-    from_even = lax.ppermute(packed[1], "area", even_pairs)
-    from_odd = lax.ppermute(packed[2], "area", odd_pairs)
+    from_odd = lax.ppermute(packed[2], both, odd_moves)
+    from_even = lax.ppermute(packed[1], both, even_moves)
     if swap:
         vert = [lax.ppermute(packed[3], "depth", swapped)]
     else:
@@ -426,21 +447,23 @@
         compiler_params=params,
         name="local",
     )(pressure, theta_old, source, soil_type, packed[0])
-    smooth, sums, to_even, to_odd = pl.pallas_call(
+    smooth, sums, to_even, to_odd, rim = pl.pallas_call(
         functools.partial(fine_kernel, swap),
         out_shape=[
             shape(layers, rows, width),
             shape(5, rows, width),
-            shape(2 * layers + 8, width),
-            shape(2 * layers + 8, width),
+            shape(layers + 8, width),
+            shape(layers + 8, width),
+            shape(2, 4, layers, width),
         ],
-        in_specs=whole(6 + verts),
-        out_specs=whole(4),
+        in_specs=whole(7 + verts),
+        out_specs=whole(5),
+        scratch_shapes=[pltpu.VMEM((2, layers, width), F32)],
         compiler_params=params,
         name="fine",
-    )(pressure, kept, kap, local_sums, from_even, from_odd, *vert)
-    from_even = lax.ppermute(to_even, "area", even_pairs)
-    from_odd = lax.ppermute(to_odd, "area", odd_pairs)
+    )(pressure, kept, kap, local_sums, packed[0], from_even, from_odd, *vert)
+    from_odd = lax.ppermute(to_odd, both, odd_moves)
+    from_even = lax.ppermute(to_even, both, even_moves)
     if swap:
         their_sums = lax.ppermute(sums, "depth", swapped)
     else:
@@ -448,11 +471,11 @@
     halo = pl.pallas_call(
         edge_kernel,
         out_shape=shape(2, 8, width),
-        in_specs=whole(4),
+        in_specs=whole(5),
         out_specs=whole(1)[0],
         compiler_params=params,
         name="edge",
-    )(to_even, to_odd, from_even, from_odd)
+    )(rim, to_odd, to_even, from_odd, from_even)
     if swap:
         their_halo = lax.ppermute(halo, "depth", swapped)
     else:

time: 26.4 us -> 23 us (0.87)
  the two profiles are of different devices: /device:TPU:27 before, /device:TPU:0 now
where the time goes in v5:
time: 23 us; the launch traced here: 22.9 us
  starting transfers between devices  8.44 us (37%)
  Pallas kernels  7.24 us (31%)
  waiting for transfers between devices  6.47 us (28%)
  between operations  0.69 us (3%)
    pallas_call x1, Pallas kernels, shards(): pl.pallas_call(local_kernel, out_shape=[shape(6, layers, rows, width), sh...  2.58 us
    ppermute x1, starting transfers between devices, shards(): from_odd = lax.ppermute(packed[2], both, odd_moves)  2.56 us
    ppermute x1, starting transfers between devices, shards(): their_halo = lax.ppermute(halo, 'depth', swapped)  2.55 us
    ppermute x1, waiting for transfers between devices, shards(): from_odd = lax.ppermute(to_odd, both, odd_moves)  2.54 us
    pallas_call x1, Pallas kernels, shards(): pl.pallas_call(functools.partial(fine_kernel, swap), out_shape=[shape(lay...  2.18 us
    ppermute x1, starting transfers between devices, shards(): from_odd = lax.ppermute(to_odd, both, odd_moves)  2.08 us
    ppermute x1, waiting for transfers between devices, shards(): vert = [lax.ppermute(packed[3], 'depth', swapped)]  1.68 us
    pallas_call x1, Pallas kernels, shards(): pl.pallas_call(functools.partial(pack_kernel, swap), out_shape=[shape(5,...  1.23 us
  transfers between devices with their start and end apart: 7, of which 4 were waited for; matrix products, arithmetic and copies ran while one was open for 0% of the time, Pallas kernels for 12%

profile of v5, /device:TPU:0, one launch (start us, length us, event | category | flops | bytes accessed | tf_op | source)
XLA Modules:
  0.0 22.9 jit_solution(4167199693300500292)
XLA Ops:
  0.6 0.0 copy-start
  0.6 0.0 copy-start.3
  0.7 0.0 copy-start.2
  0.7 0.0 copy-start.1
  0.7 1.2 %pack.1 = (f32[5,12,8,128]{3,2,1,0:T(8,128)S(1)}, f32[2,16,1024]{2,1,0:T(8,128)S(1)}, f32[2,16,1024]{2,1,0:T(8,128)S(1)}, f32[2,8,1024]{2,1,0:T(8,128)S(1)}) custom-call(f32[16,8,1024]{2,1,0:T(8,128)} %p_ref.5, s32[16,8,1024]{2,1,0:T(8,128)} %soil_ref.3, f32[5,12]{1,0:T(8,128)} %params_ref.1), custom_call_target="tpu_custom_call" | custom-call | flops 4000000000 | tf_op jit(solution)/shard_map/pack/pallas_call | solution.py:417
  1.9 0.5 %collective-permute-start = (f32[2,16,1024]{2,1,0:T(8,128)S(1)}, f32[2,16,1024]{2,1,0:T(8,128)S(1)}, u32[]{:S(2)}, u32[]{:S(2)}) collective-permute-start(f32[2,16,1024]{2,1,0:T(8,128)S(1)} %get-tuple-element.18), channel_id=1, source_target_pairs={{0,2},{1,3},{2,0},{3,1},{4,6},{5,7},{6,4},{7,5},{8,10},{9,11},{10,... | collective-permute-start | bytes 393224 | tf_op jit(solution)/shard_map/ppermute | solution.py:437
  2.4 2.6 %collective-permute-start.1 = (f32[2,16,1024]{2,1,0:T(8,128)S(1)}, f32[2,16,1024]{2,1,0:T(8,128)S(1)}, u32[]{:S(2)}, u32[]{:S(2)}) collective-permute-start(f32[2,16,1024]{2,1,0:T(8,128)S(1)} %get-tuple-element.19), channel_id=1, source_target_pairs={{0,1},{1,0},{2,4},{3,5},{4,2},{5,3},{6,8},{7,9},{8,6},{9,7},{10,12... | collective-permute-start | bytes 393224 | tf_op jit(solution)/shard_map/ppermute | solution.py:436
  5.0 0.1 collective-permute-start.2
  5.1 0.0 copy-done
  5.1 0.0 copy-done.3
  5.1 0.0 copy-done.2
  5.1 0.0 copy-done.1
  5.1 2.6 %local.1 = (f32[6,16,8,1024]{3,2,1,0:T(8,128)S(1)}, f32[16,8,1024]{2,1,0:T(8,128)S(1)}, f32[2,8,1024]{2,1,0:T(8,128)S(1)}) custom-call(f32[16,8,1024]{2,1,0:T(8,128)S(1)} %copy-done, f32[16,8,1024]{2,1,0:T(8,128)S(1)} %copy-done.1, f32[16,8,1024]{2,1,0:T(8,128)S(1)} %copy-done.2, s32[16,8,1024]{2,1,0:T(8,128)S(1)} %copy-done.3, ...), custom_call_target="tpu_custom_call" | custom-call | tf_op jit(solution)/shard_map/local/pallas_call | solution.py:442
  7.7 1.7 %collective-permute-done.2.rest_2_ = f32[2,8,1024]{2,1,0:T(8,128)S(1)} collective-permute-done((f32[2,8,1024]{2,1,0:T(8,128)S(1)}, f32[2,8,1024]{2,1,0:T(8,128)S(1)}, u32[]{:S(2)}, u32[]{:S(2)}) %collective-permute-start.2) | collective-permute-done | bytes 65568 | tf_op jit(solution)/shard_map/ppermute | solution.py:439
  9.3 0.0 collective-permute-done.rest_0_
  9.3 0.0 collective-permute-done.1.rest_1_
  9.3 2.2 %fine.1 = (f32[16,8,1024]{2,1,0:T(8,128)S(1)}, f32[5,8,1024]{2,1,0:T(8,128)S(1)}, f32[24,1024]{1,0:T(8,128)S(1)}, f32[24,1024]{1,0:T(8,128)S(1)}, f32[2,4,16,1024]{3,2,1,0:T(8,128)S(1)}) custom-call(f32[16,8,1024]{2,1,0:T(8,128)S(1)} %copy-done, f32[6,16,8,1024]{3,2,1,0:T(8,128)S(1)} %get-tuple-element.15.kept_ref, ...), custom_call_target="tpu_custom_call" | custom-call | tf_op jit(solution)/shard_map/fine/pallas_call | solution.py:450
  11.5 2.1 %collective-permute-start.4 = (f32[24,1024]{1,0:T(8,128)S(1)}, f32[24,1024]{1,0:T(8,128)S(1)}, u32[]{:S(2)}, u32[]{:S(2)}) collective-permute-start(f32[24,1024]{1,0:T(8,128)S(1)} %get-tuple-element.24.to_odd_ref), channel_id=1, source_target_pairs={{0,1},{1,0},{2,4},{3,5},{4,2},{5,3},{6,8},{7,9},{8,6},{9,7},{10,12... | collective-permute-start | bytes 294920 | tf_op jit(solution)/shard_map/ppermute | solution.py:465
  13.6 0.0 collective-permute-start.5
  13.6 0.6 %collective-permute-start.3 = (f32[5,8,1024]{2,1,0:T(8,128)S(1)}, f32[5,8,1024]{2,1,0:T(8,128)S(1)}, u32[]{:S(2)}, u32[]{:S(2)}) collective-permute-start(f32[5,8,1024]{2,1,0:T(8,128)S(1)} %get-tuple-element.22.sums_ref), channel_id=1, source_target_pairs={{0,1},{1,0},{2,3},{3,2},{4,5},{5,4},{6,7},{7,6},{8,9},{9,8},{10,11... | collective-permute-start | bytes 491528 | tf_op jit(solution)/shard_map/ppermute | solution.py:468
  14.3 2.5 %collective-permute-done.4.from_odd_ref = f32[24,1024]{1,0:T(8,128)S(1)} collective-permute-done((f32[24,1024]{1,0:T(8,128)S(1)}, f32[24,1024]{1,0:T(8,128)S(1)}, u32[]{:S(2)}, u32[]{:S(2)}) %collective-permute-start.4) | collective-permute-done | bytes 98336 | tf_op jit(solution)/shard_map/ppermute | solution.py:465
  16.8 0.0 collective-permute-done.5.from_even_ref
  16.8 0.2 edge.1.halo_ref
  17.0 2.5 %collective-permute-start.6 = (f32[2,8,1024]{2,1,0:T(8,128)S(1)}, f32[2,8,1024]{2,1,0:T(8,128)S(1)}, u32[]{:S(2)}, u32[]{:S(2)}) collective-permute-start(f32[2,8,1024]{2,1,0:T(8,128)S(1)} %edge.1.halo_ref), channel_id=1, source_target_pairs={{0,1},{1,0},{2,3},{3,2},{4,5},{5,4},{6,7},{7,6},{8,9},{9,8},{10,11... | collective-permute-start | bytes 196616 | tf_op jit(solution)/shard_map/ppermute | solution.py:480
  19.5 1.1 %collective-permute-done.3.their_sums_ref = f32[5,8,1024]{2,1,0:T(8,128)S(1)} collective-permute-done((f32[5,8,1024]{2,1,0:T(8,128)S(1)}, f32[5,8,1024]{2,1,0:T(8,128)S(1)}, u32[]{:S(2)}, u32[]{:S(2)}) %collective-permute-start.3) | collective-permute-done | bytes 163872 | tf_op jit(solution)/shard_map/ppermute | solution.py:468
  20.6 1.2 %collective-permute-done.6.their_halo_ref = f32[2,8,1024]{2,1,0:T(8,128)S(1)} collective-permute-done((f32[2,8,1024]{2,1,0:T(8,128)S(1)}, f32[2,8,1024]{2,1,0:T(8,128)S(1)}, u32[]{:S(2)}, u32[]{:S(2)}) %collective-permute-start.6) | collective-permute-done | bytes 65568 | tf_op jit(solution)/shard_map/ppermute | solution.py:480
  21.8 1.1 %coarse.1 = (f32[16,8,1024]{2,1,0:T(8,128)}, f32[8,1024]{1,0:T(8,128)}) custom-call(f32[16,8,1024]{2,1,0:T(8,128)S(1)} %get-tuple-element.21.smooth_ref, f32[5,8,1024]{2,1,0:T(8,128)S(1)} %get-tuple-element.22.sums_ref, f32[5,8,1024]{2,1,0:T(8,128)S(1)} %collective-permute-done.3.their_sums_ref, f32[2,8,1024]{2,1,0:T(8,128)S(1)} %edge.1.halo_ref, ...), custom_call_target="tpu_custom_call" | custom-call | tf_op jit(solution)/shard_map/coarse/pallas_call | solution.py:483
Async XLA Ops:
  0.6 4.4 %copy-start = (f32[16,8,1024]{2,1,0:T(8,128)S(1)}, f32[16,8,1024]{2,1,0:T(8,128)}, u32[]{:S(2)}) copy-start(f32[16,8,1024]{2,1,0:T(8,128)} %p_ref.5) | copy-start | bytes 1572868
  0.6 4.4 %copy-start.3 = (s32[16,8,1024]{2,1,0:T(8,128)S(1)}, s32[16,8,1024]{2,1,0:T(8,128)}, u32[]{:S(2)}) copy-start(s32[16,8,1024]{2,1,0:T(8,128)} %soil_ref.3) | copy-start | bytes 1572868
  0.7 4.4 %copy-start.2 = (f32[16,8,1024]{2,1,0:T(8,128)S(1)}, f32[16,8,1024]{2,1,0:T(8,128)}, u32[]{:S(2)}) copy-start(f32[16,8,1024]{2,1,0:T(8,128)} %source_ref.1) | copy-start | bytes 1572868
  0.7 4.4 %copy-start.1 = (f32[16,8,1024]{2,1,0:T(8,128)S(1)}, f32[16,8,1024]{2,1,0:T(8,128)}, u32[]{:S(2)}) copy-start(f32[16,8,1024]{2,1,0:T(8,128)} %theta_ref.1) | copy-start | bytes 1572868
  1.9 7.4 %collective-permute-start = (f32[2,16,1024]{2,1,0:T(8,128)S(1)}, f32[2,16,1024]{2,1,0:T(8,128)S(1)}, u32[]{:S(2)}, u32[]{:S(2)}) collective-permute-start(f32[2,16,1024]{2,1,0:T(8,128)S(1)} %get-tuple-element.18), channel_id=1, source_target_pairs={{0,2},{1,3},{2,0},{3,1},{4,6},{5,7},{6,4},{7,5},{8,10},{9,11},{10,... | collective-permute-start | bytes 393224 | tf_op jit(solution)/shard_map/ppermute | solution.py:437
  2.4 6.9 %collective-permute-start.1 = (f32[2,16,1024]{2,1,0:T(8,128)S(1)}, f32[2,16,1024]{2,1,0:T(8,128)S(1)}, u32[]{:S(2)}, u32[]{:S(2)}) collective-permute-start(f32[2,16,1024]{2,1,0:T(8,128)S(1)} %get-tuple-element.19), channel_id=1, source_target_pairs={{0,1},{1,0},{2,4},{3,5},{4,2},{5,3},{6,8},{7,9},{8,6},{9,7},{10,12... | collective-permute-start | bytes 393224 | tf_op jit(solution)/shard_map/ppermute | solution.py:436
  5.0 4.4 %collective-permute-start.2 = (f32[2,8,1024]{2,1,0:T(8,128)S(1)}, f32[2,8,1024]{2,1,0:T(8,128)S(1)}, u32[]{:S(2)}, u32[]{:S(2)}) collective-permute-start(f32[2,8,1024]{2,1,0:T(8,128)S(1)} %get-tuple-element.20), channel_id=1, source_target_pairs={{0,1},{1,0},{2,3},{3,2},{4,5},{5,4},{6,7},{7,6},{8,9},{9,8},{10,11... | collective-permute-start | bytes 196616 | tf_op jit(solution)/shard_map/ppermute | solution.py:439
  11.5 5.3 %collective-permute-start.4 = (f32[24,1024]{1,0:T(8,128)S(1)}, f32[24,1024]{1,0:T(8,128)S(1)}, u32[]{:S(2)}, u32[]{:S(2)}) collective-permute-start(f32[24,1024]{1,0:T(8,128)S(1)} %get-tuple-element.24.to_odd_ref), channel_id=1, source_target_pairs={{0,1},{1,0},{2,4},{3,5},{4,2},{5,3},{6,8},{7,9},{8,6},{9,7},{10,12... | collective-permute-start | bytes 294920 | tf_op jit(solution)/shard_map/ppermute | solution.py:465
  13.6 3.2 %collective-permute-start.5 = (f32[24,1024]{1,0:T(8,128)S(1)}, f32[24,1024]{1,0:T(8,128)S(1)}, u32[]{:S(2)}, u32[]{:S(2)}) collective-permute-start(f32[24,1024]{1,0:T(8,128)S(1)} %get-tuple-element.25.to_even_ref), channel_id=1, source_target_pairs={{0,2},{1,3},{2,0},{3,1},{4,6},{5,7},{6,4},{7,5},{8,10},{9,11},{10,... | collective-permute-start | bytes 294920 | tf_op jit(solution)/shard_map/ppermute | solution.py:466
  13.6 7.0 %collective-permute-start.3 = (f32[5,8,1024]{2,1,0:T(8,128)S(1)}, f32[5,8,1024]{2,1,0:T(8,128)S(1)}, u32[]{:S(2)}, u32[]{:S(2)}) collective-permute-start(f32[5,8,1024]{2,1,0:T(8,128)S(1)} %get-tuple-element.22.sums_ref), channel_id=1, source_target_pairs={{0,1},{1,0},{2,3},{3,2},{4,5},{5,4},{6,7},{7,6},{8,9},{9,8},{10,11... | collective-permute-start | bytes 491528 | tf_op jit(solution)/shard_map/ppermute | solution.py:468
  17.0 4.8 %collective-permute-start.6 = (f32[2,8,1024]{2,1,0:T(8,128)S(1)}, f32[2,8,1024]{2,1,0:T(8,128)S(1)}, u32[]{:S(2)}, u32[]{:S(2)}) collective-permute-start(f32[2,8,1024]{2,1,0:T(8,128)S(1)} %edge.1.halo_ref), channel_id=1, source_target_pairs={{0,1},{1,0},{2,3},{3,2},{4,5},{5,4},{6,7},{7,6},{8,9},{9,8},{10,11... | collective-permute-start | bytes 196616 | tf_op jit(solution)/shard_map/ppermute | solution.py:480

commit v6 on v5

--- a/solution.py
+++ b/solution.py
@@ -14,6 +14,7 @@
 LOG2E = math.log2(math.e)
 LANES = 128
 PACK_COST = 4_000_000_000
+EDGE_COST = 1_000_000_000
 F32 = jnp.float32
 
 T_A, T_N, T_SK, T_D, T_R = range(5)
@@ -57,8 +58,11 @@
     return [(kinds & (1 << i)) != 0 for i in range((count - 1).bit_length())]
 
 
-def hydraulics(h, pa, pn, psk):
-    pc = (1.0 / pn - 1.0) * (0.25 * LOG2E)
+def power(pn):
+    return (1.0 / pn - 1.0) * (0.25 * LOG2E)
+
+
+def hydraulics(h, pa, pn, pc, psk):
     q = h * h + SMALL
     u = jnp.exp2(pn * (pa + (0.5 * LOG2E) * jnp.log(q)))
     one_plus = 1.0 + u
@@ -78,8 +82,8 @@
 def code_params(codes, tab_ref):
     kinds = jnp.maximum(codes.astype(jnp.int32) - 1, 0)
     bits = type_bits(kinds, tab_ref.shape[1])
-    pa, pn, psk = [pick(tab_ref, i, bits, codes.shape[1]) for i in (T_A, T_N, T_SK)]
-    return pa, pn, jnp.where(codes > 0.5, psk, 0.0)
+    pa, pn, psk, pd = [pick(tab_ref, i, bits, codes.shape[1]) for i in (T_A, T_N, T_SK, T_D)]
+    return pa, pn, power(pn), jnp.where(codes > 0.5, psk, 0.0), pd
 
 
 def even_area():
@@ -174,12 +178,14 @@
     layers, rows, width = p_ref.shape
     kind_count = tab_ref.shape[1]
 
-    def step(layer, carry):
-        sum_fixed, sum_rate = carry
+    sum_fixed = sum_rate = jnp.zeros((rows, width), F32)
+    held = None
+    for layer in range(layers):
         bits = type_bits(soil_ref[layer], kind_count)
         pa, pn, psk, pd, pr = [pick(tab_ref, i, bits, width) for i in range(5)]
+        pc, pcap = power(pn), pd * (pn - 1.0)
         h = p_ref[layer]
-        kap, sat, over = hydraulics(h, pa, pn, psk)
+        kap, sat, over = hydraulics(h, pa, pn, pc, psk)
         fixed = pr - INV_DT * theta_ref[layer] - source_ref[layer]
         k_l, k_r = from_left(kap), from_right(kap)
         k_u, k_d = from_above(kap, 0.0), from_below(kap, 0.0)
@@ -189,172 +195,212 @@
             + k_u * (pltpu.roll(h, 1, 0) - h)
             + k_d * (pltpu.roll(h, rows - 1, 0) - h)
         )
+        total = (k_l + k_r) + (k_u + k_d)
         kap_ref[layer] = kap
-        kept_ref[0, layer] = pd * sat + fixed - kap * inflow
-        kept_ref[1, layer] = pd * (pn - 1.0) * sat * over + kap * ((k_l + k_r) + (k_u + k_d))
-        kept_ref[2, layer] = pa
-        kept_ref[3, layer] = pn
-        kept_ref[4, layer] = psk
-        kept_ref[5, layer] = pd
-        return sum_fixed + fixed, sum_rate + jnp.exp2(pa)
-
-    zero = jnp.zeros((rows, width), F32)
-    sum_fixed, sum_rate = lax.fori_loop(0, layers, step, (zero, zero), unroll=True)
+        for i, field in enumerate((pa, pn, pc, psk, pd, pcap)):
+            kept_ref[2 + i, layer] = field
+        sum_fixed, sum_rate = sum_fixed + fixed, sum_rate + jnp.exp2(pa)
+        if held is not None:
+            o_h, o_kap, o_inflow, o_total, o_fixed, o_cap = held
+            inflow = inflow + o_kap * (o_h - h + 1.0)
+            total = total + o_kap
+            o_inflow = o_inflow + kap * (h - o_h - 1.0)
+            kept_ref[0, layer - 1] = o_fixed - o_kap * o_inflow
+            kept_ref[1, layer - 1] = o_cap + o_kap * (o_total + kap)
+        held = (h, kap, inflow, total, pd * sat + fixed, pcap * sat * over)
+    _, kap, inflow, total, fixed, cap = held
+    kept_ref[0, layers - 1] = fixed - kap * inflow
+    kept_ref[1, layers - 1] = cap + kap * total
     sums_ref[0] = sum_fixed
     sums_ref[1] = sum_rate
 
 
-def fine_kernel(swap, p_ref, kept_ref, kap_ref, local_ref, tab_ref, *rest):
+def rim_kernel(odd, from_ref, tab_ref, rim_ref):
+    live = paired()[odd]
+
+    def step(i, carry):
+        at = pl.ds(i * 8, 8)
+        fields = code_params(jnp.where(live, from_ref[1, at, :], 0.0), tab_ref)
+        for spot, field in enumerate(fields):
+            rim_ref[spot, at, :] = field
+        rim_ref[5, at, :] = hydraulics(from_ref[0, at, :], *fields[:4])[0]
+        return carry
+
+    lax.fori_loop(0, from_ref.shape[1] // 8, step, 0, unroll=True)
+
+
+def tail_spots(layers, width):
+    chunks = 2 * width // LANES
+    return [(j % layers, width + j // layers * LANES) for j in range(chunks)]
+
+
+def sent_width(layers, width):
+    return width + pl.cdiv(2 * width // LANES, layers) * LANES
+
+
+def fine_kernel(
+    swap,
+    p_ref,
+    kept_ref,
+    kap_ref,
+    local_ref,
+    tab_ref,
+    from_even_ref,
+    from_odd_ref,
+    rim_even_ref,
+    rim_odd_ref,
+    *rest,
+):
     layers, rows, width = p_ref.shape
-    left = iter(rest)
-    from_even_ref = next(left)
-    from_odd_ref = next(left)
-    vert_refs = [next(left) for _ in range(1 if swap else 2)]
-    smooth_ref, sums_ref, to_even_ref, to_odd_ref, rim_ref, side_ref = left
+    verts = 1 if swap else 2
+    vert_refs = rest[:verts]
+    smooth_ref, sums_ref, to_even_ref, to_odd_ref, mine_ref, side_ref, edge_ref = rest[verts:]
     even = even_area()
     spot = row_iota((rows, width))
     is_first, is_last = spot == 0, spot == rows - 1
 
+    for i, by_even, by_odd in (
+        (0, rim_even_ref[5], rim_odd_ref[5]),
+        (2, from_even_ref[0], from_odd_ref[0]),
+    ):
+        side_ref[i] = jnp.where(even, by_odd, by_even)
+        side_ref[i + 1] = jnp.where(even, by_even, by_odd)
+    vert = [(ref[0], hydraulics(ref[0], *code_params(ref[1], tab_ref)[:4])[0]) for ref in vert_refs]
     if swap:
         at_top = lax.axis_index("depth") == 0
-        (vert_ref,) = vert_refs
-        top_h = bottom_h = vert_ref[0]
-        vert_k = hydraulics(top_h, *code_params(vert_ref[1], tab_ref))[0]
+        ((vert_h, vert_k),) = vert
+        top_h = bottom_h = vert_h
         top_k = jnp.where(at_top, 0.0, vert_k)
         bottom_k = jnp.where(at_top, vert_k, 0.0)
     else:
-        top_ref, bottom_ref = vert_refs
-        top_h, bottom_h = top_ref[0], bottom_ref[0]
-        top_k = hydraulics(top_h, *code_params(top_ref[1], tab_ref))[0]
-        bottom_k = hydraulics(bottom_h, *code_params(bottom_ref[1], tab_ref))[0]
-    def side_step(i, carry):
-        at = pl.ds(i * 8, 8)
-        for side, (from_ref, live) in enumerate(zip((from_even_ref, from_odd_ref), paired())):
-            fields = code_params(jnp.where(live, from_ref[1, at, :], 0.0), tab_ref)
-            for spot, field in enumerate(fields):
-                rim_ref[side, spot, at, :] = field
-            side_ref[side, at, :] = hydraulics(from_ref[0, at, :], *fields)[0]
-        return carry
-
-    lax.fori_loop(0, layers // 8, side_step, 0)
-
-    def step(layer, carry):
-        sum_kh, sum_k, sum_cap, sum_sat, flux_x, flux_y = carry
+        (top_h, top_k), (bottom_h, bottom_k) = vert
+
+    sum_kh = sum_k = sum_cap = sum_sat = flux_x = flux_y = jnp.zeros((rows, width), F32)
+    for layer in range(layers):
         h = p_ref[layer]
-        above, below = jnp.maximum(layer - 1, 0), jnp.minimum(layer + 1, layers - 1)
-        k_u = jnp.where(layer == 0, top_k, kap_ref[above])
-        h_u = jnp.where(layer == 0, top_h, p_ref[above])
-        k_d = jnp.where(layer == layers - 1, bottom_k, kap_ref[below])
-        h_d = jnp.where(layer == layers - 1, bottom_h, p_ref[below])
-        even_k = side_ref[0, pl.ds(layer, 1), :]
-        odd_k = side_ref[1, pl.ds(layer, 1), :]
-        even_h = from_even_ref[0, pl.ds(layer, 1), :]
-        odd_h = from_odd_ref[0, pl.ds(layer, 1), :]
-        lo_k = jnp.where(even, odd_k, even_k)
-        hi_k = jnp.where(even, even_k, odd_k)
-        lo_h = jnp.where(even, odd_h, even_h)
-        hi_h = jnp.where(even, even_h, odd_h)
-        side_k = jnp.where(is_first, lo_k, jnp.where(is_last, hi_k, 0.0))
-        side_h = jnp.where(is_first, lo_h, hi_h)
         kap = kap_ref[layer]
-        inflow = k_u * (h_u - h + 1.0) + k_d * (h_d - h - 1.0) + side_k * (side_h - h)
+        lo_k, hi_k, lo_h, hi_h = [side_ref[i, layer : layer + 1, :] for i in range(4)]
+        total = jnp.where(is_first, lo_k, jnp.where(is_last, hi_k, 0.0))
+        inflow = total * (jnp.where(is_first, lo_h, hi_h) - h)
+        if layer == 0:
+            inflow, total = inflow + top_k * (top_h - h + 1.0), total + top_k
+        if layer == layers - 1:
+            inflow, total = inflow + bottom_k * (bottom_h - h - 1.0), total + bottom_k
         balance = kept_ref[0, layer] - kap * inflow
-        diagonal = kept_ref[1, layer] + kap * (k_u + k_d + side_k)
+        diagonal = kept_ref[1, layer] + kap * total
         h = h - RELAX * balance / diagonal
         smooth_ref[layer] = h
 
-        pn = kept_ref[3, layer]
-        pd = kept_ref[5, layer]
-        kap, sat, over = hydraulics(h, kept_ref[2, layer], pn, kept_ref[4, layer])
+        pa, pn, pc, psk, pd, pcap = [kept_ref[2 + i, layer] for i in range(6)]
+        kap, sat, over = hydraulics(h, pa, pn, pc, psk)
         cond = kap * kap
         flux_x = flux_x + kap * from_below(kap, 0.0) * (pltpu.roll(h, rows - 1, 0) - h)
         flux_y = flux_y + kap * from_right(kap) * (pltpu.roll(h, width - 1, 1) - h)
-        for even_at, odd_at, value in (
-            (to_even_ref, to_odd_ref, h),
-            (rim_ref.at[0, 3], rim_ref.at[1, 3], kap),
-        ):
-            low, high = value[0:1, :], value[rows - 1 : rows, :]
-            even_at[pl.ds(layer, 1), :] = jnp.where(even, high, low)
-            odd_at[pl.ds(layer, 1), :] = jnp.where(even, low, high)
-        return (
-            sum_kh + cond * h,
-            sum_k + cond,
-            sum_cap + pd * (pn - 1.0) * sat * over,
-            sum_sat + pd * sat,
-            flux_x,
-            flux_y,
-        )
-
-    zero = jnp.zeros((rows, width), F32)
-    sum_kh, sum_k, sum_cap, sum_sat, flux_x, flux_y = lax.fori_loop(
-        0, layers, step, (zero,) * 6, unroll=True
-    )
-    sum_rate = local_ref[1]
+        for i, value in enumerate((h, kap)):
+            edge_ref[2 * i, layer : layer + 1, :] = value[0:1, :]
+            edge_ref[2 * i + 1, layer : layer + 1, :] = value[rows - 1 : rows, :]
+        sum_kh = sum_kh + cond * h
+        sum_k = sum_k + cond
+        sum_cap = sum_cap + pcap * sat * over
+        sum_sat = sum_sat + pd * sat
+
     restricted = (
         (flux_x - from_above(flux_x, 0.0)) + (flux_y - from_left(flux_y)) - sum_sat - local_ref[0]
     )
-    for at, value in enumerate((sum_kh, sum_k, sum_cap, restricted, sum_rate)):
+    for at, value in enumerate((sum_kh, sum_k, sum_cap, restricted, local_ref[1])):
         sums_ref[at] = value
-    at = layers
-    tails = []
-    for edge, inner in ((rows - 1, rows - 2), (0, 1)):
-        tail = [
-            sum_kh[edge : edge + 1],
-            sum_k[edge : edge + 1],
-            sum_kh[inner : inner + 1],
-            sum_k[inner : inner + 1],
-            sum_cap[edge : edge + 1],
-            restricted[edge : edge + 1],
-            sum_rate[edge : edge + 1],
-            zero[0:1],
-        ]
-        tails.append(jnp.concatenate(tail, axis=0))
-    high, low = tails
-    to_even_ref[at : at + 8, :] = jnp.where(even, high, low)
-    to_odd_ref[at : at + 8, :] = jnp.where(even, low, high)
-
-
-def edge_kernel(rim_ref, to_odd_ref, to_even_ref, from_odd_ref, from_even_ref, halo_ref):
-    layers = rim_ref.shape[2]
-    at = layers
-    for side, (mine_ref, their_ref, live) in enumerate(
-        zip((to_even_ref, to_odd_ref), (from_even_ref, from_odd_ref), paired())
+    low_h, high_h, low_k, high_k = [edge_ref[i] for i in range(4)]
+    to_even_ref[:, 0:width] = jnp.where(even, high_h, low_h)
+    to_odd_ref[:, 0:width] = jnp.where(even, low_h, high_h)
+    mine_ref[0] = jnp.where(even, high_k, low_k)
+    mine_ref[1] = jnp.where(even, low_k, high_k)
+    low_tail = jnp.concatenate([restricted[0:1], sum_k[1:2]], axis=1)
+    high_tail = jnp.concatenate([restricted[rows - 1 : rows], sum_k[rows - 2 : rows - 1]], axis=1)
+    for out_ref, tail in (
+        (to_even_ref, jnp.where(even, high_tail, low_tail)),
+        (to_odd_ref, jnp.where(even, low_tail, high_tail)),
     ):
-        theirs = their_ref[0:layers, :]
-        kap = hydraulics(theirs, rim_ref[side, 0], rim_ref[side, 1], rim_ref[side, 2])[0]
-        flux = rim_ref[side, 3] * kap * (theirs - mine_ref[0:layers, :])
-        flux = jnp.sum(flux, axis=0, keepdims=True)
-        block = jnp.where(live, their_ref[at : at + 8, :], 0.0)
-        spot = row_iota(block.shape)
-        block = jnp.where(spot == 5, block - flux, block)
-        halo_ref[side] = jnp.where(spot == 7, flux, block)
+        for j, (row, lane) in enumerate(tail_spots(layers, width)):
+            out_ref[row : row + 1, lane : lane + LANES] = tail[:, j * LANES : (j + 1) * LANES]
+
+
+def edge_kernel(
+    rim_odd_ref,
+    rim_even_ref,
+    mine_ref,
+    to_odd_ref,
+    to_even_ref,
+    from_odd_ref,
+    from_even_ref,
+    halo_ref,
+):
+    _, layers, width = rim_odd_ref.shape
+    sides = (
+        (rim_even_ref, to_even_ref, from_even_ref),
+        (rim_odd_ref, to_odd_ref, from_odd_ref),
+    )
+    for side, (live, (rim_ref, to_ref, from_ref)) in enumerate(zip(paired(), sides)):
+        pa, pn, pc, psk, pd = [rim_ref[i] for i in range(5)]
+        theirs = from_ref[:, 0:width]
+        kap, sat, over = hydraulics(theirs, pa, pn, pc, psk)
+        cond = kap * kap
+        tail = jnp.concatenate(
+            [
+                from_ref[row : row + 1, lane : lane + LANES]
+                for row, lane in tail_spots(layers, width)
+            ],
+            axis=1,
+        )
+
+        def total(x):
+            return jnp.sum(x, axis=0, keepdims=True)
+
+        flux = total(mine_ref[side] * kap * (theirs - to_ref[:, 0:width]))
+        block = jnp.concatenate(
+            [
+                total(cond * theirs),
+                total(cond),
+                total(pd * (pn - 1.0) * sat * over),
+                tail[:, 0:width] - flux,
+                tail[:, width:],
+                total(jnp.exp2(pa)),
+                flux,
+                jnp.zeros_like(flux),
+            ],
+            axis=0,
+        )
+        halo_ref[side] = jnp.where(live, block, 0.0)
+
+
+def columns_kernel(sums_ref, their_sums_ref, columns_ref):
+    kh, kk, cap, rest, rate = [sums_ref[i] + their_sums_ref[i] for i in range(5)]
+    for i, value in enumerate((kh / kk, jnp.sqrt(kk), cap, rest, rate)):
+        columns_ref[i] = value
 
 
 def coarse_kernel(
-    depth_total, smooth_ref, sums_ref, their_sums_ref, halo_ref, their_halo_ref, out_ref, head_ref
+    depth_total, smooth_ref, columns_ref, halo_ref, their_halo_ref, out_ref, head_ref
 ):
     rows = smooth_ref.shape[1]
-    kh, kk, cap, rest, rate = [sums_ref[i] + their_sums_ref[i] for i in range(5)]
+    base, root, cap, rest, rate = [columns_ref[i] for i in range(5)]
     by_even = halo_ref[0] + their_halo_ref[0]
     by_odd = halo_ref[1] + their_halo_ref[1]
     even = even_area()
     lo = jnp.where(even, by_odd, by_even)
     hi = jnp.where(even, by_even, by_odd)
     spot = row_iota(rest.shape)
-    rest = jnp.where(spot == 0, rest + lo[7:8], rest)
-    rest = jnp.where(spot == rows - 1, rest + hi[7:8], rest)
+    rest = jnp.where(spot == 0, rest + lo[6:7], rest)
+    rest = jnp.where(spot == rows - 1, rest + hi[6:7], rest)
 
     def pair(i):
         return jnp.where(spot == 0, lo[i : i + 1], jnp.where(spot == rows - 1, hi[i : i + 1], 0.0))
 
-    h_kh, h_k, o_kh, o_k, h_cap, h_rest, h_rate = [pair(i) for i in range(7)]
+    h_kh, h_k, h_cap, h_rest, o_k, h_rate = [pair(i) for i in range(6)]
     edge_lane = lane_iota(rest.shape)
 
     def sides(x):
         return from_left(x) + from_right(x)
 
-    base = kh / kk
-    root = jnp.sqrt(kk)
     h_live = h_k > 0.0
     h_base = jnp.where(h_live, h_kh / jnp.where(h_live, h_k, 1.0), 0.0)
     h_root = jnp.sqrt(h_k)
@@ -441,27 +487,39 @@
         vert = [lax.ppermute(packed[3], "depth", down), lax.ppermute(packed[4], "depth", up)]
     kept, kap, local_sums = pl.pallas_call(
         local_kernel,
-        out_shape=[shape(6, layers, rows, width), shape(layers, rows, width), shape(2, rows, width)],
+        out_shape=[shape(8, layers, rows, width), shape(layers, rows, width), shape(2, rows, width)],
         in_specs=whole(5),
         out_specs=whole(3),
         compiler_params=params,
         name="local",
     )(pressure, theta_old, source, soil_type, packed[0])
-    smooth, sums, to_even, to_odd, rim = pl.pallas_call(
+    rims = [
+        pl.pallas_call(
+            functools.partial(rim_kernel, odd),
+            out_shape=shape(6, layers, width),
+            in_specs=whole(2),
+            out_specs=whole(1)[0],
+            compiler_params=params,
+            name="rim",
+        )(from_area, packed[0])
+        for odd, from_area in enumerate((from_even, from_odd))
+    ]
+    sent = shape(layers, sent_width(layers, width))
+    smooth, sums, to_even, to_odd, mine = pl.pallas_call(
         functools.partial(fine_kernel, swap),
         out_shape=[
             shape(layers, rows, width),
             shape(5, rows, width),
-            shape(layers + 8, width),
-            shape(layers + 8, width),
-            shape(2, 4, layers, width),
+            sent,
+            sent,
+            shape(2, layers, width),
         ],
-        in_specs=whole(7 + verts),
+        in_specs=whole(9 + verts),
         out_specs=whole(5),
-        scratch_shapes=[pltpu.VMEM((2, layers, width), F32)],
+        scratch_shapes=[pltpu.VMEM((4, layers, width), F32)] * 2,
         compiler_params=params,
         name="fine",
-    )(pressure, kept, kap, local_sums, packed[0], from_even, from_odd, *vert)
+    )(pressure, kept, kap, local_sums, packed[0], from_even, from_odd, *rims, *vert)
     from_odd = lax.ppermute(to_odd, both, odd_moves)
     from_even = lax.ppermute(to_even, both, even_moves)
     if swap:
@@ -471,23 +529,32 @@
     halo = pl.pallas_call(
         edge_kernel,
         out_shape=shape(2, 8, width),
-        in_specs=whole(5),
+        in_specs=whole(7),
         out_specs=whole(1)[0],
+        cost_estimate=pl.CostEstimate(flops=EDGE_COST, transcendentals=0, bytes_accessed=0),
         compiler_params=params,
         name="edge",
-    )(rim, to_odd, to_even, from_odd, from_even)
+    )(rims[1], rims[0], mine, to_odd, to_even, from_odd, from_even)
     if swap:
         their_halo = lax.ppermute(halo, "depth", swapped)
     else:
         halo, their_halo = lax.psum(halo, "depth"), jnp.zeros_like(halo)
+    columns = pl.pallas_call(
+        columns_kernel,
+        out_shape=shape(5, rows, width),
+        in_specs=whole(2),
+        out_specs=whole(1)[0],
+        compiler_params=params,
+        name="columns",
+    )(sums, their_sums)
     out, head = pl.pallas_call(
         functools.partial(coarse_kernel, layers * depths),
         out_shape=[shape(layers, rows, width), shape(rows, width)],
-        in_specs=whole(5),
+        in_specs=whole(4),
         out_specs=whole(2),
         compiler_params=params,
         name="coarse",
-    )(smooth, sums, their_sums, halo, their_halo)
+    )(smooth, columns, halo, their_halo)
     return out, head
 
 

time: 23 us -> 22.1 us (0.961)
  waiting for transfers between devices: 6.47 us -> 4.4 us
  starting transfers between devices: 8.44 us -> 9.46 us
    ppermute x1, waiting for transfers between devices: 1.68 us -> 0.01 us  [shards(): vert = [lax.ppermute(packed[3], 'depth', swapped)]]
    ppermute x1, starting transfers between devices: 0.08 us -> 1.49 us  [shards(): vert = [lax.ppermute(packed[3], 'depth', swapped)]]
    ppermute x1, waiting for transfers between devices: 1.07 us -> 2.26 us  [shards(): their_sums = lax.ppermute(sums, 'depth', swapped)]
    ppermute x1, waiting for transfers between devices: 2.54 us -> 1.35 us  [shards(): from_odd = lax.ppermute(to_odd, both, odd_moves)]
    ppermute x1, starting transfers between devices: 2.55 us -> 1.76 us  [shards(): their_halo = lax.ppermute(halo, 'depth', swapped)]
    ppermute x1, starting transfers between devices: 0.65 us -> 1.37 us  [shards(): their_sums = lax.ppermute(sums, 'depth', swapped)]
    pallas_call x1, Pallas kernels: 2.18 us -> 1.51 us  [shards(): pl.pallas_call(functools.partial(fine_kernel, swap), out_shape=[shape(lay...]
    pallas_call x1 -> x4, Pallas kernels: 2.58 us -> 3.24 us  [the longest x1 2.76 us: shards(): pl.pallas_call(local_kernel, out_shape=[shape(8, layers, rows, width), sh...]
  transfers between devices with their start and end apart: 7 -> 7, of which waited for: 4 -> 3; matrix products, arithmetic and copies ran while one was open for 0% -> 0% of each run, Pallas kernels for 12% -> 16%
where the time goes in v6:
time: 22.1 us; the launch traced here: 21.9 us
  starting transfers between devices  9.46 us (43%)
  Pallas kernels  7.31 us (33%)
  waiting for transfers between devices  4.4 us (20%)
  between operations  0.74 us (3%)
    ppermute x1, starting transfers between devices, shards(): from_odd = lax.ppermute(packed[2], both, odd_moves)  3 us
    pallas_call x1, Pallas kernels, shards(): pl.pallas_call(local_kernel, out_shape=[shape(8, layers, rows, width), sh...  2.76 us
    ppermute x1, waiting for transfers between devices, shards(): their_sums = lax.ppermute(sums, 'depth', swapped)  2.26 us
    ppermute x1, starting transfers between devices, shards(): their_halo = lax.ppermute(halo, 'depth', swapped)  1.76 us
    pallas_call x1, Pallas kernels, shards(): pl.pallas_call(functools.partial(fine_kernel, swap), out_shape=[shape(lay...  1.51 us
    ppermute x1, starting transfers between devices, shards(): from_odd = lax.ppermute(to_odd, both, odd_moves)  1.5 us
    ppermute x1, starting transfers between devices, shards(): vert = [lax.ppermute(packed[3], 'depth', swapped)]  1.49 us
    ppermute x1, starting transfers between devices, shards(): their_sums = lax.ppermute(sums, 'depth', swapped)  1.37 us
  transfers between devices with their start and end apart: 7, of which 3 were waited for; matrix products, arithmetic and copies ran while one was open for 0% of the time, Pallas kernels for 16%

profile of v6, /device:TPU:0, one launch (start us, length us, event | category | flops | bytes accessed | tf_op | source)
XLA Modules:
  0.0 21.9 jit_solution(17850503248720660555)
XLA Ops:
  0.6 0.0 copy-start
  0.6 0.0 copy-start.3
  0.7 0.0 copy-start.2
  0.7 0.0 copy-start.1
  0.7 1.2 %pack.1 = (f32[5,12,8,128]{3,2,1,0:T(8,128)S(1)}, f32[2,16,1024]{2,1,0:T(8,128)S(1)}, f32[2,16,1024]{2,1,0:T(8,128)S(1)}, f32[2,8,1024]{2,1,0:T(8,128)S(1)}) custom-call(f32[16,8,1024]{2,1,0:T(8,128)} %p_ref.5, s32[16,8,1024]{2,1,0:T(8,128)} %soil_ref.3, f32[5,12]{1,0:T(8,128)} %params_ref.1), custom_call_target="tpu_custom_call" | custom-call | flops 4000000000 | tf_op jit(solution)/shard_map/pack/pallas_call | solution.py:463
  1.9 3.0 %collective-permute-start.1 = (f32[2,16,1024]{2,1,0:T(8,128)S(1)}, f32[2,16,1024]{2,1,0:T(8,128)S(1)}, u32[]{:S(2)}, u32[]{:S(2)}) collective-permute-start(f32[2,16,1024]{2,1,0:T(8,128)S(1)} %get-tuple-element.19), channel_id=1, source_target_pairs={{0,1},{1,0},{2,4},{3,5},{4,2},{5,3},{6,8},{7,9},{8,6},{9,7},{10,12... | collective-permute-start | bytes 393224 | tf_op jit(solution)/shard_map/ppermute | solution.py:482
  4.9 0.1 collective-permute-start
  5.1 1.5 %collective-permute-start.2 = (f32[2,8,1024]{2,1,0:T(8,128)S(1)}, f32[2,8,1024]{2,1,0:T(8,128)S(1)}, u32[]{:S(2)}, u32[]{:S(2)}) collective-permute-start(f32[2,8,1024]{2,1,0:T(8,128)S(1)} %get-tuple-element.20), channel_id=1, source_target_pairs={{0,1},{1,0},{2,3},{3,2},{4,5},{5,4},{6,7},{7,6},{8,9},{9,8},{10,11... | collective-permute-start | bytes 196616 | tf_op jit(solution)/shard_map/ppermute | solution.py:485
  6.5 0.0 copy-done
  6.5 0.0 copy-done.3
  6.5 0.0 copy-done.2
  6.6 0.0 copy-done.1
  6.6 2.8 %local.1 = (f32[8,16,8,1024]{3,2,1,0:T(8,128)S(1)}, f32[16,8,1024]{2,1,0:T(8,128)S(1)}, f32[2,8,1024]{2,1,0:T(8,128)S(1)}) custom-call(f32[16,8,1024]{2,1,0:T(8,128)S(1)} %copy-done, f32[16,8,1024]{2,1,0:T(8,128)S(1)} %copy-done.1, f32[16,8,1024]{2,1,0:T(8,128)S(1)} %copy-done.2, s32[16,8,1024]{2,1,0:T(8,128)S(1)} %copy-done.3, ...), custom_call_target="tpu_custom_call" | custom-call | tf_op jit(solution)/shard_map/local/pallas_call | solution.py:488
  9.3 0.0 collective-permute-done.1.from_ref.from_odd_ref
  9.3 0.2 %rim.3.rim_odd_ref = f32[6,16,1024]{2,1,0:T(8,128)S(1)} custom-call(f32[2,16,1024]{2,1,0:T(8,128)S(1)} %collective-permute-done.1.from_ref.from_odd_ref, f32[5,12,8,128]{3,2,1,0:T(8,128)S(1)} %get-tuple-element.14.tab_ref), custom_call_target="tpu_custom_call" | custom-call | tf_op jit(solution)/shard_map/rim/pallas_call | solution.py:497
  9.6 0.0 collective-permute-done.from_ref.from_even_ref
  9.6 0.2 %rim.2.rim_even_ref = f32[6,16,1024]{2,1,0:T(8,128)S(1)} custom-call(f32[2,16,1024]{2,1,0:T(8,128)S(1)} %collective-permute-done.from_ref.from_even_ref, f32[5,12,8,128]{3,2,1,0:T(8,128)S(1)} %get-tuple-element.14.tab_ref), custom_call_target="tpu_custom_call" | custom-call | tf_op jit(solution)/shard_map/rim/pallas_call | solution.py:497
  9.8 0.0 collective-permute-done.2.rest_0_
  9.8 1.5 %fine.1 = (f32[16,8,1024]{2,1,0:T(8,128)S(1)}, f32[5,8,1024]{2,1,0:T(8,128)S(1)}, f32[16,1152]{1,0:T(8,128)S(1)}, f32[16,1152]{1,0:T(8,128)S(1)}, f32[2,16,1024]{2,1,0:T(8,128)S(1)}) custom-call(f32[16,8,1024]{2,1,0:T(8,128)S(1)} %copy-done, f32[8,16,8,1024]{3,2,1,0:T(8,128)S(1)} %get-tuple-element.15.kept_ref, ...), custom_call_target="tpu_custom_call" | custom-call | tf_op jit(solution)/shard_map/fine/pallas_call | solution.py:508
  11.3 1.5 %collective-permute-start.4 = (f32[16,1152]{1,0:T(8,128)S(1)}, f32[16,1152]{1,0:T(8,128)S(1)}, u32[]{:S(2)}, u32[]{:S(2)}) collective-permute-start(f32[16,1152]{1,0:T(8,128)S(1)} %get-tuple-element.24.to_odd_ref), channel_id=1, source_target_pairs={{0,1},{1,0},{2,4},{3,5},{4,2},{5,3},{6,8},{7,9},{8,6},{9,7},{10,12... | collective-permute-start | bytes 221192 | tf_op jit(solution)/shard_map/ppermute | solution.py:523
  12.8 0.2 collective-permute-start.5
  13.0 1.4 %collective-permute-start.3 = (f32[5,8,1024]{2,1,0:T(8,128)S(1)}, f32[5,8,1024]{2,1,0:T(8,128)S(1)}, u32[]{:S(2)}, u32[]{:S(2)}) collective-permute-start(f32[5,8,1024]{2,1,0:T(8,128)S(1)} %get-tuple-element.22.sums_ref), channel_id=1, source_target_pairs={{0,1},{1,0},{2,3},{3,2},{4,5},{5,4},{6,7},{7,6},{8,9},{9,8},{10,11... | collective-permute-start | bytes 491528 | tf_op jit(solution)/shard_map/ppermute | solution.py:526
  14.4 1.4 %collective-permute-done.4.from_odd_ref = f32[16,1152]{1,0:T(8,128)S(1)} collective-permute-done((f32[16,1152]{1,0:T(8,128)S(1)}, f32[16,1152]{1,0:T(8,128)S(1)}, u32[]{:S(2)}, u32[]{:S(2)}) %collective-permute-start.4) | collective-permute-done | bytes 73760 | tf_op jit(solution)/shard_map/ppermute | solution.py:523
  15.8 0.0 collective-permute-done.5.from_even_ref
  15.8 0.3 %edge.1.halo_ref = f32[2,8,1024]{2,1,0:T(8,128)S(1)} custom-call(f32[6,16,1024]{2,1,0:T(8,128)S(1)} %rim.3.rim_odd_ref, f32[6,16,1024]{2,1,0:T(8,128)S(1)} %rim.2.rim_even_ref, f32[2,16,1024]{2,1,0:T(8,128)S(1)} %get-tuple-element.23.mine_ref, f32[16,1152]{1,0:T(8,128)S(1)} %get-tuple-element.24.to_odd_ref, f32[16,1152]{1,0:T(8,128)S(1)} %get-tuple-element.25.to_even_ref, ...), custom_call_target="tpu_custom_call" | custom-call | flops 1000000000 | tf_op jit(solution)/shard_map/edge/pallas_call | solution.py:529
  16.1 1.8 %collective-permute-start.6 = (f32[2,8,1024]{2,1,0:T(8,128)S(1)}, f32[2,8,1024]{2,1,0:T(8,128)S(1)}, u32[]{:S(2)}, u32[]{:S(2)}) collective-permute-start(f32[2,8,1024]{2,1,0:T(8,128)S(1)} %edge.1.halo_ref), channel_id=1, source_target_pairs={{0,1},{1,0},{2,3},{3,2},{4,5},{5,4},{6,7},{7,6},{8,9},{9,8},{10,11... | collective-permute-start | bytes 196616 | tf_op jit(solution)/shard_map/ppermute | solution.py:539
  17.8 2.3 %collective-permute-done.3.their_sums_ref = f32[5,8,1024]{2,1,0:T(8,128)S(1)} collective-permute-done((f32[5,8,1024]{2,1,0:T(8,128)S(1)}, f32[5,8,1024]{2,1,0:T(8,128)S(1)}, u32[]{:S(2)}, u32[]{:S(2)}) %collective-permute-start.3) | collective-permute-done | bytes 163872 | tf_op jit(solution)/shard_map/ppermute | solution.py:526
  20.1 0.8 %collective-permute-done.6.their_halo_ref = f32[2,8,1024]{2,1,0:T(8,128)S(1)} collective-permute-done((f32[2,8,1024]{2,1,0:T(8,128)S(1)}, f32[2,8,1024]{2,1,0:T(8,128)S(1)}, u32[]{:S(2)}, u32[]{:S(2)}) %collective-permute-start.6) | collective-permute-done | bytes 65568 | tf_op jit(solution)/shard_map/ppermute | solution.py:539
  20.9 1.1 %coarse.1 = (f32[16,8,1024]{2,1,0:T(8,128)}, f32[8,1024]{1,0:T(8,128)}) custom-call(f32[16,8,1024]{2,1,0:T(8,128)S(1)} %get-tuple-element.21.smooth_ref, f32[5,8,1024]{2,1,0:T(8,128)S(1)} %columns.1.columns_ref, f32[2,8,1024]{2,1,0:T(8,128)S(1)} %edge.1.halo_ref, f32[2,8,1024]{2,1,0:T(8,128)S(1)} %collective-permute-done.6.their_halo_ref), custom_call_target="tpu_custom_call" | custom-call | tf_op jit(solution)/shard_map/coarse/pallas_call | solution.py:550
  (1 shorter events, 0.0 us)
Async XLA Ops:
  0.6 5.9 %copy-start = (f32[16,8,1024]{2,1,0:T(8,128)S(1)}, f32[16,8,1024]{2,1,0:T(8,128)}, u32[]{:S(2)}) copy-start(f32[16,8,1024]{2,1,0:T(8,128)} %p_ref.5) | copy-start | bytes 1572868
  0.6 5.9 %copy-start.3 = (s32[16,8,1024]{2,1,0:T(8,128)S(1)}, s32[16,8,1024]{2,1,0:T(8,128)}, u32[]{:S(2)}) copy-start(s32[16,8,1024]{2,1,0:T(8,128)} %soil_ref.3) | copy-start | bytes 1572868
  0.7 5.9 %copy-start.2 = (f32[16,8,1024]{2,1,0:T(8,128)S(1)}, f32[16,8,1024]{2,1,0:T(8,128)}, u32[]{:S(2)}) copy-start(f32[16,8,1024]{2,1,0:T(8,128)} %source_ref.1) | copy-start | bytes 1572868
  0.7 5.9 %copy-start.1 = (f32[16,8,1024]{2,1,0:T(8,128)S(1)}, f32[16,8,1024]{2,1,0:T(8,128)}, u32[]{:S(2)}) copy-start(f32[16,8,1024]{2,1,0:T(8,128)} %theta_ref.1) | copy-start | bytes 1572868
  1.9 7.4 %collective-permute-start.1 = (f32[2,16,1024]{2,1,0:T(8,128)S(1)}, f32[2,16,1024]{2,1,0:T(8,128)S(1)}, u32[]{:S(2)}, u32[]{:S(2)}) collective-permute-start(f32[2,16,1024]{2,1,0:T(8,128)S(1)} %get-tuple-element.19), channel_id=1, source_target_pairs={{0,1},{1,0},{2,4},{3,5},{4,2},{5,3},{6,8},{7,9},{8,6},{9,7},{10,12... | collective-permute-start | bytes 393224 | tf_op jit(solution)/shard_map/ppermute | solution.py:482
  4.9 4.7 %collective-permute-start = (f32[2,16,1024]{2,1,0:T(8,128)S(1)}, f32[2,16,1024]{2,1,0:T(8,128)S(1)}, u32[]{:S(2)}, u32[]{:S(2)}) collective-permute-start(f32[2,16,1024]{2,1,0:T(8,128)S(1)} %get-tuple-element.18), channel_id=1, source_target_pairs={{0,2},{1,3},{2,0},{3,1},{4,6},{5,7},{6,4},{7,5},{8,10},{9,11},{10,... | collective-permute-start | bytes 393224 | tf_op jit(solution)/shard_map/ppermute | solution.py:483
  5.1 4.8 %collective-permute-start.2 = (f32[2,8,1024]{2,1,0:T(8,128)S(1)}, f32[2,8,1024]{2,1,0:T(8,128)S(1)}, u32[]{:S(2)}, u32[]{:S(2)}) collective-permute-start(f32[2,8,1024]{2,1,0:T(8,128)S(1)} %get-tuple-element.20), channel_id=1, source_target_pairs={{0,1},{1,0},{2,3},{3,2},{4,5},{5,4},{6,7},{7,6},{8,9},{9,8},{10,11... | collective-permute-start | bytes 196616 | tf_op jit(solution)/shard_map/ppermute | solution.py:485
  11.3 4.4 %collective-permute-start.4 = (f32[16,1152]{1,0:T(8,128)S(1)}, f32[16,1152]{1,0:T(8,128)S(1)}, u32[]{:S(2)}, u32[]{:S(2)}) collective-permute-start(f32[16,1152]{1,0:T(8,128)S(1)} %get-tuple-element.24.to_odd_ref), channel_id=1, source_target_pairs={{0,1},{1,0},{2,4},{3,5},{4,2},{5,3},{6,8},{7,9},{8,6},{9,7},{10,12... | collective-permute-start | bytes 221192 | tf_op jit(solution)/shard_map/ppermute | solution.py:523
  12.8 2.9 %collective-permute-start.5 = (f32[16,1152]{1,0:T(8,128)S(1)}, f32[16,1152]{1,0:T(8,128)S(1)}, u32[]{:S(2)}, u32[]{:S(2)}) collective-permute-start(f32[16,1152]{1,0:T(8,128)S(1)} %get-tuple-element.25.to_even_ref), channel_id=1, source_target_pairs={{0,2},{1,3},{2,0},{3,1},{4,6},{5,7},{6,4},{7,5},{8,10},{9,11},{10,... | collective-permute-start | bytes 221192 | tf_op jit(solution)/shard_map/ppermute | solution.py:524
  13.0 7.0 %collective-permute-start.3 = (f32[5,8,1024]{2,1,0:T(8,128)S(1)}, f32[5,8,1024]{2,1,0:T(8,128)S(1)}, u32[]{:S(2)}, u32[]{:S(2)}) collective-permute-start(f32[5,8,1024]{2,1,0:T(8,128)S(1)} %get-tuple-element.22.sums_ref), channel_id=1, source_target_pairs={{0,1},{1,0},{2,3},{3,2},{4,5},{5,4},{6,7},{7,6},{8,9},{9,8},{10,11... | collective-permute-start | bytes 491528 | tf_op jit(solution)/shard_map/ppermute | solution.py:526
  16.1 4.8 %collective-permute-start.6 = (f32[2,8,1024]{2,1,0:T(8,128)S(1)}, f32[2,8,1024]{2,1,0:T(8,128)S(1)}, u32[]{:S(2)}, u32[]{:S(2)}) collective-permute-start(f32[2,8,1024]{2,1,0:T(8,128)S(1)} %edge.1.halo_ref), channel_id=1, source_target_pairs={{0,1},{1,0},{2,3},{3,2},{4,5},{5,4},{6,7},{7,6},{8,9},{9,8},{10,11... | collective-permute-start | bytes 196616 | tf_op jit(solution)/shard_map/ppermute | solution.py:539

commit v7 on v6

--- a/solution.py
+++ b/solution.py
@@ -14,10 +14,11 @@
 LOG2E = math.log2(math.e)
 LANES = 128
 PACK_COST = 4_000_000_000
-EDGE_COST = 1_000_000_000
+EDGE_COST = 1000_000_000
 F32 = jnp.float32
 
 T_A, T_N, T_SK, T_D, T_R = range(5)
+GATHERED = (2, 3, 4,)
 
 
 def whole(count):
@@ -35,8 +36,21 @@
     }
 
 
-def spread_table(table, tab_ref):
+def gather(table, kinds):
+    return jnp.concatenate(
+        [
+            jnp.take_along_axis(
+                table, kinds[:, c : c + LANES], axis=1, mode="promise_in_bounds"
+            )
+            for c in range(0, kinds.shape[1], LANES)
+        ],
+        axis=1,
+    )
+
+
+def spread_table(table, tab_ref, rows_ref):
     for row_id, row in table.items():
+        rows_ref[row_id, :, 0 : row.shape[1]] = jnp.broadcast_to(row, (8, row.shape[1]))
         for kind in range(row.shape[1]):
             tab_ref[row_id, kind] = jnp.broadcast_to(row[:, kind : kind + 1], (8, LANES))
 
@@ -111,7 +125,7 @@
     return moves
 
 
-def pack_kernel(swap, p_ref, soil_ref, params_ref, tab_ref, even_ref, odd_ref, *rest):
+def pack_kernel(swap, p_ref, soil_ref, params_ref, tab_ref, rows_ref, even_ref, odd_ref, *rest):
     layers, rows, _ = p_ref.shape
     count = 1 if swap else 2
     vert_refs = rest[:count]
@@ -135,7 +149,7 @@
     for copy in copies:
         copy.start()
     copies[0].wait()
-    spread_table(build_table(params_buf), tab_ref)
+    spread_table(build_table(params_buf), tab_ref, rows_ref)
     for copy in copies[1:]:
         copy.wait()
     for i, low, high in ((0, p_buf[0], p_buf[1]), (1, code(soil_buf[0]), code(soil_buf[1]))):
@@ -173,7 +187,7 @@
 
 
 def local_kernel(
-    p_ref, theta_ref, source_ref, soil_ref, tab_ref, kept_ref, kap_ref, sums_ref
+    p_ref, theta_ref, source_ref, soil_ref, tab_ref, rows_ref, kept_ref, kap_ref, sums_ref
 ):
     layers, rows, width = p_ref.shape
     kind_count = tab_ref.shape[1]
@@ -182,7 +196,10 @@
     held = None
     for layer in range(layers):
         bits = type_bits(soil_ref[layer], kind_count)
-        pa, pn, psk, pd, pr = [pick(tab_ref, i, bits, width) for i in range(5)]
+        pa, pn, psk, pd, pr = [
+            gather(rows_ref[i], soil_ref[layer]) if i in GATHERED else pick(tab_ref, i, bits, width)
+            for i in range(5)
+        ]
         pc, pcap = power(pn), pd * (pn - 1.0)
         h = p_ref[layer]
         kap, sat, over = hydraulics(h, pa, pn, pc, psk)
@@ -324,52 +341,44 @@
             out_ref[row : row + 1, lane : lane + LANES] = tail[:, j * LANES : (j + 1) * LANES]
 
 
-def edge_kernel(
-    rim_odd_ref,
-    rim_even_ref,
-    mine_ref,
-    to_odd_ref,
-    to_even_ref,
-    from_odd_ref,
-    from_even_ref,
-    halo_ref,
-):
-    _, layers, width = rim_odd_ref.shape
-    sides = (
-        (rim_even_ref, to_even_ref, from_even_ref),
-        (rim_odd_ref, to_odd_ref, from_odd_ref),
+def edge_block(odd, rim_ref, mine_ref, to_ref, from_ref):
+    _, layers, width = rim_ref.shape
+    pa, pn, pc, psk, pd = [rim_ref[i] for i in range(5)]
+    theirs = from_ref[:, 0:width]
+    kap, sat, over = hydraulics(theirs, pa, pn, pc, psk)
+    cond = kap * kap
+    tail = jnp.concatenate(
+        [from_ref[row : row + 1, lane : lane + LANES] for row, lane in tail_spots(layers, width)],
+        axis=1,
     )
-    for side, (live, (rim_ref, to_ref, from_ref)) in enumerate(zip(paired(), sides)):
-        pa, pn, pc, psk, pd = [rim_ref[i] for i in range(5)]
-        theirs = from_ref[:, 0:width]
-        kap, sat, over = hydraulics(theirs, pa, pn, pc, psk)
-        cond = kap * kap
-        tail = jnp.concatenate(
-            [
-                from_ref[row : row + 1, lane : lane + LANES]
-                for row, lane in tail_spots(layers, width)
-            ],
-            axis=1,
-        )
-
-        def total(x):
-            return jnp.sum(x, axis=0, keepdims=True)
-
-        flux = total(mine_ref[side] * kap * (theirs - to_ref[:, 0:width]))
-        block = jnp.concatenate(
-            [
-                total(cond * theirs),
-                total(cond),
-                total(pd * (pn - 1.0) * sat * over),
-                tail[:, 0:width] - flux,
-                tail[:, width:],
-                total(jnp.exp2(pa)),
-                flux,
-                jnp.zeros_like(flux),
-            ],
-            axis=0,
-        )
-        halo_ref[side] = jnp.where(live, block, 0.0)
+
+    def total(x):
+        return jnp.sum(x, axis=0, keepdims=True)
+
+    flux = total(mine_ref[odd] * kap * (theirs - to_ref[:, 0:width]))
+    block = jnp.concatenate(
+        [
+            total(cond * theirs),
+            total(cond),
+            total(pd * (pn - 1.0) * sat * over),
+            tail[:, 0:width] - flux,
+            tail[:, width:],
+            total(jnp.exp2(pa)),
+            flux,
+            jnp.zeros_like(flux),
+        ],
+        axis=0,
+    )
+    return jnp.where(paired()[odd], block, 0.0)
+
+
+def odd_edge_kernel(rim_ref, mine_ref, to_ref, from_ref, block_ref):
+    block_ref[...] = edge_block(1, rim_ref, mine_ref, to_ref, from_ref)
+
+
+def even_edge_kernel(rim_ref, mine_ref, to_ref, from_ref, odd_block_ref, halo_ref):
+    halo_ref[0] = edge_block(0, rim_ref, mine_ref, to_ref, from_ref)
+    halo_ref[1] = odd_block_ref[...]
 
 
 def columns_kernel(sums_ref, their_sums_ref, columns_ref):
@@ -462,11 +471,11 @@
     ]
     packed = pl.pallas_call(
         functools.partial(pack_kernel, swap),
-        out_shape=[shape(5, kind_count, 8, LANES)]
+        out_shape=[shape(5, kind_count, 8, LANES), shape(5, 8, LANES)]
         + [shape(2, layers, width)] * 2
         + [shape(2, rows, width)] * verts,
         in_specs=[pl.BlockSpec(memory_space=pltpu.HBM)] * 3,
-        out_specs=whole(3 + verts),
+        out_specs=whole(4 + verts),
         scratch_shapes=[
             pltpu.VMEM((2, layers, width), F32),
             pltpu.VMEM((2, layers, width), jnp.int32),
@@ -479,20 +488,20 @@
         cost_estimate=pl.CostEstimate(flops=PACK_COST, transcendentals=0, bytes_accessed=0),
         name="pack",
     )(*in_hbm)
-    from_odd = lax.ppermute(packed[2], both, odd_moves)
-    from_even = lax.ppermute(packed[1], both, even_moves)
+    from_odd = lax.ppermute(packed[3], both, odd_moves)
+    from_even = lax.ppermute(packed[2], both, even_moves)
     if swap:
-        vert = [lax.ppermute(packed[3], "depth", swapped)]
+        vert = [lax.ppermute(packed[4], "depth", swapped)]
     else:
-        vert = [lax.ppermute(packed[3], "depth", down), lax.ppermute(packed[4], "depth", up)]
+        vert = [lax.ppermute(packed[4], "depth", down), lax.ppermute(packed[5], "depth", up)]
     kept, kap, local_sums = pl.pallas_call(
         local_kernel,
         out_shape=[shape(8, layers, rows, width), shape(layers, rows, width), shape(2, rows, width)],
-        in_specs=whole(5),
+        in_specs=whole(6),
         out_specs=whole(3),
         compiler_params=params,
         name="local",
-    )(pressure, theta_old, source, soil_type, packed[0])
+    )(pressure, theta_old, source, soil_type, packed[0], packed[1])
     rims = [
         pl.pallas_call(
             functools.partial(rim_kernel, odd),
@@ -526,15 +535,23 @@
         their_sums = lax.ppermute(sums, "depth", swapped)
     else:
         sums, their_sums = lax.psum(sums, "depth"), jnp.zeros_like(sums)
+    odd_block = pl.pallas_call(
+        odd_edge_kernel,
+        out_shape=shape(8, width),
+        in_specs=whole(4),
+        out_specs=whole(1)[0],
+        compiler_params=params,
+        cost_estimate=pl.CostEstimate(flops=EDGE_COST, transcendentals=0, bytes_accessed=0),
+        name="odd_edge",
+    )(rims[1], mine, to_odd, from_odd)
     halo = pl.pallas_call(
-        edge_kernel,
+        even_edge_kernel,
         out_shape=shape(2, 8, width),
-        in_specs=whole(7),
+        in_specs=whole(5),
         out_specs=whole(1)[0],
-        cost_estimate=pl.CostEstimate(flops=EDGE_COST, transcendentals=0, bytes_accessed=0),
-        compiler_params=params,
-        name="edge",
-    )(rims[1], rims[0], mine, to_odd, to_even, from_odd, from_even)
+        compiler_params=params,
+        name="even_edge",
+    )(rims[0], mine, to_even, from_even, odd_block)
     if swap:
         their_halo = lax.ppermute(halo, "depth", swapped)
     else:

time: 22.1 us -> 21.7 us (0.982)
  starting transfers between devices: 9.46 us -> 10 us
  Pallas kernels: 7.31 us -> 6.81 us
  waiting for transfers between devices: 4.4 us -> 3.91 us
    ppermute x1, starting transfers between devices: 1.37 us -> 0.16 us  [shards(): their_sums = lax.ppermute(sums, 'depth', swapped)]
    ppermute x1, starting transfers between devices: 0.2 us -> 1.12 us  [shards(): from_even = lax.ppermute(to_even, both, even_moves)]
    pallas_call x1, Pallas kernels: 2.76 us -> 2.22 us  [shards(): pl.pallas_call(local_kernel, out_shape=[shape(8, layers, rows, width), sh...]
    ppermute x1, starting transfers between devices: 1.76 us -> 2.18 us  [shards(): their_halo = lax.ppermute(halo, 'depth', swapped)]
    ppermute x1, starting transfers between devices: 1.5 us -> 1.93 us  [shards(): from_odd = lax.ppermute(to_odd, both, odd_moves)]
    ppermute x1, waiting for transfers between devices: 2.26 us -> 1.88 us  [shards(): their_sums = lax.ppermute(sums, 'depth', swapped)]
  transfers between devices with their start and end apart: 7 -> 7, of which waited for: 3 -> 4; matrix products, arithmetic and copies ran while one was open for 0% -> 0% of each run, Pallas kernels for 16% -> 14%
where the time goes in v7:
time: 21.7 us; the launch traced here: 21.5 us
  starting transfers between devices  10 us (46%)
  Pallas kernels  6.81 us (31%)
  waiting for transfers between devices  3.91 us (18%)
  between operations  0.74 us (3%)
    ppermute x1, starting transfers between devices, shards(): from_odd = lax.ppermute(packed[3], both, odd_moves)  3 us
    pallas_call x1, Pallas kernels, shards(): pl.pallas_call(local_kernel, out_shape=[shape(8, layers, rows, width), sh...  2.22 us
    ppermute x1, starting transfers between devices, shards(): their_halo = lax.ppermute(halo, 'depth', swapped)  2.18 us
    ppermute x1, starting transfers between devices, shards(): from_odd = lax.ppermute(to_odd, both, odd_moves)  1.93 us
    ppermute x1, waiting for transfers between devices, shards(): their_sums = lax.ppermute(sums, 'depth', swapped)  1.88 us
    pallas_call x1, Pallas kernels, shards(): pl.pallas_call(functools.partial(fine_kernel, swap), out_shape=[shape(lay...  1.52 us
    ppermute x1, starting transfers between devices, shards(): vert = [lax.ppermute(packed[4], 'depth', swapped)]  1.49 us
    pallas_call x1, Pallas kernels, shards(): pl.pallas_call(functools.partial(pack_kernel, swap), out_shape=[shape(5,...  1.23 us
  transfers between devices with their start and end apart: 7, of which 4 were waited for; matrix products, arithmetic and copies ran while one was open for 0% of the time, Pallas kernels for 14%

profile of v7, /device:TPU:0, one launch (start us, length us, event | category | flops | bytes accessed | tf_op | source)
XLA Modules:
  0.0 21.5 jit_solution(2391850412926392505)
XLA Ops:
  0.6 0.0 copy-start
  0.6 0.0 copy-start.3
  0.7 0.0 copy-start.2
  0.7 0.0 copy-start.1
  0.7 1.2 %pack.1 = (f32[5,12,8,128]{3,2,1,0:T(8,128)S(1)}, f32[5,8,128]{2,1,0:T(8,128)S(1)}, f32[2,16,1024]{2,1,0:T(8,128)S(1)}, f32[2,16,1024]{2,1,0:T(8,128)S(1)}, f32[2,8,1024]{2,1,0:T(8,128)S(1)}) custom-call(f32[16,8,1024]{2,1,0:T(8,128)} %p_ref.5, s32[16,8,1024]{2,1,0:T(8,128)} %soil_ref.3, f32[5,12]{1,0:T(8,128)} %params_ref.1), custom_call_target="tpu_custom_call" | custom-call | flops 4000000000 | tf_op jit(solution)/shard_map/pack/pallas_call | solution.py:472
  1.9 3.0 %collective-permute-start.1 = (f32[2,16,1024]{2,1,0:T(8,128)S(1)}, f32[2,16,1024]{2,1,0:T(8,128)S(1)}, u32[]{:S(2)}, u32[]{:S(2)}) collective-permute-start(f32[2,16,1024]{2,1,0:T(8,128)S(1)} %get-tuple-element.21), channel_id=1, source_target_pairs={{0,1},{1,0},{2,4},{3,5},{4,2},{5,3},{6,8},{7,9},{8,6},{9,7},{10,12... | collective-permute-start | bytes 393224 | tf_op jit(solution)/shard_map/ppermute | solution.py:491
  4.9 0.1 collective-permute-start
  5.1 1.5 %collective-permute-start.2 = (f32[2,8,1024]{2,1,0:T(8,128)S(1)}, f32[2,8,1024]{2,1,0:T(8,128)S(1)}, u32[]{:S(2)}, u32[]{:S(2)}) collective-permute-start(f32[2,8,1024]{2,1,0:T(8,128)S(1)} %get-tuple-element.22), channel_id=1, source_target_pairs={{0,1},{1,0},{2,3},{3,2},{4,5},{5,4},{6,7},{7,6},{8,9},{9,8},{10,11... | collective-permute-start | bytes 196616 | tf_op jit(solution)/shard_map/ppermute | solution.py:494
  6.5 0.0 copy-done
  6.5 0.0 copy-done.3
  6.5 0.0 copy-done.2
  6.6 0.0 copy-done.1
  6.6 2.2 %local.1 = (f32[8,16,8,1024]{3,2,1,0:T(8,128)S(1)}, f32[16,8,1024]{2,1,0:T(8,128)S(1)}, f32[2,8,1024]{2,1,0:T(8,128)S(1)}) custom-call(f32[16,8,1024]{2,1,0:T(8,128)S(1)} %copy-done, f32[16,8,1024]{2,1,0:T(8,128)S(1)} %copy-done.1, f32[16,8,1024]{2,1,0:T(8,128)S(1)} %copy-done.2, s32[16,8,1024]{2,1,0:T(8,128)S(1)} %copy-done.3, ...), custom_call_target="tpu_custom_call" | custom-call | tf_op jit(solution)/shard_map/local/pallas_call | solution.py:497
  8.8 0.0 collective-permute-done.1.from_ref.from_odd_ref
  8.8 0.2 %rim.3.rim_odd_ref.rim_ref = f32[6,16,1024]{2,1,0:T(8,128)S(1)} custom-call(f32[2,16,1024]{2,1,0:T(8,128)S(1)} %collective-permute-done.1.from_ref.from_odd_ref, f32[5,12,8,128]{3,2,1,0:T(8,128)S(1)} %get-tuple-element.15.tab_ref), custom_call_target="tpu_custom_call" | custom-call | tf_op jit(solution)/shard_map/rim/pallas_call | solution.py:506
  9.0 0.0 collective-permute-done.from_ref.from_even_ref
  9.0 0.2 %rim.2.rim_even_ref.rim_ref = f32[6,16,1024]{2,1,0:T(8,128)S(1)} custom-call(f32[2,16,1024]{2,1,0:T(8,128)S(1)} %collective-permute-done.from_ref.from_even_ref, f32[5,12,8,128]{3,2,1,0:T(8,128)S(1)} %get-tuple-element.15.tab_ref), custom_call_target="tpu_custom_call" | custom-call | tf_op jit(solution)/shard_map/rim/pallas_call | solution.py:506
  9.3 0.1 collective-permute-done.2.rest_0_
  9.4 1.5 %fine.1 = (f32[16,8,1024]{2,1,0:T(8,128)S(1)}, f32[5,8,1024]{2,1,0:T(8,128)S(1)}, f32[16,1152]{1,0:T(8,128)S(1)}, f32[16,1152]{1,0:T(8,128)S(1)}, f32[2,16,1024]{2,1,0:T(8,128)S(1)}) custom-call(f32[16,8,1024]{2,1,0:T(8,128)S(1)} %copy-done, f32[8,16,8,1024]{3,2,1,0:T(8,128)S(1)} %get-tuple-element.17.kept_ref, ...), custom_call_target="tpu_custom_call" | custom-call | tf_op jit(solution)/shard_map/fine/pallas_call | solution.py:517
  10.9 1.9 %collective-permute-start.5 = (f32[16,1152]{1,0:T(8,128)S(1)}, f32[16,1152]{1,0:T(8,128)S(1)}, u32[]{:S(2)}, u32[]{:S(2)}) collective-permute-start(f32[16,1152]{1,0:T(8,128)S(1)} %get-tuple-element.27.to_ref), channel_id=1, source_target_pairs={{0,1},{1,0},{2,4},{3,5},{4,2},{5,3},{6,8},{7,9},{8,6},{9,7},{10,12... | collective-permute-start | bytes 221192 | tf_op jit(solution)/shard_map/ppermute | solution.py:532
  12.9 0.2 collective-permute-start.3
  13.0 1.1 %collective-permute-start.4 = (f32[16,1152]{1,0:T(8,128)S(1)}, f32[16,1152]{1,0:T(8,128)S(1)}, u32[]{:S(2)}, u32[]{:S(2)}) collective-permute-start(f32[16,1152]{1,0:T(8,128)S(1)} %get-tuple-element.26.to_ref), channel_id=1, source_target_pairs={{0,2},{1,3},{2,0},{3,1},{4,6},{5,7},{6,4},{7,5},{8,10},{9,11},{10,... | collective-permute-start | bytes 221192 | tf_op jit(solution)/shard_map/ppermute | solution.py:533
  14.2 1.2 %collective-permute-done.5.from_ref = f32[16,1152]{1,0:T(8,128)S(1)} collective-permute-done((f32[16,1152]{1,0:T(8,128)S(1)}, f32[16,1152]{1,0:T(8,128)S(1)}, u32[]{:S(2)}, u32[]{:S(2)}) %collective-permute-start.5) | collective-permute-done | bytes 73760 | tf_op jit(solution)/shard_map/ppermute | solution.py:532
  15.4 0.2 odd_edge.1.odd_block_ref
  15.5 0.0 collective-permute-done.4.from_ref
  15.5 0.2 even_edge.1.halo_ref
  15.7 2.2 %collective-permute-start.6 = (f32[2,8,1024]{2,1,0:T(8,128)S(1)}, f32[2,8,1024]{2,1,0:T(8,128)S(1)}, u32[]{:S(2)}, u32[]{:S(2)}) collective-permute-start(f32[2,8,1024]{2,1,0:T(8,128)S(1)} %even_edge.1.halo_ref), channel_id=1, source_target_pairs={{0,1},{1,0},{2,3},{3,2},{4,5},{5,4},{6,7},{7,6},{8,9},{9,8},{10,11... | collective-permute-start | bytes 196616 | tf_op jit(solution)/shard_map/ppermute | solution.py:556
  17.9 1.9 %collective-permute-done.3.their_sums_ref = f32[5,8,1024]{2,1,0:T(8,128)S(1)} collective-permute-done((f32[5,8,1024]{2,1,0:T(8,128)S(1)}, f32[5,8,1024]{2,1,0:T(8,128)S(1)}, u32[]{:S(2)}, u32[]{:S(2)}) %collective-permute-start.3) | collective-permute-done | bytes 163872 | tf_op jit(solution)/shard_map/ppermute | solution.py:535
  19.8 0.7 %collective-permute-done.6.their_halo_ref = f32[2,8,1024]{2,1,0:T(8,128)S(1)} collective-permute-done((f32[2,8,1024]{2,1,0:T(8,128)S(1)}, f32[2,8,1024]{2,1,0:T(8,128)S(1)}, u32[]{:S(2)}, u32[]{:S(2)}) %collective-permute-start.6) | collective-permute-done | bytes 65568 | tf_op jit(solution)/shard_map/ppermute | solution.py:556
  20.5 1.1 %coarse.1 = (f32[16,8,1024]{2,1,0:T(8,128)}, f32[8,1024]{1,0:T(8,128)}) custom-call(f32[16,8,1024]{2,1,0:T(8,128)S(1)} %get-tuple-element.23.smooth_ref, f32[5,8,1024]{2,1,0:T(8,128)S(1)} %columns.1.columns_ref, f32[2,8,1024]{2,1,0:T(8,128)S(1)} %even_edge.1.halo_ref, f32[2,8,1024]{2,1,0:T(8,128)S(1)} %collective-permute-done.6.their_halo_ref), custom_call_target="tpu_custom_call" | custom-call | tf_op jit(solution)/shard_map/coarse/pallas_call | solution.py:567
  (1 shorter events, 0.0 us)
Async XLA Ops:
  0.6 5.9 %copy-start = (f32[16,8,1024]{2,1,0:T(8,128)S(1)}, f32[16,8,1024]{2,1,0:T(8,128)}, u32[]{:S(2)}) copy-start(f32[16,8,1024]{2,1,0:T(8,128)} %p_ref.5) | copy-start | bytes 1572868
  0.6 5.9 %copy-start.3 = (s32[16,8,1024]{2,1,0:T(8,128)S(1)}, s32[16,8,1024]{2,1,0:T(8,128)}, u32[]{:S(2)}) copy-start(s32[16,8,1024]{2,1,0:T(8,128)} %soil_ref.3) | copy-start | bytes 1572868
  0.7 5.9 %copy-start.2 = (f32[16,8,1024]{2,1,0:T(8,128)S(1)}, f32[16,8,1024]{2,1,0:T(8,128)}, u32[]{:S(2)}) copy-start(f32[16,8,1024]{2,1,0:T(8,128)} %source_ref.1) | copy-start | bytes 1572868
  0.7 5.9 %copy-start.1 = (f32[16,8,1024]{2,1,0:T(8,128)S(1)}, f32[16,8,1024]{2,1,0:T(8,128)}, u32[]{:S(2)}) copy-start(f32[16,8,1024]{2,1,0:T(8,128)} %theta_ref.1) | copy-start | bytes 1572868
  1.9 6.9 %collective-permute-start.1 = (f32[2,16,1024]{2,1,0:T(8,128)S(1)}, f32[2,16,1024]{2,1,0:T(8,128)S(1)}, u32[]{:S(2)}, u32[]{:S(2)}) collective-permute-start(f32[2,16,1024]{2,1,0:T(8,128)S(1)} %get-tuple-element.21), channel_id=1, source_target_pairs={{0,1},{1,0},{2,4},{3,5},{4,2},{5,3},{6,8},{7,9},{8,6},{9,7},{10,12... | collective-permute-start | bytes 393224 | tf_op jit(solution)/shard_map/ppermute | solution.py:491
  4.9 4.1 %collective-permute-start = (f32[2,16,1024]{2,1,0:T(8,128)S(1)}, f32[2,16,1024]{2,1,0:T(8,128)S(1)}, u32[]{:S(2)}, u32[]{:S(2)}) collective-permute-start(f32[2,16,1024]{2,1,0:T(8,128)S(1)} %get-tuple-element.20), channel_id=1, source_target_pairs={{0,2},{1,3},{2,0},{3,1},{4,6},{5,7},{6,4},{7,5},{8,10},{9,11},{10,... | collective-permute-start | bytes 393224 | tf_op jit(solution)/shard_map/ppermute | solution.py:492
  5.1 4.4 %collective-permute-start.2 = (f32[2,8,1024]{2,1,0:T(8,128)S(1)}, f32[2,8,1024]{2,1,0:T(8,128)S(1)}, u32[]{:S(2)}, u32[]{:S(2)}) collective-permute-start(f32[2,8,1024]{2,1,0:T(8,128)S(1)} %get-tuple-element.22), channel_id=1, source_target_pairs={{0,1},{1,0},{2,3},{3,2},{4,5},{5,4},{6,7},{7,6},{8,9},{9,8},{10,11... | collective-permute-start | bytes 196616 | tf_op jit(solution)/shard_map/ppermute | solution.py:494
  10.9 4.4 %collective-permute-start.5 = (f32[16,1152]{1,0:T(8,128)S(1)}, f32[16,1152]{1,0:T(8,128)S(1)}, u32[]{:S(2)}, u32[]{:S(2)}) collective-permute-start(f32[16,1152]{1,0:T(8,128)S(1)} %get-tuple-element.27.to_ref), channel_id=1, source_target_pairs={{0,1},{1,0},{2,4},{3,5},{4,2},{5,3},{6,8},{7,9},{8,6},{9,7},{10,12... | collective-permute-start | bytes 221192 | tf_op jit(solution)/shard_map/ppermute | solution.py:532
  12.9 6.9 %collective-permute-start.3 = (f32[5,8,1024]{2,1,0:T(8,128)S(1)}, f32[5,8,1024]{2,1,0:T(8,128)S(1)}, u32[]{:S(2)}, u32[]{:S(2)}) collective-permute-start(f32[5,8,1024]{2,1,0:T(8,128)S(1)} %get-tuple-element.24.sums_ref), channel_id=1, source_target_pairs={{0,1},{1,0},{2,3},{3,2},{4,5},{5,4},{6,7},{7,6},{8,9},{9,8},{10,11... | collective-permute-start | bytes 491528 | tf_op jit(solution)/shard_map/ppermute | solution.py:535
  13.0 2.5 %collective-permute-start.4 = (f32[16,1152]{1,0:T(8,128)S(1)}, f32[16,1152]{1,0:T(8,128)S(1)}, u32[]{:S(2)}, u32[]{:S(2)}) collective-permute-start(f32[16,1152]{1,0:T(8,128)S(1)} %get-tuple-element.26.to_ref), channel_id=1, source_target_pairs={{0,2},{1,3},{2,0},{3,1},{4,6},{5,7},{6,4},{7,5},{8,10},{9,11},{10,... | collective-permute-start | bytes 221192 | tf_op jit(solution)/shard_map/ppermute | solution.py:533
  15.7 4.8 %collective-permute-start.6 = (f32[2,8,1024]{2,1,0:T(8,128)S(1)}, f32[2,8,1024]{2,1,0:T(8,128)S(1)}, u32[]{:S(2)}, u32[]{:S(2)}) collective-permute-start(f32[2,8,1024]{2,1,0:T(8,128)S(1)} %even_edge.1.halo_ref), channel_id=1, source_target_pairs={{0,1},{1,0},{2,3},{3,2},{4,5},{5,4},{6,7},{7,6},{8,9},{9,8},{10,11... | collective-permute-start | bytes 196616 | tf_op jit(solution)/shard_map/ppermute | solution.py:556

commit v8 on v7

--- a/solution.py
+++ b/solution.py
@@ -376,9 +376,21 @@
     block_ref[...] = edge_block(1, rim_ref, mine_ref, to_ref, from_ref)
 
 
-def even_edge_kernel(rim_ref, mine_ref, to_ref, from_ref, odd_block_ref, halo_ref):
-    halo_ref[0] = edge_block(0, rim_ref, mine_ref, to_ref, from_ref)
-    halo_ref[1] = odd_block_ref[...]
+def fold_spots(row, width):
+    chunks = width // LANES
+    return [((row * chunks + c) % 8, width + (row * chunks + c) // 8 * LANES) for c in range(chunks)]
+
+
+def even_edge_kernel(rim_ref, mine_ref, to_ref, from_ref, odd_block_ref, halo_ref, block_ref):
+    width = block_ref.shape[1]
+    block_ref[...] = edge_block(0, rim_ref, mine_ref, to_ref, from_ref)
+    for side, source in enumerate((block_ref, odd_block_ref)):
+        halo_ref[4 * side : 4 * side + 4, 0:width] = source[0:4, :]
+        for row in range(3):
+            for c, (at, lane) in enumerate(fold_spots(3 * side + row, width)):
+                halo_ref[at : at + 1, lane : lane + LANES] = source[
+                    4 + row : 5 + row, c * LANES : (c + 1) * LANES
+                ]
 
 
 def columns_kernel(sums_ref, their_sums_ref, columns_ref):
@@ -392,22 +404,37 @@
 ):
     rows = smooth_ref.shape[1]
     base, root, cap, rest, rate = [columns_ref[i] for i in range(5)]
-    by_even = halo_ref[0] + their_halo_ref[0]
-    by_odd = halo_ref[1] + their_halo_ref[1]
+    width = columns_ref.shape[2]
+    head = halo_ref[:, 0:width] + their_halo_ref[:, 0:width]
+    sides = []
+    for side in range(2):
+        rows_of = [head[i : i + 1] for i in range(4 * side, 4 * side + 4)]
+        for row in range(3 * side, 3 * side + 3):
+            rows_of.append(
+                jnp.concatenate(
+                    [
+                        halo_ref[at : at + 1, lane : lane + LANES]
+                        + their_halo_ref[at : at + 1, lane : lane + LANES]
+                        for at, lane in fold_spots(row, width)
+                    ],
+                    axis=1,
+                )
+            )
+        sides.append(rows_of)
     even = even_area()
-    lo = jnp.where(even, by_odd, by_even)
-    hi = jnp.where(even, by_even, by_odd)
+    lo = [jnp.where(even, b, a) for a, b in zip(*sides)]
+    hi = [jnp.where(even, a, b) for a, b in zip(*sides)]
     spot = row_iota(rest.shape)
-    rest = jnp.where(spot == 0, rest + lo[6:7], rest)
-    rest = jnp.where(spot == rows - 1, rest + hi[6:7], rest)
+    rest = jnp.where(spot == 0, rest + lo[6], rest)
+    rest = jnp.where(spot == rows - 1, rest + hi[6], rest)
 
     def pair(i):
-        return jnp.where(spot == 0, lo[i : i + 1], jnp.where(spot == rows - 1, hi[i : i + 1], 0.0))
+        return jnp.where(spot == 0, lo[i], jnp.where(spot == rows - 1, hi[i], 0.0))
 
     h_kh, h_k, h_cap, h_rest, o_k, h_rate = [pair(i) for i in range(6)]
     edge_lane = lane_iota(rest.shape)
 
-    def sides(x):
+    def lateral(x):
         return from_left(x) + from_right(x)
 
     h_live = h_k > 0.0
@@ -434,7 +461,7 @@
     start_in, start_sum = flow(base, h_base, root, h_root)
     rhs = rest - start_in
     first = base + RELAX * rest / (cap + start_sum)
-    h_diag = h_cap + h_root * (o_root + root + sides(h_root))
+    h_diag = h_cap + h_root * (o_root + root + lateral(h_root))
     h_first = h_base + jnp.where(h_live, RELAX * h_rest / jnp.where(h_live, h_diag, 1.0), 0.0)
     half = 0.5 / depth_total
     tau = root * jnp.exp(half * rate * jnp.tanh(first - base))
@@ -546,9 +573,10 @@
     )(rims[1], mine, to_odd, from_odd)
     halo = pl.pallas_call(
         even_edge_kernel,
-        out_shape=shape(2, 8, width),
+        out_shape=shape(8, width + pl.cdiv(6 * width // LANES, 8) * LANES),
         in_specs=whole(5),
         out_specs=whole(1)[0],
+        scratch_shapes=[pltpu.VMEM((8, width), F32)],
         compiler_params=params,
         name="even_edge",
     )(rims[0], mine, to_even, from_even, odd_block)

time: 21.7 us -> 21.5 us (level)
  no operation moved by 1% of the time
where the time goes in v8:
time: 21.5 us; the launch traced here: 21.3 us
  starting transfers between devices  10 us (47%)
  Pallas kernels  6.83 us (32%)
  waiting for transfers between devices  3.71 us (17%)
  between operations  0.74 us (3%)
    ppermute x1, starting transfers between devices, shards(): from_odd = lax.ppermute(packed[3], both, odd_moves)  3 us
    pallas_call x1, Pallas kernels, shards(): pl.pallas_call(local_kernel, out_shape=[shape(8, layers, rows, width), sh...  2.22 us
    ppermute x1, starting transfers between devices, shards(): their_halo = lax.ppermute(halo, 'depth', swapped)  2.18 us
    ppermute x1, starting transfers between devices, shards(): from_odd = lax.ppermute(to_odd, both, odd_moves)  1.93 us
    ppermute x1, waiting for transfers between devices, shards(): their_sums = lax.ppermute(sums, 'depth', swapped)  1.77 us
    pallas_call x1, Pallas kernels, shards(): pl.pallas_call(functools.partial(fine_kernel, swap), out_shape=[shape(lay...  1.52 us
    ppermute x1, starting transfers between devices, shards(): vert = [lax.ppermute(packed[4], 'depth', swapped)]  1.49 us
    pallas_call x1, Pallas kernels, shards(): pl.pallas_call(functools.partial(pack_kernel, swap), out_shape=[shape(5,...  1.23 us
  transfers between devices with their start and end apart: 7, of which 4 were waited for; matrix products, arithmetic and copies ran while one was open for 0% of the time, Pallas kernels for 14%

profile of v8, /device:TPU:0, one launch (start us, length us, event | category | flops | bytes accessed | tf_op | source)
XLA Modules:
  0.0 21.3 jit_solution(6711559219258621792)
XLA Ops:
  0.6 0.0 copy-start
  0.6 0.0 copy-start.3
  0.7 0.0 copy-start.2
  0.7 0.0 copy-start.1
  0.7 1.2 %pack.1 = (f32[5,12,8,128]{3,2,1,0:T(8,128)S(1)}, f32[5,8,128]{2,1,0:T(8,128)S(1)}, f32[2,16,1024]{2,1,0:T(8,128)S(1)}, f32[2,16,1024]{2,1,0:T(8,128)S(1)}, f32[2,8,1024]{2,1,0:T(8,128)S(1)}) custom-call(f32[16,8,1024]{2,1,0:T(8,128)} %p_ref.5, s32[16,8,1024]{2,1,0:T(8,128)} %soil_ref.3, f32[5,12]{1,0:T(8,128)} %params_ref.1), custom_call_target="tpu_custom_call" | custom-call | flops 4000000000 | tf_op jit(solution)/shard_map/pack/pallas_call | solution.py:499
  1.9 3.0 %collective-permute-start.1 = (f32[2,16,1024]{2,1,0:T(8,128)S(1)}, f32[2,16,1024]{2,1,0:T(8,128)S(1)}, u32[]{:S(2)}, u32[]{:S(2)}) collective-permute-start(f32[2,16,1024]{2,1,0:T(8,128)S(1)} %get-tuple-element.21), channel_id=1, source_target_pairs={{0,1},{1,0},{2,4},{3,5},{4,2},{5,3},{6,8},{7,9},{8,6},{9,7},{10,12... | collective-permute-start | bytes 393224 | tf_op jit(solution)/shard_map/ppermute | solution.py:518
  4.9 0.1 collective-permute-start
  5.1 1.5 %collective-permute-start.2 = (f32[2,8,1024]{2,1,0:T(8,128)S(1)}, f32[2,8,1024]{2,1,0:T(8,128)S(1)}, u32[]{:S(2)}, u32[]{:S(2)}) collective-permute-start(f32[2,8,1024]{2,1,0:T(8,128)S(1)} %get-tuple-element.22), channel_id=1, source_target_pairs={{0,1},{1,0},{2,3},{3,2},{4,5},{5,4},{6,7},{7,6},{8,9},{9,8},{10,11... | collective-permute-start | bytes 196616 | tf_op jit(solution)/shard_map/ppermute | solution.py:521
  6.5 0.0 copy-done
  6.5 0.0 copy-done.3
  6.5 0.0 copy-done.2
  6.6 0.0 copy-done.1
  6.6 2.2 %local.1 = (f32[8,16,8,1024]{3,2,1,0:T(8,128)S(1)}, f32[16,8,1024]{2,1,0:T(8,128)S(1)}, f32[2,8,1024]{2,1,0:T(8,128)S(1)}) custom-call(f32[16,8,1024]{2,1,0:T(8,128)S(1)} %copy-done, f32[16,8,1024]{2,1,0:T(8,128)S(1)} %copy-done.1, f32[16,8,1024]{2,1,0:T(8,128)S(1)} %copy-done.2, s32[16,8,1024]{2,1,0:T(8,128)S(1)} %copy-done.3, ...), custom_call_target="tpu_custom_call" | custom-call | tf_op jit(solution)/shard_map/local/pallas_call | solution.py:524
  8.8 0.0 collective-permute-done.1.from_ref.from_odd_ref
  8.8 0.2 %rim.3.rim_odd_ref.rim_ref = f32[6,16,1024]{2,1,0:T(8,128)S(1)} custom-call(f32[2,16,1024]{2,1,0:T(8,128)S(1)} %collective-permute-done.1.from_ref.from_odd_ref, f32[5,12,8,128]{3,2,1,0:T(8,128)S(1)} %get-tuple-element.15.tab_ref), custom_call_target="tpu_custom_call" | custom-call | tf_op jit(solution)/shard_map/rim/pallas_call | solution.py:533
  9.0 0.0 collective-permute-done.from_ref.from_even_ref
  9.0 0.2 %rim.2.rim_even_ref.rim_ref = f32[6,16,1024]{2,1,0:T(8,128)S(1)} custom-call(f32[2,16,1024]{2,1,0:T(8,128)S(1)} %collective-permute-done.from_ref.from_even_ref, f32[5,12,8,128]{3,2,1,0:T(8,128)S(1)} %get-tuple-element.15.tab_ref), custom_call_target="tpu_custom_call" | custom-call | tf_op jit(solution)/shard_map/rim/pallas_call | solution.py:533
  9.3 0.1 collective-permute-done.2.rest_0_
  9.4 1.5 %fine.1 = (f32[16,8,1024]{2,1,0:T(8,128)S(1)}, f32[5,8,1024]{2,1,0:T(8,128)S(1)}, f32[16,1152]{1,0:T(8,128)S(1)}, f32[16,1152]{1,0:T(8,128)S(1)}, f32[2,16,1024]{2,1,0:T(8,128)S(1)}) custom-call(f32[16,8,1024]{2,1,0:T(8,128)S(1)} %copy-done, f32[8,16,8,1024]{3,2,1,0:T(8,128)S(1)} %get-tuple-element.17.kept_ref, ...), custom_call_target="tpu_custom_call" | custom-call | tf_op jit(solution)/shard_map/fine/pallas_call | solution.py:544
  10.9 1.9 %collective-permute-start.5 = (f32[16,1152]{1,0:T(8,128)S(1)}, f32[16,1152]{1,0:T(8,128)S(1)}, u32[]{:S(2)}, u32[]{:S(2)}) collective-permute-start(f32[16,1152]{1,0:T(8,128)S(1)} %get-tuple-element.27.to_ref), channel_id=1, source_target_pairs={{0,1},{1,0},{2,4},{3,5},{4,2},{5,3},{6,8},{7,9},{8,6},{9,7},{10,12... | collective-permute-start | bytes 221192 | tf_op jit(solution)/shard_map/ppermute | solution.py:559
  12.9 0.2 collective-permute-start.3
  13.0 1.1 %collective-permute-start.4 = (f32[16,1152]{1,0:T(8,128)S(1)}, f32[16,1152]{1,0:T(8,128)S(1)}, u32[]{:S(2)}, u32[]{:S(2)}) collective-permute-start(f32[16,1152]{1,0:T(8,128)S(1)} %get-tuple-element.26.to_ref), channel_id=1, source_target_pairs={{0,2},{1,3},{2,0},{3,1},{4,6},{5,7},{6,4},{7,5},{8,10},{9,11},{10,... | collective-permute-start | bytes 221192 | tf_op jit(solution)/shard_map/ppermute | solution.py:560
  14.2 1.2 %collective-permute-done.5.from_ref = f32[16,1152]{1,0:T(8,128)S(1)} collective-permute-done((f32[16,1152]{1,0:T(8,128)S(1)}, f32[16,1152]{1,0:T(8,128)S(1)}, u32[]{:S(2)}, u32[]{:S(2)}) %collective-permute-start.5) | collective-permute-done | bytes 73760 | tf_op jit(solution)/shard_map/ppermute | solution.py:559
  15.4 0.2 odd_edge.1.odd_block_ref
  15.5 0.0 collective-permute-done.4.from_ref
  15.5 0.2 even_edge.1.halo_ref
  15.7 2.2 %collective-permute-start.6 = (f32[8,1792]{1,0:T(8,128)S(1)}, f32[8,1792]{1,0:T(8,128)S(1)}, u32[]{:S(2)}, u32[]{:S(2)}) collective-permute-start(f32[8,1792]{1,0:T(8,128)S(1)} %even_edge.1.halo_ref), channel_id=1, source_target_pairs={{0,1},{1,0},{2,3},{3,2},{4,5},{5,4},{6,7},{7,6},{8,9},{9,8},{10,11... | collective-permute-start | bytes 172040 | tf_op jit(solution)/shard_map/ppermute | solution.py:584
  17.9 1.8 %collective-permute-done.3.their_sums_ref = f32[5,8,1024]{2,1,0:T(8,128)S(1)} collective-permute-done((f32[5,8,1024]{2,1,0:T(8,128)S(1)}, f32[5,8,1024]{2,1,0:T(8,128)S(1)}, u32[]{:S(2)}, u32[]{:S(2)}) %collective-permute-start.3) | collective-permute-done | bytes 163872 | tf_op jit(solution)/shard_map/ppermute | solution.py:562
  19.7 0.6 %collective-permute-done.6.their_halo_ref = f32[8,1792]{1,0:T(8,128)S(1)} collective-permute-done((f32[8,1792]{1,0:T(8,128)S(1)}, f32[8,1792]{1,0:T(8,128)S(1)}, u32[]{:S(2)}, u32[]{:S(2)}) %collective-permute-start.6) | collective-permute-done | bytes 57376 | tf_op jit(solution)/shard_map/ppermute | solution.py:584
  20.3 1.0 %coarse.1 = (f32[16,8,1024]{2,1,0:T(8,128)}, f32[8,1024]{1,0:T(8,128)}) custom-call(f32[16,8,1024]{2,1,0:T(8,128)S(1)} %get-tuple-element.23.smooth_ref, f32[5,8,1024]{2,1,0:T(8,128)S(1)} %columns.1.columns_ref, f32[8,1792]{1,0:T(8,128)S(1)} %even_edge.1.halo_ref, f32[8,1792]{1,0:T(8,128)S(1)} %collective-permute-done.6.their_halo_ref), custom_call_target="tpu_custom_call" | custom-call | tf_op jit(solution)/shard_map/coarse/pallas_call | solution.py:595
  (1 shorter events, 0.0 us)
Async XLA Ops:
  0.6 5.9 %copy-start = (f32[16,8,1024]{2,1,0:T(8,128)S(1)}, f32[16,8,1024]{2,1,0:T(8,128)}, u32[]{:S(2)}) copy-start(f32[16,8,1024]{2,1,0:T(8,128)} %p_ref.5) | copy-start | bytes 1572868
  0.6 5.9 %copy-start.3 = (s32[16,8,1024]{2,1,0:T(8,128)S(1)}, s32[16,8,1024]{2,1,0:T(8,128)}, u32[]{:S(2)}) copy-start(s32[16,8,1024]{2,1,0:T(8,128)} %soil_ref.3) | copy-start | bytes 1572868
  0.7 5.9 %copy-start.2 = (f32[16,8,1024]{2,1,0:T(8,128)S(1)}, f32[16,8,1024]{2,1,0:T(8,128)}, u32[]{:S(2)}) copy-start(f32[16,8,1024]{2,1,0:T(8,128)} %source_ref.1) | copy-start | bytes 1572868
  0.7 5.9 %copy-start.1 = (f32[16,8,1024]{2,1,0:T(8,128)S(1)}, f32[16,8,1024]{2,1,0:T(8,128)}, u32[]{:S(2)}) copy-start(f32[16,8,1024]{2,1,0:T(8,128)} %theta_ref.1) | copy-start | bytes 1572868
  1.9 6.9 %collective-permute-start.1 = (f32[2,16,1024]{2,1,0:T(8,128)S(1)}, f32[2,16,1024]{2,1,0:T(8,128)S(1)}, u32[]{:S(2)}, u32[]{:S(2)}) collective-permute-start(f32[2,16,1024]{2,1,0:T(8,128)S(1)} %get-tuple-element.21), channel_id=1, source_target_pairs={{0,1},{1,0},{2,4},{3,5},{4,2},{5,3},{6,8},{7,9},{8,6},{9,7},{10,12... | collective-permute-start | bytes 393224 | tf_op jit(solution)/shard_map/ppermute | solution.py:518
  4.9 4.1 %collective-permute-start = (f32[2,16,1024]{2,1,0:T(8,128)S(1)}, f32[2,16,1024]{2,1,0:T(8,128)S(1)}, u32[]{:S(2)}, u32[]{:S(2)}) collective-permute-start(f32[2,16,1024]{2,1,0:T(8,128)S(1)} %get-tuple-element.20), channel_id=1, source_target_pairs={{0,2},{1,3},{2,0},{3,1},{4,6},{5,7},{6,4},{7,5},{8,10},{9,11},{10,... | collective-permute-start | bytes 393224 | tf_op jit(solution)/shard_map/ppermute | solution.py:519
  5.1 4.4 %collective-permute-start.2 = (f32[2,8,1024]{2,1,0:T(8,128)S(1)}, f32[2,8,1024]{2,1,0:T(8,128)S(1)}, u32[]{:S(2)}, u32[]{:S(2)}) collective-permute-start(f32[2,8,1024]{2,1,0:T(8,128)S(1)} %get-tuple-element.22), channel_id=1, source_target_pairs={{0,1},{1,0},{2,3},{3,2},{4,5},{5,4},{6,7},{7,6},{8,9},{9,8},{10,11... | collective-permute-start | bytes 196616 | tf_op jit(solution)/shard_map/ppermute | solution.py:521
  10.9 4.4 %collective-permute-start.5 = (f32[16,1152]{1,0:T(8,128)S(1)}, f32[16,1152]{1,0:T(8,128)S(1)}, u32[]{:S(2)}, u32[]{:S(2)}) collective-permute-start(f32[16,1152]{1,0:T(8,128)S(1)} %get-tuple-element.27.to_ref), channel_id=1, source_target_pairs={{0,1},{1,0},{2,4},{3,5},{4,2},{5,3},{6,8},{7,9},{8,6},{9,7},{10,12... | collective-permute-start | bytes 221192 | tf_op jit(solution)/shard_map/ppermute | solution.py:559
  12.9 6.8 %collective-permute-start.3 = (f32[5,8,1024]{2,1,0:T(8,128)S(1)}, f32[5,8,1024]{2,1,0:T(8,128)S(1)}, u32[]{:S(2)}, u32[]{:S(2)}) collective-permute-start(f32[5,8,1024]{2,1,0:T(8,128)S(1)} %get-tuple-element.24.sums_ref), channel_id=1, source_target_pairs={{0,1},{1,0},{2,3},{3,2},{4,5},{5,4},{6,7},{7,6},{8,9},{9,8},{10,11... | collective-permute-start | bytes 491528 | tf_op jit(solution)/shard_map/ppermute | solution.py:562
  13.0 2.5 %collective-permute-start.4 = (f32[16,1152]{1,0:T(8,128)S(1)}, f32[16,1152]{1,0:T(8,128)S(1)}, u32[]{:S(2)}, u32[]{:S(2)}) collective-permute-start(f32[16,1152]{1,0:T(8,128)S(1)} %get-tuple-element.26.to_ref), channel_id=1, source_target_pairs={{0,2},{1,3},{2,0},{3,1},{4,6},{5,7},{6,4},{7,5},{8,10},{9,11},{10,... | collective-permute-start | bytes 221192 | tf_op jit(solution)/shard_map/ppermute | solution.py:560
  15.7 4.6 %collective-permute-start.6 = (f32[8,1792]{1,0:T(8,128)S(1)}, f32[8,1792]{1,0:T(8,128)S(1)}, u32[]{:S(2)}, u32[]{:S(2)}) collective-permute-start(f32[8,1792]{1,0:T(8,128)S(1)} %even_edge.1.halo_ref), channel_id=1, source_target_pairs={{0,1},{1,0},{2,3},{3,2},{4,5},{5,4},{6,7},{7,6},{8,9},{9,8},{10,11... | collective-permute-start | bytes 172040 | tf_op jit(solution)/shard_map/ppermute | solution.py:584

commit v9 on v8

--- a/solution.py
+++ b/solution.py
@@ -125,17 +125,21 @@
     return moves
 
 
-def pack_kernel(swap, p_ref, soil_ref, params_ref, tab_ref, rows_ref, even_ref, odd_ref, *rest):
+def table_kernel(params_ref, tab_ref, rows_ref):
+    spread_table(build_table(params_ref), tab_ref, rows_ref)
+
+
+def pack_kernel(swap, p_ref, soil_ref, even_ref, odd_ref, *rest):
     layers, rows, _ = p_ref.shape
     count = 1 if swap else 2
     vert_refs = rest[:count]
-    p_buf, soil_buf, vert_p, vert_soil, params_buf, sems = rest[count:]
+    p_buf, soil_buf, vert_p, vert_soil, sems = rest[count:]
     even = even_area()
     if swap:
         spots = [jnp.where(lax.axis_index("depth") == 0, layers - 1, 0)]
     else:
         spots = [layers - 1, 0]
-    copies = [(params_ref, params_buf)]
+    copies = []
     for side, row in enumerate((0, rows - 1)):
         copies.append((p_ref.at[:, row, :], p_buf.at[side]))
         copies.append((soil_ref.at[:, row, :], soil_buf.at[side]))
@@ -148,9 +152,7 @@
     ]
     for copy in copies:
         copy.start()
-    copies[0].wait()
-    spread_table(build_table(params_buf), tab_ref, rows_ref)
-    for copy in copies[1:]:
+    for copy in copies:
         copy.wait()
     for i, low, high in ((0, p_buf[0], p_buf[1]), (1, code(soil_buf[0]), code(soil_buf[1]))):
         even_ref[i] = jnp.where(even, high, low)
@@ -494,33 +496,38 @@
     kind_count = soil_params.shape[1]
     in_hbm = [
         pltpu.with_memory_space_constraint(x, pltpu.HBM)
-        for x in (pressure, soil_type, soil_params)
+        for x in (pressure, soil_type)
     ]
+    tab, tab_rows = pl.pallas_call(
+        table_kernel,
+        out_shape=[shape(5, kind_count, 8, LANES), shape(5, 8, LANES)],
+        in_specs=whole(1),
+        out_specs=whole(2),
+        compiler_params=params,
+        name="table",
+    )(soil_params)
     packed = pl.pallas_call(
         functools.partial(pack_kernel, swap),
-        out_shape=[shape(5, kind_count, 8, LANES), shape(5, 8, LANES)]
-        + [shape(2, layers, width)] * 2
-        + [shape(2, rows, width)] * verts,
-        in_specs=[pl.BlockSpec(memory_space=pltpu.HBM)] * 3,
-        out_specs=whole(4 + verts),
+        out_shape=[shape(2, layers, width)] * 2 + [shape(2, rows, width)] * verts,
+        in_specs=[pl.BlockSpec(memory_space=pltpu.HBM)] * 2,
+        out_specs=whole(2 + verts),
         scratch_shapes=[
             pltpu.VMEM((2, layers, width), F32),
             pltpu.VMEM((2, layers, width), jnp.int32),
             pltpu.VMEM((verts, rows, width), F32),
             pltpu.VMEM((verts, rows, width), jnp.int32),
-            pltpu.VMEM(soil_params.shape, F32),
-            pltpu.SemaphoreType.DMA((5 + 2 * verts,)),
+            pltpu.SemaphoreType.DMA((4 + 2 * verts,)),
         ],
         compiler_params=params,
         cost_estimate=pl.CostEstimate(flops=PACK_COST, transcendentals=0, bytes_accessed=0),
         name="pack",
     )(*in_hbm)
-    from_odd = lax.ppermute(packed[3], both, odd_moves)
-    from_even = lax.ppermute(packed[2], both, even_moves)
+    from_odd = lax.ppermute(packed[1], both, odd_moves)
+    from_even = lax.ppermute(packed[0], both, even_moves)
     if swap:
-        vert = [lax.ppermute(packed[4], "depth", swapped)]
+        vert = [lax.ppermute(packed[2], "depth", swapped)]
     else:
-        vert = [lax.ppermute(packed[4], "depth", down), lax.ppermute(packed[5], "depth", up)]
+        vert = [lax.ppermute(packed[2], "depth", down), lax.ppermute(packed[3], "depth", up)]
     kept, kap, local_sums = pl.pallas_call(
         local_kernel,
         out_shape=[shape(8, layers, rows, width), shape(layers, rows, width), shape(2, rows, width)],
@@ -528,7 +535,7 @@
         out_specs=whole(3),
         compiler_params=params,
         name="local",
-    )(pressure, theta_old, source, soil_type, packed[0], packed[1])
+    )(pressure, theta_old, source, soil_type, tab, tab_rows)
     rims = [
         pl.pallas_call(
             functools.partial(rim_kernel, odd),
@@ -537,7 +544,7 @@
             out_specs=whole(1)[0],
             compiler_params=params,
             name="rim",
-        )(from_area, packed[0])
+        )(from_area, tab)
         for odd, from_area in enumerate((from_even, from_odd))
     ]
     sent = shape(layers, sent_width(layers, width))
@@ -555,7 +562,7 @@
         scratch_shapes=[pltpu.VMEM((4, layers, width), F32)] * 2,
         compiler_params=params,
         name="fine",
-    )(pressure, kept, kap, local_sums, packed[0], from_even, from_odd, *rims, *vert)
+    )(pressure, kept, kap, local_sums, tab, from_even, from_odd, *rims, *vert)
     from_odd = lax.ppermute(to_odd, both, odd_moves)
     from_even = lax.ppermute(to_even, both, even_moves)
     if swap:

time: 21.5 us -> 21.5 us (level)
    pallas_call x1 -> x2, Pallas kernels: 1.23 us -> 1.38 us  [the longest x1 1.2 us: shards(): pl.pallas_call(functools.partial(pack_kernel, swap), out_shape=[shape(2,...]
  transfers between devices with their start and end apart: 7 -> 7, of which waited for: 4 -> 3; matrix products, arithmetic and copies ran while one was open for 0% -> 0% of each run, Pallas kernels for 14% -> 15%
where the time goes in v9:
time: 21.5 us; the launch traced here: 21.3 us
  starting transfers between devices  9.79 us (46%)
  Pallas kernels  7.02 us (33%)
  waiting for transfers between devices  3.7 us (17%)
  between operations  0.79 us (4%)
    ppermute x1, starting transfers between devices, shards(): from_odd = lax.ppermute(packed[1], both, odd_moves)  3 us
    pallas_call x1, Pallas kernels, shards(): pl.pallas_call(local_kernel, out_shape=[shape(8, layers, rows, width), sh...  2.23 us
    ppermute x1, starting transfers between devices, shards(): their_halo = lax.ppermute(halo, 'depth', swapped)  2.06 us
    ppermute x1, starting transfers between devices, shards(): from_odd = lax.ppermute(to_odd, both, odd_moves)  1.81 us
    ppermute x1, waiting for transfers between devices, shards(): their_sums = lax.ppermute(sums, 'depth', swapped)  1.78 us
    pallas_call x1, Pallas kernels, shards(): pl.pallas_call(functools.partial(fine_kernel, swap), out_shape=[shape(lay...  1.54 us
    ppermute x1, starting transfers between devices, shards(): vert = [lax.ppermute(packed[2], 'depth', swapped)]  1.49 us
    ppermute x1, waiting for transfers between devices, shards(): from_odd = lax.ppermute(to_odd, both, odd_moves)  1.32 us
  transfers between devices with their start and end apart: 7, of which 3 were waited for; matrix products, arithmetic and copies ran while one was open for 0% of the time, Pallas kernels for 15%

profile of v9, /device:TPU:0, one launch (start us, length us, event | category | flops | bytes accessed | tf_op | source)
XLA Modules:
  0.0 21.3 jit_solution(3897639169161901169)
XLA Ops:
  0.6 0.0 copy-start
  0.6 0.0 copy-start.3
  0.7 0.0 copy-start.4
  0.7 0.0 copy-start.2
  0.7 0.0 copy-start.1
  0.7 1.2 %pack.1 = (f32[2,16,1024]{2,1,0:T(8,128)S(1)}, f32[2,16,1024]{2,1,0:T(8,128)S(1)}, f32[2,8,1024]{2,1,0:T(8,128)S(1)}) custom-call(f32[16,8,1024]{2,1,0:T(8,128)} %p_ref.5, s32[16,8,1024]{2,1,0:T(8,128)} %soil_ref.3), custom_call_target="tpu_custom_call" | custom-call | flops 4000000000 | tf_op jit(solution)/shard_map/pack/pallas_call | solution.py:509
  1.9 3.0 %collective-permute-start.1 = (f32[2,16,1024]{2,1,0:T(8,128)S(1)}, f32[2,16,1024]{2,1,0:T(8,128)S(1)}, u32[]{:S(2)}, u32[]{:S(2)}) collective-permute-start(f32[2,16,1024]{2,1,0:T(8,128)S(1)} %get-tuple-element.21), channel_id=1, source_target_pairs={{0,1},{1,0},{2,4},{3,5},{4,2},{5,3},{6,8},{7,9},{8,6},{9,7},{10,12... | collective-permute-start | bytes 393224 | tf_op jit(solution)/shard_map/ppermute | solution.py:525
  4.9 0.1 collective-permute-start
  5.0 1.5 %collective-permute-start.2 = (f32[2,8,1024]{2,1,0:T(8,128)S(1)}, f32[2,8,1024]{2,1,0:T(8,128)S(1)}, u32[]{:S(2)}, u32[]{:S(2)}) collective-permute-start(f32[2,8,1024]{2,1,0:T(8,128)S(1)} %get-tuple-element.22), channel_id=1, source_target_pairs={{0,1},{1,0},{2,3},{3,2},{4,5},{5,4},{6,7},{7,6},{8,9},{9,8},{10,11... | collective-permute-start | bytes 196616 | tf_op jit(solution)/shard_map/ppermute | solution.py:528
  6.5 0.0 copy-done.4
  6.5 0.2 table.1
  6.7 0.0 copy-done
  6.7 0.0 copy-done.3
  6.7 0.0 copy-done.2
  6.8 0.0 copy-done.1
  6.8 2.2 %local.1 = (f32[8,16,8,1024]{3,2,1,0:T(8,128)S(1)}, f32[16,8,1024]{2,1,0:T(8,128)S(1)}, f32[2,8,1024]{2,1,0:T(8,128)S(1)}) custom-call(f32[16,8,1024]{2,1,0:T(8,128)S(1)} %copy-done, f32[16,8,1024]{2,1,0:T(8,128)S(1)} %copy-done.1, f32[16,8,1024]{2,1,0:T(8,128)S(1)} %copy-done.2, s32[16,8,1024]{2,1,0:T(8,128)S(1)} %copy-done.3, ...), custom_call_target="tpu_custom_call" | custom-call | tf_op jit(solution)/shard_map/local/pallas_call | solution.py:531
  9.0 0.0 collective-permute-done.1.from_ref.from_odd_ref
  9.0 0.2 %rim.3.rim_odd_ref.rim_ref = f32[6,16,1024]{2,1,0:T(8,128)S(1)} custom-call(f32[2,16,1024]{2,1,0:T(8,128)S(1)} %collective-permute-done.1.from_ref.from_odd_ref, f32[5,12,8,128]{3,2,1,0:T(8,128)S(1)} %get-tuple-element.15.tab_ref), custom_call_target="tpu_custom_call" | custom-call | tf_op jit(solution)/shard_map/rim/pallas_call | solution.py:540
  9.3 0.0 collective-permute-done.from_ref.from_even_ref
  9.3 0.2 %rim.2.rim_even_ref.rim_ref = f32[6,16,1024]{2,1,0:T(8,128)S(1)} custom-call(f32[2,16,1024]{2,1,0:T(8,128)S(1)} %collective-permute-done.from_ref.from_even_ref, f32[5,12,8,128]{3,2,1,0:T(8,128)S(1)} %get-tuple-element.15.tab_ref), custom_call_target="tpu_custom_call" | custom-call | tf_op jit(solution)/shard_map/rim/pallas_call | solution.py:540
  9.5 0.0 collective-permute-done.2.rest_0_
  9.5 1.5 %fine.1 = (f32[16,8,1024]{2,1,0:T(8,128)S(1)}, f32[5,8,1024]{2,1,0:T(8,128)S(1)}, f32[16,1152]{1,0:T(8,128)S(1)}, f32[16,1152]{1,0:T(8,128)S(1)}, f32[2,16,1024]{2,1,0:T(8,128)S(1)}) custom-call(f32[16,8,1024]{2,1,0:T(8,128)S(1)} %copy-done, f32[8,16,8,1024]{3,2,1,0:T(8,128)S(1)} %get-tuple-element.17.kept_ref, ...), custom_call_target="tpu_custom_call" | custom-call | tf_op jit(solution)/shard_map/fine/pallas_call | solution.py:551
  11.1 1.8 %collective-permute-start.5 = (f32[16,1152]{1,0:T(8,128)S(1)}, f32[16,1152]{1,0:T(8,128)S(1)}, u32[]{:S(2)}, u32[]{:S(2)}) collective-permute-start(f32[16,1152]{1,0:T(8,128)S(1)} %get-tuple-element.27.to_ref), channel_id=1, source_target_pairs={{0,1},{1,0},{2,4},{3,5},{4,2},{5,3},{6,8},{7,9},{8,6},{9,7},{10,12... | collective-permute-start | bytes 221192 | tf_op jit(solution)/shard_map/ppermute | solution.py:566
  12.9 0.3 %collective-permute-start.3 = (f32[5,8,1024]{2,1,0:T(8,128)S(1)}, f32[5,8,1024]{2,1,0:T(8,128)S(1)}, u32[]{:S(2)}, u32[]{:S(2)}) collective-permute-start(f32[5,8,1024]{2,1,0:T(8,128)S(1)} %get-tuple-element.24.sums_ref), channel_id=1, source_target_pairs={{0,1},{1,0},{2,3},{3,2},{4,5},{5,4},{6,7},{7,6},{8,9},{9,8},{10,11... | collective-permute-start | bytes 491528 | tf_op jit(solution)/shard_map/ppermute | solution.py:569
  13.1 1.0 %collective-permute-start.4 = (f32[16,1152]{1,0:T(8,128)S(1)}, f32[16,1152]{1,0:T(8,128)S(1)}, u32[]{:S(2)}, u32[]{:S(2)}) collective-permute-start(f32[16,1152]{1,0:T(8,128)S(1)} %get-tuple-element.26.to_ref), channel_id=1, source_target_pairs={{0,2},{1,3},{2,0},{3,1},{4,6},{5,7},{6,4},{7,5},{8,10},{9,11},{10,... | collective-permute-start | bytes 221192 | tf_op jit(solution)/shard_map/ppermute | solution.py:567
  14.2 1.3 %collective-permute-done.5.from_ref = f32[16,1152]{1,0:T(8,128)S(1)} collective-permute-done((f32[16,1152]{1,0:T(8,128)S(1)}, f32[16,1152]{1,0:T(8,128)S(1)}, u32[]{:S(2)}, u32[]{:S(2)}) %collective-permute-start.5) | collective-permute-done | bytes 73760 | tf_op jit(solution)/shard_map/ppermute | solution.py:566
  15.5 0.2 odd_edge.1.odd_block_ref
  15.6 0.0 collective-permute-done.4.from_ref
  15.6 0.2 even_edge.1.halo_ref
  15.8 2.1 %collective-permute-start.6 = (f32[8,1792]{1,0:T(8,128)S(1)}, f32[8,1792]{1,0:T(8,128)S(1)}, u32[]{:S(2)}, u32[]{:S(2)}) collective-permute-start(f32[8,1792]{1,0:T(8,128)S(1)} %even_edge.1.halo_ref), channel_id=1, source_target_pairs={{0,1},{1,0},{2,3},{3,2},{4,5},{5,4},{6,7},{7,6},{8,9},{9,8},{10,11... | collective-permute-start | bytes 172040 | tf_op jit(solution)/shard_map/ppermute | solution.py:591
  17.9 1.8 %collective-permute-done.3.their_sums_ref = f32[5,8,1024]{2,1,0:T(8,128)S(1)} collective-permute-done((f32[5,8,1024]{2,1,0:T(8,128)S(1)}, f32[5,8,1024]{2,1,0:T(8,128)S(1)}, u32[]{:S(2)}, u32[]{:S(2)}) %collective-permute-start.3) | collective-permute-done | bytes 163872 | tf_op jit(solution)/shard_map/ppermute | solution.py:569
  19.7 0.6 %collective-permute-done.6.their_halo_ref = f32[8,1792]{1,0:T(8,128)S(1)} collective-permute-done((f32[8,1792]{1,0:T(8,128)S(1)}, f32[8,1792]{1,0:T(8,128)S(1)}, u32[]{:S(2)}, u32[]{:S(2)}) %collective-permute-start.6) | collective-permute-done | bytes 57376 | tf_op jit(solution)/shard_map/ppermute | solution.py:591
  20.3 1.0 %coarse.1 = (f32[16,8,1024]{2,1,0:T(8,128)}, f32[8,1024]{1,0:T(8,128)}) custom-call(f32[16,8,1024]{2,1,0:T(8,128)S(1)} %get-tuple-element.23.smooth_ref, f32[5,8,1024]{2,1,0:T(8,128)S(1)} %columns.1.columns_ref, f32[8,1792]{1,0:T(8,128)S(1)} %even_edge.1.halo_ref, f32[8,1792]{1,0:T(8,128)S(1)} %collective-permute-done.6.their_halo_ref), custom_call_target="tpu_custom_call" | custom-call | tf_op jit(solution)/shard_map/coarse/pallas_call | solution.py:602
  (1 shorter events, 0.0 us)
Async XLA Ops:
  0.6 6.1 %copy-start = (f32[16,8,1024]{2,1,0:T(8,128)S(1)}, f32[16,8,1024]{2,1,0:T(8,128)}, u32[]{:S(2)}) copy-start(f32[16,8,1024]{2,1,0:T(8,128)} %p_ref.5) | copy-start | bytes 1572868
  0.6 6.1 %copy-start.3 = (s32[16,8,1024]{2,1,0:T(8,128)S(1)}, s32[16,8,1024]{2,1,0:T(8,128)}, u32[]{:S(2)}) copy-start(s32[16,8,1024]{2,1,0:T(8,128)} %soil_ref.3) | copy-start | bytes 1572868
  0.7 5.9 %copy-start.4 = (f32[5,12]{1,0:T(8,128)S(1)}, f32[5,12]{1,0:T(8,128)}, u32[]{:S(2)}) copy-start(f32[5,12]{1,0:T(8,128)} %params_ref.1) | copy-start | bytes 724
  0.7 6.1 %copy-start.2 = (f32[16,8,1024]{2,1,0:T(8,128)S(1)}, f32[16,8,1024]{2,1,0:T(8,128)}, u32[]{:S(2)}) copy-start(f32[16,8,1024]{2,1,0:T(8,128)} %source_ref.1) | copy-start | bytes 1572868
  0.7 6.1 %copy-start.1 = (f32[16,8,1024]{2,1,0:T(8,128)S(1)}, f32[16,8,1024]{2,1,0:T(8,128)}, u32[]{:S(2)}) copy-start(f32[16,8,1024]{2,1,0:T(8,128)} %theta_ref.1) | copy-start | bytes 1572868
  1.9 7.1 %collective-permute-start.1 = (f32[2,16,1024]{2,1,0:T(8,128)S(1)}, f32[2,16,1024]{2,1,0:T(8,128)S(1)}, u32[]{:S(2)}, u32[]{:S(2)}) collective-permute-start(f32[2,16,1024]{2,1,0:T(8,128)S(1)} %get-tuple-element.21), channel_id=1, source_target_pairs={{0,1},{1,0},{2,4},{3,5},{4,2},{5,3},{6,8},{7,9},{8,6},{9,7},{10,12... | collective-permute-start | bytes 393224 | tf_op jit(solution)/shard_map/ppermute | solution.py:525
  4.9 4.4 %collective-permute-start = (f32[2,16,1024]{2,1,0:T(8,128)S(1)}, f32[2,16,1024]{2,1,0:T(8,128)S(1)}, u32[]{:S(2)}, u32[]{:S(2)}) collective-permute-start(f32[2,16,1024]{2,1,0:T(8,128)S(1)} %get-tuple-element.20), channel_id=1, source_target_pairs={{0,2},{1,3},{2,0},{3,1},{4,6},{5,7},{6,4},{7,5},{8,10},{9,11},{10,... | collective-permute-start | bytes 393224 | tf_op jit(solution)/shard_map/ppermute | solution.py:526
  5.0 4.5 %collective-permute-start.2 = (f32[2,8,1024]{2,1,0:T(8,128)S(1)}, f32[2,8,1024]{2,1,0:T(8,128)S(1)}, u32[]{:S(2)}, u32[]{:S(2)}) collective-permute-start(f32[2,8,1024]{2,1,0:T(8,128)S(1)} %get-tuple-element.22), channel_id=1, source_target_pairs={{0,1},{1,0},{2,3},{3,2},{4,5},{5,4},{6,7},{7,6},{8,9},{9,8},{10,11... | collective-permute-start | bytes 196616 | tf_op jit(solution)/shard_map/ppermute | solution.py:528
  11.1 4.4 %collective-permute-start.5 = (f32[16,1152]{1,0:T(8,128)S(1)}, f32[16,1152]{1,0:T(8,128)S(1)}, u32[]{:S(2)}, u32[]{:S(2)}) collective-permute-start(f32[16,1152]{1,0:T(8,128)S(1)} %get-tuple-element.27.to_ref), channel_id=1, source_target_pairs={{0,1},{1,0},{2,4},{3,5},{4,2},{5,3},{6,8},{7,9},{8,6},{9,7},{10,12... | collective-permute-start | bytes 221192 | tf_op jit(solution)/shard_map/ppermute | solution.py:566
  12.9 6.8 %collective-permute-start.3 = (f32[5,8,1024]{2,1,0:T(8,128)S(1)}, f32[5,8,1024]{2,1,0:T(8,128)S(1)}, u32[]{:S(2)}, u32[]{:S(2)}) collective-permute-start(f32[5,8,1024]{2,1,0:T(8,128)S(1)} %get-tuple-element.24.sums_ref), channel_id=1, source_target_pairs={{0,1},{1,0},{2,3},{3,2},{4,5},{5,4},{6,7},{7,6},{8,9},{9,8},{10,11... | collective-permute-start | bytes 491528 | tf_op jit(solution)/shard_map/ppermute | solution.py:569
  13.1 2.5 %collective-permute-start.4 = (f32[16,1152]{1,0:T(8,128)S(1)}, f32[16,1152]{1,0:T(8,128)S(1)}, u32[]{:S(2)}, u32[]{:S(2)}) collective-permute-start(f32[16,1152]{1,0:T(8,128)S(1)} %get-tuple-element.26.to_ref), channel_id=1, source_target_pairs={{0,2},{1,3},{2,0},{3,1},{4,6},{5,7},{6,4},{7,5},{8,10},{9,11},{10,... | collective-permute-start | bytes 221192 | tf_op jit(solution)/shard_map/ppermute | solution.py:567
  15.8 4.5 %collective-permute-start.6 = (f32[8,1792]{1,0:T(8,128)S(1)}, f32[8,1792]{1,0:T(8,128)S(1)}, u32[]{:S(2)}, u32[]{:S(2)}) collective-permute-start(f32[8,1792]{1,0:T(8,128)S(1)} %even_edge.1.halo_ref), channel_id=1, source_target_pairs={{0,1},{1,0},{2,3},{3,2},{4,5},{5,4},{6,7},{7,6},{8,9},{9,8},{10,11... | collective-permute-start | bytes 172040 | tf_op jit(solution)/shard_map/ppermute | solution.py:591
